TPU v7x, 512 devices: a whole 4x8x8 slice. The times are simulated.
512 devices in a mesh: exp: 32 (over x_lo, z, core), ccd: 16 (over x_hi, y).
Axes of the slice: x: 4 (x_hi: 2, x_lo: 2; x = x_hi * 2 + x_lo), y: 8, z: 8, core: 2. Of those that a mesh axis runs over, the one named last changes fastest.
Arguments:
- pixels: bfloat16 [32, 16000, 4, 128], P('exp', 'ccd'), may hold values from -24 to 24
- psf_proj: bfloat16 [32, 100, 2160], P('ccd'), may hold values from -0.5 to 0.5
- resolution: float32 [800, 11, 512], P('ccd', None, 'exp'), may hold values from 0.02 to 0.16
- basis: float32 [10, 528], replicated, may hold values from -4 to 4
- sky_fibres: int32 [96], replicated, may hold values from 0 to 799, as said below
- fibre_slot: int32 [800], P('ccd'), may hold values from 0 to 799, as said below
- band_shift: int32 [800], P('ccd'), may hold values from -3 to 3
Outputs:
- sky_subtracted: float32 [32, 800, 512], P(None, 'ccd', 'exp')
- noise_rms: float32 [800, 512], P('ccd', 'exp')
Inputs may be any that keep to these rules, and one draw needn't show every extreme that they name: `sky_fibres`: 96 distinct fibre numbers, listed group by group: entries g * 6 to (g + 1) * 6 - 1 are fibres of the group g of 50 consecutive fibres. `fibre_slot`: for each group g of 50 consecutive fibres, a permutation of the slots g * 50 to (g + 1) * 50 - 1.
All inputs are finite; a program needn't handle non-finite values.
Results may differ from a plain program's by a relative error of at most 0.00095.
Values may be sent and summed in bfloat16 or wider, within the bound.
No kernel may reach another device: no remote copies, remote signals or barrier semaphores. Data moves between devices by JAX's collectives and lax.ppermute only.
A program may use at most 64 MiB of HBM per device.

v0:
```python
import jax
import jax.numpy as jnp
from jax import lax
from jax.sharding import PartitionSpec as P

BPIX = 500
MARG = 20
ROWS = 4
BAND = 11
SHIFT = 3
FC = 50
SPAN = 540


highest = lax.Precision.HIGHEST


def extended(x, sides, width):
    for axis, dim in sides:
        size, length = (lax.axis_size(axis), x.shape[dim])
        up = [(i, (i + 1) % size) for i in range(size - 1)]
        down = [(j, i) for i, j in up]
        last = lax.slice_in_dim(x, length - width, length, axis=dim)
        leading = lax.slice_in_dim(x, 0, width, axis=dim)
        before = lax.ppermute(last, axis, up)
        after = lax.ppermute(leading, axis, down)
        x = jnp.concatenate([before, x, after], axis=dim)
    return x


def band_model(pieces, spectra, shifts):
    length = pieces.shape[2]

    def window_of(shift):
        return lax.dynamic_slice(
            spectra, (jnp.int32(0), shift + SHIFT), (spectra.shape[0], length + BAND - 1)
        )

    windows = jax.vmap(window_of)(shifts)
    total = jnp.zeros((pieces.shape[0], spectra.shape[0], length), jnp.float32)
    for offset in range(BAND):
        total = total + pieces[:, offset, None, :] * windows[:, :, offset : offset + length]
    return total


def solve_small(gram, target):
    factor = jnp.linalg.cholesky(gram)
    return jax.scipy.linalg.cho_solve((factor, True), target[..., None])[..., 0]


def shards(pixels, psf_proj, resolution, basis, sky_fibres, fibre_slot, band_shift):
    padded = extended(pixels, (("ccd", 1),), MARG)
    pixvar = (0.25 + jnp.square(padded.astype(jnp.float32))).astype(jnp.bfloat16)
    proj_square = jnp.square(psf_proj.astype(jnp.float32)).astype(jnp.bfloat16)
    groups = pixels.shape[3]
    flux_parts = []
    var_parts = []
    for block in range(psf_proj.shape[0]):
        lower = block * BPIX
        window = padded[0, lower : lower + SPAN].reshape(SPAN * ROWS, groups)
        window_var = pixvar[0, lower : lower + SPAN].reshape(SPAN * ROWS, groups)
        flux_parts.append(jnp.dot(psf_proj[block], window, preferred_element_type=jnp.float32))
        var_parts.append(
            jnp.dot(proj_square[block], window_var, preferred_element_type=jnp.float32)
        )
    flux_slots = jnp.concatenate(flux_parts, 0).reshape(FC, ROWS * groups)
    var_slots = jnp.concatenate(var_parts, 0).reshape(FC, ROWS * groups)
    group_base = lax.axis_index("ccd") * FC
    local_slot = fibre_slot - group_base
    flux_rows = jnp.take(flux_slots, local_slot, axis=0)
    var_rows = jnp.take(var_slots, local_slot, axis=0)
    fibre_ids = group_base + jnp.arange(FC, dtype=jnp.int32)
    skymask = jnp.any(fibre_ids[:, None] == sky_fibres[None, :], axis=1).astype(jnp.float32)
    model = band_model(
        lax.all_gather(resolution.astype(jnp.bfloat16), "exp", axis=2, tiled=True).astype(
            jnp.float32
        ),
        basis,
        band_shift,
    )
    weight = skymask[:, None] / var_rows
    weighted = model * weight[:, None, :]
    gram = jnp.einsum("fkw,flw->kl", weighted, model, precision=highest)
    target = jnp.einsum("fkw,fw->k", weighted, flux_rows, precision=highest)
    gram, target = lax.psum((gram, target), "ccd")
    coeffs = solve_small(gram, target)
    residual = flux_rows - jnp.einsum("k,fkw->fw", coeffs, model, precision=highest)
    sky_subtracted = lax.all_to_all(residual[None], "exp", split_axis=2, concat_axis=0, tiled=True)
    centred = sky_subtracted - jnp.mean(sky_subtracted, axis=0)
    noise_rms = jnp.sqrt(jnp.mean(jnp.square(centred), axis=0) + 1e-06)
    return (sky_subtracted, noise_rms)


def solution(mesh):
    in_specs = (
        P("exp", "ccd", None, None),
        P("ccd", None, None),
        P("ccd", None, "exp"),
        P(),
        P(),
        P("ccd"),
        P("ccd"),
    )
    out_specs = (P(None, "ccd", "exp"), P("ccd", "exp"))
    return jax.shard_map(shards, mesh=mesh, in_specs=in_specs, out_specs=out_specs, check_vma=False)
```

profile of v0, /device:TPU:1, one launch (start us, length us, event | category | flops | bytes accessed | tf_op | source)
XLA Modules:
  0.0 216.6 jit_solution(9551410797200062274)
XLA Ops:
  0.6 1.4 fusion.23
  2.0 4.0 %collective-permute-start = (bf16[1,20,4,128]{3,2,1,0:T(4,128)(2,1)}, bf16[1,20,4,128]{3,2,1,0:T(4,128)(2,1)S(1)}, u32[]{:S(2)}, u32[]{:S(2)}) collective-permute-start(bf16[1,20,4,128]{3,2,1,0:T(4,128)(2,1)} %get-tuple-element.38), channel_id=1, source_target_pairs={{0,1},{1,2},{2,3},{3,4},{4,5},{5,6},{6,7},{7,8},{8,9},{9,10},{10,1... | collective-permute-start | bytes 61448 | tf_op jit(solution)/shard_map/ppermute | solution.py:25
  6.0 1.3 collective-permute-start.1
  7.4 0.9 convert_element_type.41
  8.3 45.0 %all_gather.3 = bf16[50,11,512]{0,2,1:T(8,128)(2,1)S(1)} all-gather(bf16[50,11,16]{0,2,1:T(8,128)(2,1)S(1)} %convert_element_type.41), channel_id=1, replica_groups=mesh['exp'=32,'ccd'=16] {'exp'}, dimensions={2}, use_global_device_ids=true | all-gather | bytes 580800 | tf_op jit(solution)/shard_map/all_gather | solution.py:75
  53.5 1.2 slice_bitcast_fusion.18
  54.7 1.1 copy.62
  55.8 1.7 copy.63
  57.5 1.7 copy.64
  59.2 1.7 copy.65
  60.9 1.7 copy.66
  62.6 1.7 copy.67
  64.4 0.8 copy.68
  65.2 0.8 copy.69
  65.9 0.8 copy.70
  66.7 0.8 copy.71
  67.5 0.8 copy.72
  68.3 0.7 fusion.20
  68.9 61.5 %while.1 = (s32[]{:T(128)}, f32[10,528]{1,0:T(8,128)S(1)}, s32[50,2]{0,1:T(2,128)S(1)}, f32[50,10,522]{2,1,0:T(8,128)S(1)}, s32[]{:T(128)}) while((s32[]{:T(128)}, f32[10,528]{1,0:T(8,128)S(1)}, s32[50,2]{0,1:T(2,128)S(1)}, f32[50,10,522]{2,1,0:T(8,128)S(1)}, s32[]{:T(128)}) %tuple.39), condition=%wide.while_cond, body=%wide.while_body.sunk | while | flops 2 | bytes 82017 | solution.py:35
  69.6 0.6 bitcast_dynamic-update-slice_fusion.2
  70.8 0.6 bitcast_dynamic-update-slice_fusion.2
  72.0 0.6 bitcast_dynamic-update-slice_fusion.2
  73.2 0.6 bitcast_dynamic-update-slice_fusion.2
  74.5 0.6 bitcast_dynamic-update-slice_fusion.2
  75.7 0.6 bitcast_dynamic-update-slice_fusion.2
  76.9 0.6 bitcast_dynamic-update-slice_fusion.2
  78.2 0.6 bitcast_dynamic-update-slice_fusion.2
  79.4 0.6 bitcast_dynamic-update-slice_fusion.2
  80.6 0.6 bitcast_dynamic-update-slice_fusion.2
  81.9 0.6 bitcast_dynamic-update-slice_fusion.2
  83.1 0.6 bitcast_dynamic-update-slice_fusion.2
  84.3 0.6 bitcast_dynamic-update-slice_fusion.2
  85.5 0.6 bitcast_dynamic-update-slice_fusion.2
  86.8 0.6 bitcast_dynamic-update-slice_fusion.2
  88.0 0.6 bitcast_dynamic-update-slice_fusion.2
  89.2 0.6 bitcast_dynamic-update-slice_fusion.2
  90.5 0.6 bitcast_dynamic-update-slice_fusion.2
  91.7 0.6 bitcast_dynamic-update-slice_fusion.2
  92.9 0.6 bitcast_dynamic-update-slice_fusion.2
  94.2 0.6 bitcast_dynamic-update-slice_fusion.2
  95.4 0.6 bitcast_dynamic-update-slice_fusion.2
  96.6 0.6 bitcast_dynamic-update-slice_fusion.2
  97.8 0.6 bitcast_dynamic-update-slice_fusion.2
  99.1 0.6 bitcast_dynamic-update-slice_fusion.2
  100.3 0.6 bitcast_dynamic-update-slice_fusion.2
  101.5 0.6 bitcast_dynamic-update-slice_fusion.2
  102.8 0.6 bitcast_dynamic-update-slice_fusion.2
  104.0 0.6 bitcast_dynamic-update-slice_fusion.2
  130.5 1.4 multiply_convert_fusion
  132.2 6.5 %multiply_add_fusion = f32[50,10,512]{2,1,0:T(8,128)} fusion(f32[50,10,522]{2,1,0:T(8,128)S(1)} %get-tuple-element.10, f32[50,512]{1,0:T(8,128)S(1)} %copy-done.10, f32[50,512]{1,0:T(8,128)S(1)} %copy-done.9, f32[50,512]{1,0:T(8,128)S(1)} %copy-done.8, f32[50,512]{1,0:T(8,128)} %copy.69, f32[50,512]{1,0:T(8,128)} %copy.68, f32[50,512]{1,0:T(8,128)} %copy.67, ...), kind=kLoop, calls=%fused_computation.10 | loop fusion | flops 5376000 | bytes 13414400 | tf_op jit(solution)/shard_map/add | solution.py:42
  138.8 1.1 copy-done.1
  139.9 0.7 pad_maximum_fusion.1
  141.2 3.7 %add_convert_fusion = bf16[1,1040,4,128]{3,2,1,0:T(4,128)(2,1)S(1)} fusion(bf16[1,20,4,128]{3,2,1,0:T(4,128)(2,1)S(1)} %collective-permute-done.1, bf16[1,1000,4,128]{3,2,1,0:T(4,128)(2,1)S(1)} %copy-done.1, bf16[1,20,4,128]{3,2,1,0:T(4,128)(2,1)S(1)} %collective-permute-done), kind=kLoop, calls=%fused_computation.8 | loop fusion | flops 3194880 | bytes 2129920 | tf_op jit(solution)/shard_map/convert_element_type | solution.py:53
  147.4 2.3 %fusion.4 = f32[10,10]{0,1:T(8,128)S(1)} fusion(f32[50,10,512]{2,1,0:T(8,128)S(1)} %copy-done, f32[50,512]{1,0:T(8,128)S(1)} %get-tuple-element.41), kind=kOutput, calls=%fused_computation.13 | convolution fusion | flops 30976000 | bytes 1126800 | tf_op jit(solution)/shard_map/fkw,flw->kl/dot_general | solution.py:83
  149.7 2.0 fusion.7
  151.7 37.4 %all-reduce.1 = (f32[10,10]{0,1:T(8,128)S(1)}, f32[10]{0:T(128)S(1)}) all-reduce(f32[10,10]{0,1:T(8,128)S(1)} %fusion.4, f32[10]{0:T(128)S(1)} %fusion.7), channel_id=1, replica_groups=mesh['exp'=32,'ccd'=16] {'ccd'}, use_global_device_ids=true, to_apply=%region_1.3 | all-reduce | flops 110 | bytes 880 | tf_op jit(solution)/shard_map/psum | solution.py:85
  189.3 0.9 cholesky.16
  190.2 0.6 compare_reduce_fusion.1
  190.8 0.6 fusion.16
  191.5 0.8 custom-call.10
  192.6 0.9 fusion.24
  194.2 1.3 reduce.7
  195.8 18.6 %all_to_all.18 = f32[32,1,800]{2,1,0:T(1,128)S(1)} all-to-all(f32[32,1,800]{2,1,0:T(1,128)S(1)} %reshape.151), channel_id=1, replica_groups=mesh['exp'=32,'ccd'=16] {'exp'}, dimensions={0} | all-to-all | bytes 204800 | tf_op jit(solution)/shard_map/all_to_all | solution.py:88
  214.4 0.9 reduce.8
  (183 shorter events, 49.2 us)
Async XLA Ops:
  2.0 136.8 %collective-permute-start = (bf16[1,20,4,128]{3,2,1,0:T(4,128)(2,1)}, bf16[1,20,4,128]{3,2,1,0:T(4,128)(2,1)S(1)}, u32[]{:S(2)}, u32[]{:S(2)}) collective-permute-start(bf16[1,20,4,128]{3,2,1,0:T(4,128)(2,1)} %get-tuple-element.38), channel_id=1, source_target_pairs={{0,1},{1,2},{2,3},{3,4},{4,5},{5,6},{6,7},{7,8},{8,9},{9,10},{10,1... | collective-permute-start | bytes 61448 | tf_op jit(solution)/shard_map/ppermute | solution.py:25
  6.0 132.7 %collective-permute-start.1 = (bf16[1,20,4,128]{3,2,1,0:T(4,128)(2,1)}, bf16[1,20,4,128]{3,2,1,0:T(4,128)(2,1)S(1)}, u32[]{:S(2)}, u32[]{:S(2)}) collective-permute-start(bf16[1,20,4,128]{3,2,1,0:T(4,128)(2,1)} %get-tuple-element.39), channel_id=1, source_target_pairs={{1,0},{2,1},{3,2},{4,3},{5,4},{6,5},{7,6},{8,7},{9,8},{10,9},{11,1... | collective-permute-start | bytes 61448 | tf_op jit(solution)/shard_map/ppermute | solution.py:26
  57.5 11.5 %copy-start.4 = (f32[10,528]{1,0:T(8,128)S(1)}, f32[10,528]{1,0:T(8,128)}, u32[]{:S(2)}) copy-start(f32[10,528]{1,0:T(8,128)} %param.12) | copy-start | bytes 63364
  65.2 65.3 %copy-start.11 = (s32[50]{0:T(128)S(1)}, s32[50]{0:T(128)}, u32[]{:S(2)}) copy-start(s32[50]{0:T(128)} %param.14) | copy-start | bytes 604
  66.7 65.2 %copy-start.12 = (s32[96]{0:T(128)S(1)}, s32[96]{0:T(128)}, u32[]{:S(2)}) copy-start(s32[96]{0:T(128)} %param.13) | copy-start | bytes 1156
  66.7 65.4 %copy-start.5 = (f32[50,512]{1,0:T(8,128)S(1)}, f32[50,512]{1,0:T(8,128)}, u32[]{:S(2)}) copy-start(f32[50,512]{1,0:T(8,128)} %copy.63) | copy-start | bytes 307204
  66.7 65.4 %copy-start.6 = (f32[50,512]{1,0:T(8,128)S(1)}, f32[50,512]{1,0:T(8,128)}, u32[]{:S(2)}) copy-start(f32[50,512]{1,0:T(8,128)} %copy.64) | copy-start | bytes 307204
  66.7 65.4 %copy-start.7 = (f32[50,512]{1,0:T(8,128)S(1)}, f32[50,512]{1,0:T(8,128)}, u32[]{:S(2)}) copy-start(f32[50,512]{1,0:T(8,128)} %copy.65) | copy-start | bytes 307204
  130.5 1.7 copy-start.8
  130.5 1.7 copy-start.9
  130.5 1.7 copy-start.10
  132.2 6.5 %copy-start.2 = (bf16[2,100,2160]{2,0,1:T(2,128)(2,1)S(1)}, bf16[2,100,2160]{2,0,1:T(2,128)(2,1)}, u32[]{:S(2)}) copy-start(bf16[2,100,2160]{2,0,1:T(2,128)(2,1)} %param.10) | copy-start | bytes 2592004
  138.6 1.2 copy-start.1
  145.9 1.4 copy-start
  215.9 0.7 copy-start.3
where the time goes:
time: 220 us; the launch traced here: 217 us
  blocking collectives  101 us (46%)
  local copies, waits for them, and re-layouts  82 us (37%)
  other arithmetic  20.4 us (9%)
  matrix products  6.68 us (3%)
  starting transfers between devices  5.31 us (2%)
    gather x150, local copies, waits for them, and re-layouts  61.4 us
    all_gather x1, blocking collectives, shards(): lax.all_gather(resolution.astype(jnp.bfloat16), 'exp', axis=2, tiled=True)  45 us
    psum x1, blocking collectives, shards(): gram, target = lax.psum((gram, target), 'ccd')  37.4 us
    all_to_all x1, blocking collectives, shards(): lax.all_to_all(residual[None], 'exp', split_axis=2, concat_axis=0, tiled=...  18.6 us
    mul x12, local copies, waits for them, and re-layouts, band_model(): pieces[:, offset, None, :] * windows[:, :, offset:offset + length]  14.7 us
    add x1, other arithmetic, band_model(): total + pieces[:, offset, None, :] * windows[:, :, offset:offset + length]  6.47 us
  transfers between devices with their start and end apart: 2, of which 0 were waited for; matrix products, arithmetic and copies ran while one was open for 40% of the time, Pallas kernels for 0%

commit v1 on v0

v1 whole, which is shorter than its diff:
```python
import jax
import jax.numpy as jnp
from jax import lax
from jax.experimental import pallas as pl
from jax.experimental.pallas import tpu as pltpu
from jax.sharding import PartitionSpec as P

BPIX = 500
MARG = 20
ROWS = 4
COMP = 10
BAND = 11
SHIFT = 3
FIBBLK = 25
FC = 50
SPAN = 540
SKYC = 6
EXPOS = 32
CHUNK = 16
GROUPS = 128
LANES = 128
HALF = 64
SUB = 8
TAPS = BAND + 2 * SHIFT
EDGE = MARG * ROWS
DEPTH = SPAN * ROWS
LOCAL = 2 * BPIX * ROWS


f32 = jnp.float32
highest = lax.Precision.HIGHEST


def lanes_of(shape=(SUB, LANES), dim=1):
    return lax.broadcasted_iota(jnp.int32, shape, dim)


def sky_index(lane):
    within = lane & (HALF - 1)
    fibre = jnp.zeros_like(within)
    for i in range(1, SKYC):
        fibre = fibre + jnp.where(within >= i * COMP, 1, 0)
    comp = within - fibre * COMP
    valid = within < SKYC * COMP
    return fibre, comp, valid


def pick(x, idx):
    return jnp.take_along_axis(x, idx, axis=1, mode="promise_in_bounds")


def by_sky(fibre, values):
    out = jnp.zeros_like(fibre)
    for i, value in enumerate(values):
        out = jnp.where(fibre == i, value, out)
    return out


def doubled(row_ref, scratch):
    scratch[...] = jnp.zeros((SUB, LANES), jnp.int32)
    row = row_ref[...]
    scratch[0:1, 0:FC] = row
    scratch[0:1, HALF : HALF + FC] = row
    return jnp.broadcast_to(scratch[0:1, :], (SUB, LANES))


def model_kernel(pos_ref, sky_ref, res_ref, basis_ref, shift_ref, send_ref, model_ref, res_s, basis_s, row_s, turned_s):
    exp_at = pos_ref[0]
    ccd_at = pos_ref[1]
    lane = lanes_of()
    shift = doubled(shift_ref, row_s) + SHIFT
    res_s[...] = jnp.zeros((BAND, SUB, LANES), f32)
    for d in range(BAND):
        res_s[d, :, 0:FC] = res_ref[d, 0:SUB, :]
        res_s[d, :, HALF : HALF + FC] = res_ref[d, SUB:CHUNK, :]
    bands = [res_s[d] for d in range(BAND)]
    masks = [shift == s for s in range(2 * SHIFT + 1)]
    basis_s[...] = jnp.zeros((16, 640), f32)
    basis_s[0:COMP, 0:528] = basis_ref[...]
    tile = exp_at // 8
    offset = CHUNK * (exp_at % 8)
    near = basis_s[:, pl.ds(pl.multiple_of(tile * LANES, LANES), LANES)]
    far = basis_s[:, pl.ds(pl.multiple_of(tile * LANES + LANES, LANES), LANES)]
    turn = (LANES - offset) % LANES
    wide = lanes_of((16, LANES))
    window = jnp.where(wide < LANES - offset, pltpu.roll(near, turn, 1), pltpu.roll(far, turn, 1))
    turned = jnp.transpose(jnp.concatenate([window, jnp.zeros((LANES - 16, LANES), f32)], axis=0))
    turned_s[...] = turned[0:32]
    totals = [jnp.zeros((SUB, LANES), f32) for _ in range(COMP)]
    for t in range(TAPS):
        tap = jnp.zeros((SUB, LANES), f32)
        for s in range(2 * SHIFT + 1):
            if 0 <= t - s < BAND:
                tap = jnp.where(masks[s], bands[t - s], tap)
        upper = turned_s[t : t + SUB, :]
        lower = turned_s[t + SUB : t + 2 * SUB, :]
        both = jnp.where(lane < HALF, upper, pltpu.roll(lower, HALF, 1))
        for k in range(COMP):
            totals[k] = totals[k] + tap * pick(both, (lane & HALF) + k)
    for k in range(COMP):
        model_ref[k] = totals[k]
    fibre, comp, valid = sky_index(lane)
    sky = by_sky(fibre, [sky_ref[ccd_at * SKYC + i] - ccd_at * FC for i in range(SKYC)])
    source = (lane & HALF) + sky
    out = jnp.zeros((SUB, LANES), f32)
    for k in range(COMP):
        out = jnp.where((comp == k) & valid, pick(totals[k], source), out)
    send_ref[...] = jnp.broadcast_to(out[None], (EXPOS, SUB, LANES))


def extract_kernel(pos_ref, sky_ref, slots_ref, pix_ref, before_ref, after_ref, psf_ref, slot_ref, flux_ref, weight_ref, skyflux_ref, pix_s, var_s, pad_s, flux_s, vari_s, row_s):
    ccd_at = pos_ref[1]
    base = ccd_at * FC
    lane = lanes_of()
    pix_s[0:EDGE, :] = before_ref[...]
    pix_s[EDGE : EDGE + LOCAL, :] = pix_ref[...]
    pix_s[EDGE + LOCAL : 2 * EDGE + LOCAL, :] = after_ref[...]
    var_s[...] = (0.25 + jnp.square(pix_s[...].astype(f32))).astype(jnp.bfloat16)
    pad_s[...] = jnp.zeros((LANES, LANES), f32)
    for b in range(2):
        lower = b * BPIX * ROWS
        psf = psf_ref[b]
        pad_s[0:100, :] = jnp.dot(psf, pix_s[lower : lower + DEPTH, :], preferred_element_type=f32)
        flux_s[b] = jnp.transpose(pad_s[...])
        square = jnp.square(psf.astype(f32)).astype(jnp.bfloat16)
        pad_s[0:100, :] = jnp.dot(square, var_s[lower : lower + DEPTH, :], preferred_element_type=f32)
        vari_s[b] = jnp.transpose(pad_s[...])
    slot = doubled(slot_ref, row_s)
    used = (lane & (HALF - 1)) < FC
    slot = jnp.where(used, slot - base, 0)
    second = slot >= FIBBLK
    place = jnp.where(second, slot - FIBBLK, slot) * ROWS
    fibre, _, valid = sky_index(lane)
    local = [sky_ref[ccd_at * SKYC + i] - base for i in range(SKYC)]
    sky = (lane & HALF) + by_sky(fibre, local)
    sky_slot = by_sky(fibre, [slots_ref[f] - base for f in local])
    sky_second = sky_slot >= FIBBLK
    sky_place = jnp.where(sky_second, sky_slot - FIBBLK, sky_slot) * ROWS

    def gathered(ref, row, spot, late):
        upper = jnp.where(late, pick(ref[1, row : row + SUB, :], spot), pick(ref[0, row : row + SUB, :], spot))
        row = row + SUB
        lower = jnp.where(late, pick(ref[1, row : row + SUB, :], spot), pick(ref[0, row : row + SUB, :], spot))
        return jnp.where(lane < HALF, upper, lower)

    for r in range(ROWS):
        for m in range(GROUPS // CHUNK):
            flux = jnp.where(used, gathered(flux_s, m * CHUNK, place + r, second), 0.0)
            flux_ref[r * 8 + m] = flux
            skyflux_ref[r * 8 + m] = jnp.where(valid, pick(flux, sky), 0.0)
            vari = gathered(vari_s, m * CHUNK, sky_place + r, sky_second)
            weight_ref[r * 8 + m] = jnp.where(valid, 1.0 / vari, 0.0)


def gram_kernel(model_ref, weight_ref, flux_ref, out_ref):
    model = model_ref[...].reshape(EXPOS * SUB, LANES)
    weighted = model * weight_ref[...].reshape(EXPOS * SUB, LANES)
    target = jnp.sum(weighted * flux_ref[...].reshape(EXPOS * SUB, LANES), axis=0, keepdims=True)
    square = lax.dot_general(weighted, model, (((0,), (0,)), ((), ())), precision=highest, preferred_element_type=f32)
    shape = (LANES, LANES)
    fibre_r, comp_r, valid_r = sky_index(lanes_of(shape, 0))
    row, col = lanes_of(shape, 0), lanes_of(shape, 1)
    fibre_c, comp_c, valid_c = sky_index(col)
    same = (fibre_r == fibre_c) & ((row & HALF) == (col & HALF)) & valid_r & valid_c
    square = jnp.where(same, square, 0.0)
    select = jnp.where((row == comp_c) & valid_c, 1.0, 0.0)
    half = jnp.dot(select[0:16], square, precision=highest, preferred_element_type=f32)
    half = jnp.where(row[0:16] == COMP, target, half)
    full = lax.dot_general(half, select, (((1,), (1,)), ((), ())), precision=highest, preferred_element_type=f32)
    tile = full[0:SUB] + pltpu.roll(full[SUB : 2 * SUB], HALF, 1)
    out_ref[...] = jnp.broadcast_to(tile[None], out_ref.shape)


def solve_kernel(parts_ref, flux_ref, out_ref):
    total = jnp.sum(parts_ref[...], axis=0)
    system = jnp.concatenate([total, pltpu.roll(total, HALF, 1)], axis=0)
    col = lanes_of((16, LANES))
    row = lanes_of((16, LANES), 0)
    system = jnp.where((col < COMP) & (row <= COMP), system, 0.0)
    for k in range(COMP):
        column = pick(system, jnp.full((16, LANES), k, jnp.int32))
        line = system[k : k + 1, :]
        pivot = column[k : k + 1, :]
        unit = jnp.where(col[0:1] == k, 1.0, 0.0)
        system = system - column * ((line - unit) / pivot)
    coeffs = jnp.broadcast_to(system[COMP : COMP + 1, :], (SUB, LANES))
    coeffs = pltpu.roll(coeffs, FC, 1)
    lane = lanes_of()
    here = (lane >= FC) & (lane < FC + COMP)
    for e in range(EXPOS):
        out_ref[e] = jnp.where(here, coeffs, flux_ref[e])


def subtract_kernel(flux_ref, model_ref, out_ref, noise_ref, left_s):
    models = [model_ref[k] for k in range(COMP)]
    spots = [jnp.full((SUB, LANES), FC + k, jnp.int32) for k in range(COMP)]
    total = jnp.zeros((SUB, LANES), f32)
    for e in range(EXPOS):
        left = flux_ref[e]
        sky = pick(left, spots[0]) * models[0]
        for k in range(1, COMP):
            sky = sky + pick(left, spots[k]) * models[k]
        left = left - sky
        left_s[e] = left
        total = total + left
        out_ref[e, 0:SUB, :] = left[:, 0:FC]
        out_ref[e, SUB:CHUNK, :] = pltpu.roll(left, HALF, 1)[:, 0:FC]
    mean = total * (1.0 / EXPOS)
    spread = jnp.zeros((SUB, LANES), f32)
    for e in range(EXPOS):
        spread = spread + jnp.square(left_s[e] - mean)
    noise = jnp.sqrt(spread * (1.0 / EXPOS) + 1e-06)
    noise_ref[0:SUB, :] = noise[:, 0:FC]
    noise_ref[SUB:CHUNK, :] = pltpu.roll(noise, HALF, 1)[:, 0:FC]


VMEM = pl.BlockSpec(memory_space=pltpu.VMEM)
SMEM = pl.BlockSpec(memory_space=pltpu.SMEM)
TILES = jax.ShapeDtypeStruct((EXPOS, SUB, LANES), f32)
PARAMS = pltpu.CompilerParams(vmem_limit_bytes=40 * 1024 * 1024)


def local_model(pos, sky_fibres, resolution, basis, band_shift):
    return pl.pallas_call(
        model_kernel,
        out_shape=(TILES, jax.ShapeDtypeStruct((COMP, SUB, LANES), f32)),
        in_specs=[SMEM, SMEM, VMEM, VMEM, VMEM],
        out_specs=(VMEM, VMEM),
        scratch_shapes=[
            pltpu.VMEM((BAND, SUB, LANES), f32),
            pltpu.VMEM((16, 640), f32),
            pltpu.VMEM((SUB, LANES), jnp.int32),
            pltpu.VMEM((32, LANES), f32),
        ],
        compiler_params=PARAMS,
        name="model",
    )(pos, sky_fibres, resolution.transpose(1, 2, 0), basis, band_shift.reshape(1, FC))


def extract(pos, sky_fibres, fibre_slot, pixels, before, after, psf):
    return pl.pallas_call(
        extract_kernel,
        out_shape=(TILES, TILES, TILES),
        in_specs=[SMEM, SMEM, SMEM, VMEM, VMEM, VMEM, VMEM, VMEM],
        out_specs=(VMEM, VMEM, VMEM),
        scratch_shapes=[
            pltpu.VMEM((2 * EDGE + LOCAL, LANES), jnp.bfloat16),
            pltpu.VMEM((2 * EDGE + LOCAL, LANES), jnp.bfloat16),
            pltpu.VMEM((LANES, LANES), f32),
            pltpu.VMEM((2, LANES, LANES), f32),
            pltpu.VMEM((2, LANES, LANES), f32),
            pltpu.VMEM((SUB, LANES), jnp.int32),
        ],
        compiler_params=PARAMS,
        name="extract",
    )(pos, sky_fibres, fibre_slot, pixels, before, after, psf, fibre_slot.reshape(1, FC))


def gram_parts(model, weight, flux, copies):
    return pl.pallas_call(
        gram_kernel,
        out_shape=jax.ShapeDtypeStruct((copies, SUB, LANES), f32),
        in_specs=[VMEM, VMEM, VMEM],
        out_specs=VMEM,
        compiler_params=PARAMS,
        name="gram",
    )(model, weight, flux)


def solve(parts, flux):
    return pl.pallas_call(
        solve_kernel, out_shape=TILES, in_specs=[VMEM, VMEM], out_specs=VMEM, compiler_params=PARAMS, name="solve"
    )(parts, flux)


def subtract(flux, model):
    return pl.pallas_call(
        subtract_kernel,
        out_shape=(jax.ShapeDtypeStruct((EXPOS, CHUNK, FC), f32), jax.ShapeDtypeStruct((CHUNK, FC), f32)),
        in_specs=[VMEM, VMEM],
        out_specs=(VMEM, VMEM),
        scratch_shapes=[pltpu.VMEM((EXPOS, SUB, LANES), f32)],
        compiler_params=PARAMS,
        name="subtract",
    )(flux, model)


def shards(pixels, psf_proj, resolution, basis, sky_fibres, fibre_slot, band_shift):
    size = lax.axis_size("ccd")
    rows = pixels.reshape(LOCAL, GROUPS)
    up = [(i, i + 1) for i in range(size - 1)]
    down = [(j, i) for i, j in up]
    before = lax.ppermute(rows[LOCAL - EDGE :], "ccd", up)
    after = lax.ppermute(rows[:EDGE], "ccd", down)
    pos = jnp.stack([lax.axis_index("exp"), lax.axis_index("ccd")]).astype(jnp.int32)
    send, model = local_model(pos, sky_fibres, resolution, basis, band_shift)
    sky_model = lax.all_to_all(send, "exp", split_axis=0, concat_axis=0, tiled=True)
    flux, weight, sky_flux = extract(pos, sky_fibres, fibre_slot, rows, before, after, psf_proj)
    parts = gram_parts(sky_model, weight, sky_flux, size)
    parts = lax.all_to_all(parts, "ccd", split_axis=0, concat_axis=0, tiled=True)
    flux = solve(parts, flux)
    flux = lax.all_to_all(flux, "exp", split_axis=0, concat_axis=0, tiled=True)
    sky_subtracted, noise_rms = subtract(flux, model)
    return (sky_subtracted.transpose(0, 2, 1), noise_rms.transpose(1, 0))


def solution(mesh):
    in_specs = (
        P("exp", "ccd", None, None),
        P("ccd", None, None),
        P("ccd", None, "exp"),
        P(),
        P(),
        P("ccd"),
        P("ccd"),
    )
    out_specs = (P(None, "ccd", "exp"), P("ccd", "exp"))
    return jax.shard_map(shards, mesh=mesh, in_specs=in_specs, out_specs=out_specs, check_vma=False)
```

time: 220 us -> 72.2 us (0.33); the launches traced: 217 us -> 71.7 us
  local copies, waits for them, and re-layouts: 82 us -> 5.01 us
  blocking collectives: 101 us -> 37.1 us
  other arithmetic: 20.4 us -> 0.08 us
  starting transfers between devices: 5.31 us -> 17.5 us
  Pallas kernels: 0 us -> 8.92 us
  matrix products: 6.68 us -> 0 us
  waiting for transfers between devices: 0.01 us -> 2.26 us
    gather x152 -> x0, local copies, waits for them, and re-layouts: 62.7 us -> none
    all_gather x1 -> x0, blocking collectives: 45 us -> none  [shards(): lax.all_gather(resolution.astype(jnp.bfloat16), 'exp', axis=2, tiled=True)]
    psum x1 -> x0, blocking collectives: 37.4 us -> none  [shards(): gram, target = lax.psum((gram, target), 'ccd')]
    all_to_all x1 -> x2, blocking collectives: 18.6 us -> 37.1 us  [the longest x1 19.4 us: shards(): flux = lax.all_to_all(flux, 'exp', split_axis=0, concat_axis=0, tiled=True)]
    mul x12 -> x0, local copies, waits for them, and re-layouts: 14.7 us -> none  [band_model(): pieces[:, offset, None, :] * windows[:, :, offset:offset + length]]
    all_to_all x0 -> x1, starting transfers between devices: none -> 13 us  [shards(): lax.all_to_all(send, 'exp', split_axis=0, concat_axis=0, tiled=True)]
    pallas_call x0 -> x5, Pallas kernels: none -> 8.92 us  [the longest x1 2.82 us: subtract(): pl.pallas_call(subtract_kernel, out_shape=(jax.ShapeDtypeStruct((EXPOS, C...]
    add x2 -> x0, other arithmetic: 6.48 us -> none  [the longest x1 6.47 us: band_model(): total + pieces[:, offset, None, :] * windows[:, :, offset:offset + length]]
  transfers between devices with their start and end apart: 2 -> 3, of which waited for: 0 -> 1; matrix products, arithmetic and copies ran while one was open for 40% -> 3% of each run, Pallas kernels for 0% -> 3%
where the time goes in v1:
time: 72.2 us; the launch traced here: 71.7 us
  blocking collectives  37.1 us (51%)
  starting transfers between devices  17.5 us (24%)
  Pallas kernels  8.92 us (12%)
  local copies, waits for them, and re-layouts  5.01 us (7%)
  waiting for transfers between devices  2.26 us (3%)
  between operations  0.75 us (1%)
    all_to_all x1, blocking collectives, shards(): flux = lax.all_to_all(flux, 'exp', split_axis=0, concat_axis=0, tiled=True)  19.4 us
    all_to_all x1, blocking collectives, shards(): lax.all_to_all(parts, 'ccd', split_axis=0, concat_axis=0, tiled=True)  17.7 us
    all_to_all x1, starting transfers between devices, shards(): lax.all_to_all(send, 'exp', split_axis=0, concat_axis=0, tiled=True)  13 us
    unnamed x13, local copies, waits for them, and re-layouts  4.25 us
    ppermute x1, starting transfers between devices, shards(): before = lax.ppermute(rows[LOCAL - EDGE:], 'ccd', up)  3.2 us
    pallas_call x1, Pallas kernels, subtract(): pl.pallas_call(subtract_kernel, out_shape=(jax.ShapeDtypeStruct((EXPOS, C...  2.82 us
    pallas_call x1, Pallas kernels, extract(): pl.pallas_call(extract_kernel, out_shape=(TILES, TILES, TILES), in_specs=...  2.26 us
    ppermute x1, waiting for transfers between devices, shards(): after = lax.ppermute(rows[:EDGE], 'ccd', down)  2.25 us
  transfers between devices with their start and end apart: 3, of which 1 were waited for; matrix products, arithmetic and copies ran while one was open for 3% of the time, Pallas kernels for 3%

profile of v1, /device:TPU:1, one launch (start us, length us, event | category | flops | bytes accessed | tf_op | source)
XLA Modules:
  0.0 71.7 jit_solution(7809903723325469091)
XLA Ops:
  0.6 0.1 pad_add_fusion.pos_ref
  0.7 0.0 copy-start.3
  0.7 0.0 copy-start.5
  0.7 0.7 copy-done.3
  1.4 0.0 copy-done.5
  1.4 0.0 copy-start.1
  1.4 0.9 %copy-done.1 = f32[50,11,16]{0,2,1:T(8,128)S(1)} copy-done((f32[50,11,16]{0,2,1:T(8,128)S(1)}, f32[50,11,16]{0,2,1:T(8,128)}, u32[]{:S(2)}) %copy-start.1) | copy-done | bytes 35224
  2.3 0.0 copy-start.2
  2.3 0.8 %copy-done.2 = f32[10,528]{1,0:T(8,128)S(1)} copy-done((f32[10,528]{1,0:T(8,128)S(1)}, f32[10,528]{1,0:T(8,128)}, u32[]{:S(2)}) %copy-start.2) | copy-done | bytes 21144
  3.1 2.1 %model.1 = (f32[32,8,128]{2,1,0:T(8,128)}, f32[10,8,128]{2,1,0:T(8,128)S(1)}) custom-call(s32[2]{0:T(128)S(1)} %pad_add_fusion.pos_ref, s32[96]{0:T(128)S(1)} %copy-done.3, f32[11,16,50]{2,1,0:T(8,128)S(1)} %bitcast.11, f32[10,528]{1,0:T(8,128)S(1)} %copy-done.2, s32[1,50]{1,0:T(1,128)S(1)} %bitcast.13), custom_call_target="tpu_custom_call" | custom-call | tf_op jit(solution)/shard_map/model/pallas_call | solution.py:224
  5.2 0.0 copy-start
  5.2 13.0 %all-to-all-start = ((f32[32,8,128]{2,1,0:T(8,128)}), f32[32,8,128]{2,1,0:T(8,128)S(1)}, u32[]{:S(2)}, u32[]{:S(2)}) async-start(f32[32,8,128]{2,1,0:T(8,128)} %get-tuple-element.9), calls=%async_computation | async-start | bytes 262144 | tf_op jit(solution)/shard_map/all_to_all | solution.py:297
  18.2 0.8 %fusion = (bf16[1,20,4,128]{3,2,1,0:T(4,128)(2,1)S(1)}, bf16[1,20,4,128]{3,2,1,0:T(4,128)(2,1)S(1)}) fusion(bf16[1,1000,4,128]{3,2,1,0:T(4,128)(2,1)} %param.7), kind=kLoop, calls=%fused_computation.1 | loop fusion | bytes 81920 | tf_op jit(solution)/shard_map/slice | solution.py:294
  19.0 3.2 %collective-permute-start = (bf16[80,128]{1,0:T(8,128)(2,1)S(1)}, bf16[80,128]{1,0:T(8,128)(2,1)S(1)}, u32[]{:S(2)}, u32[]{:S(2)}) collective-permute-start(bf16[80,128]{1,0:T(8,128)(2,1)S(1)} %bitcast.15), channel_id=1, source_target_pairs={{0,1},{1,2},{2,3},{3,4},{4,5},{5,6},{6,7},{7,8},{8,9},{9,10},{10,1... | collective-permute-start | bytes 61448 | tf_op jit(solution)/shard_map/ppermute | solution.py:293
  22.2 1.3 %collective-permute-start.1 = (bf16[80,128]{1,0:T(8,128)(2,1)S(1)}, bf16[80,128]{1,0:T(8,128)(2,1)S(1)}, u32[]{:S(2)}, u32[]{:S(2)}) collective-permute-start(bf16[80,128]{1,0:T(8,128)(2,1)S(1)} %bitcast.14), channel_id=1, source_target_pairs={{1,0},{2,1},{3,2},{4,3},{5,4},{6,5},{7,6},{8,7},{9,8},{10,9},{11,1... | collective-permute-start | bytes 61448 | tf_op jit(solution)/shard_map/ppermute | solution.py:294
  23.5 1.3 %copy.9.psf_ref = bf16[2,100,2160]{2,1,0:T(8,128)(2,1)S(1)} copy(bf16[2,100,2160]{2,0,1:T(2,128)(2,1)} %param.8) | data formatting | bytes 1728000 | tf_op args[1]
  24.8 0.0 collective-permute-done.before_ref
  24.8 2.3 %collective-permute-done.1.after_ref = bf16[80,128]{1,0:T(8,128)(2,1)S(1)} collective-permute-done((bf16[80,128]{1,0:T(8,128)(2,1)S(1)}, bf16[80,128]{1,0:T(8,128)(2,1)S(1)}, u32[]{:S(2)}, u32[]{:S(2)}) %collective-permute-start.1) | collective-permute-done | bytes 20512 | tf_op jit(solution)/shard_map/ppermute | solution.py:294
  27.0 0.0 copy-start.4
  27.0 0.0 copy-done
  27.0 0.7 copy-done.4
  27.7 2.3 %extract.1 = (f32[32,8,128]{2,1,0:T(8,128)S(1)}, f32[32,8,128]{2,1,0:T(8,128)S(1)}, f32[32,8,128]{2,1,0:T(8,128)S(1)}) custom-call(s32[2]{0:T(128)S(1)} %pad_add_fusion.pos_ref, s32[96]{0:T(128)S(1)} %copy-done.3, s32[50]{0:T(128)S(1)} %copy-done.4, bf16[4000,128]{1,0:T(8,128)(2,1)S(1)} %bitcast.10, bf16[80,128]{1,0:T(8,128)(2,1)S(1)} %collective-permute-done.before_ref, ...), custom_call_target="tpu_custom_call" | custom-call | tf_op jit(solution)/shard_map/extract/pallas_call | solution.py:241
  30.0 0.0 all-to-all-done.model_ref
  30.0 0.9 %gram.1 = f32[16,8,128]{2,1,0:T(8,128)S(1)} custom-call(f32[32,8,128]{2,1,0:T(8,128)S(1)} %all-to-all-done.model_ref, f32[32,8,128]{2,1,0:T(8,128)S(1)} %get-tuple-element.10.weight_ref, f32[32,8,128]{2,1,0:T(8,128)S(1)} %get-tuple-element.11.flux_ref), custom_call_target="tpu_custom_call" | custom-call | tf_op jit(solution)/shard_map/gram/pallas_call | solution.py:260
  30.8 17.7 %all_to_all.15.parts_ref = f32[16,8,128]{2,1,0:T(8,128)S(1)} all-to-all(f32[16,8,128]{2,1,0:T(8,128)S(1)} %gram.1), channel_id=1, replica_groups=mesh['exp'=32,'ccd'=16] {'ccd'}, dimensions={0} | all-to-all | bytes 131072 | tf_op jit(solution)/shard_map/all_to_all | solution.py:300
  48.5 0.8 %solve.1 = f32[32,8,128]{2,1,0:T(8,128)S(1)} custom-call(f32[16,8,128]{2,1,0:T(8,128)S(1)} %all_to_all.15.parts_ref, f32[32,8,128]{2,1,0:T(8,128)S(1)} %get-tuple-element.12.flux_ref), custom_call_target="tpu_custom_call" | custom-call | tf_op jit(solution)/shard_map/solve/pallas_call | solution.py:271
  49.4 19.4 %all_to_all.16.flux_ref = f32[32,8,128]{2,1,0:T(8,128)S(1)} all-to-all(f32[32,8,128]{2,1,0:T(8,128)S(1)} %solve.1), channel_id=1, replica_groups=mesh['exp'=32,'ccd'=16] {'exp'}, dimensions={0} | all-to-all | bytes 262144 | tf_op jit(solution)/shard_map/all_to_all | solution.py:302
  68.8 2.8 %subtract.1 = (f32[32,16,50]{2,1,0:T(8,128)}, f32[16,50]{1,0:T(8,128)}) custom-call(f32[32,8,128]{2,1,0:T(8,128)S(1)} %all_to_all.16.flux_ref, f32[10,8,128]{2,1,0:T(8,128)S(1)} %get-tuple-element.13.model_ref), custom_call_target="tpu_custom_call" | custom-call | tf_op jit(solution)/shard_map/subtract/pallas_call | solution.py:277
Async XLA Ops:
  0.7 0.7 copy-start.3
  0.7 0.7 copy-start.5
  1.4 0.9 %copy-start.1 = (f32[50,11,16]{0,2,1:T(8,128)S(1)}, f32[50,11,16]{0,2,1:T(8,128)}, u32[]{:S(2)}) copy-start(f32[50,11,16]{0,2,1:T(8,128)} %param.9) | copy-start | bytes 105604
  2.3 0.8 %copy-start.2 = (f32[10,528]{1,0:T(8,128)S(1)}, f32[10,528]{1,0:T(8,128)}, u32[]{:S(2)}) copy-start(f32[10,528]{1,0:T(8,128)} %basis_ref.1) | copy-start | bytes 63364
  5.2 21.8 %copy-start = (bf16[1,1000,4,128]{3,2,1,0:T(4,128)(2,1)S(1)}, bf16[1,1000,4,128]{3,2,1,0:T(4,128)(2,1)}, u32[]{:S(2)}) copy-start(bf16[1,1000,4,128]{3,2,1,0:T(4,128)(2,1)} %param.7) | copy-start | bytes 3072004
  5.2 24.8 %all-to-all-start = ((f32[32,8,128]{2,1,0:T(8,128)}), f32[32,8,128]{2,1,0:T(8,128)S(1)}, u32[]{:S(2)}, u32[]{:S(2)}) async-start(f32[32,8,128]{2,1,0:T(8,128)} %get-tuple-element.9), calls=%async_computation | async-start | bytes 262144 | tf_op jit(solution)/shard_map/all_to_all | solution.py:297
  19.0 5.8 %collective-permute-start = (bf16[80,128]{1,0:T(8,128)(2,1)S(1)}, bf16[80,128]{1,0:T(8,128)(2,1)S(1)}, u32[]{:S(2)}, u32[]{:S(2)}) collective-permute-start(bf16[80,128]{1,0:T(8,128)(2,1)S(1)} %bitcast.15), channel_id=1, source_target_pairs={{0,1},{1,2},{2,3},{3,4},{4,5},{5,6},{6,7},{7,8},{8,9},{9,10},{10,1... | collective-permute-start | bytes 61448 | tf_op jit(solution)/shard_map/ppermute | solution.py:293
  22.2 4.8 %collective-permute-start.1 = (bf16[80,128]{1,0:T(8,128)(2,1)S(1)}, bf16[80,128]{1,0:T(8,128)(2,1)S(1)}, u32[]{:S(2)}, u32[]{:S(2)}) collective-permute-start(bf16[80,128]{1,0:T(8,128)(2,1)S(1)} %bitcast.14), channel_id=1, source_target_pairs={{1,0},{2,1},{3,2},{4,3},{5,4},{6,5},{7,6},{8,7},{9,8},{10,9},{11,1... | collective-permute-start | bytes 61448 | tf_op jit(solution)/shard_map/ppermute | solution.py:294
  27.0 0.7 copy-start.4

commit v2 on v1

--- a/solution.py
+++ b/solution.py
@@ -16,6 +16,7 @@
 SPAN = 540
 SKYC = 6
 EXPOS = 32
+PIECE = 8
 CHUNK = 16
 GROUPS = 128
 LANES = 128
@@ -49,32 +50,29 @@
     return jnp.take_along_axis(x, idx, axis=1, mode="promise_in_bounds")
 
 
-def by_sky(fibre, values):
-    out = jnp.zeros_like(fibre)
-    for i, value in enumerate(values):
-        out = jnp.where(fibre == i, value, out)
-    return out
-
-
-def doubled(row_ref, scratch):
+def doubled(row, scratch):
     scratch[...] = jnp.zeros((SUB, LANES), jnp.int32)
-    row = row_ref[...]
     scratch[0:1, 0:FC] = row
     scratch[0:1, HALF : HALF + FC] = row
     return jnp.broadcast_to(scratch[0:1, :], (SUB, LANES))
 
 
-def model_kernel(pos_ref, sky_ref, res_ref, basis_ref, shift_ref, send_ref, model_ref, res_s, basis_s, row_s, turned_s):
-    exp_at = pos_ref[0]
-    ccd_at = pos_ref[1]
-    lane = lanes_of()
-    shift = doubled(shift_ref, row_s) + SHIFT
+def sky_lanes(row, scratch, ccd_at, fibre):
+    scratch[...] = jnp.zeros((SUB, LANES), jnp.int32)
+    scratch[0:1, 0 : row.shape[1]] = row
+    listed = jnp.broadcast_to(scratch[0:1, :], (SUB, LANES))
+    return (lanes_of() & HALF) + pick(listed, fibre + ccd_at * SKYC) - ccd_at * FC
+
+
+def banded(res_ref, res_s):
     res_s[...] = jnp.zeros((BAND, SUB, LANES), f32)
     for d in range(BAND):
         res_s[d, :, 0:FC] = res_ref[d, 0:SUB, :]
         res_s[d, :, HALF : HALF + FC] = res_ref[d, SUB:CHUNK, :]
-    bands = [res_s[d] for d in range(BAND)]
-    masks = [shift == s for s in range(2 * SHIFT + 1)]
+    return [res_s[d] for d in range(BAND)]
+
+
+def turned_basis(basis_ref, basis_s, turned_s, exp_at):
     basis_s[...] = jnp.zeros((16, 640), f32)
     basis_s[0:COMP, 0:528] = basis_ref[...]
     tile = exp_at // 8
@@ -84,34 +82,91 @@
     turn = (LANES - offset) % LANES
     wide = lanes_of((16, LANES))
     window = jnp.where(wide < LANES - offset, pltpu.roll(near, turn, 1), pltpu.roll(far, turn, 1))
-    turned = jnp.transpose(jnp.concatenate([window, jnp.zeros((LANES - 16, LANES), f32)], axis=0))
-    turned_s[...] = turned[0:32]
+    turned_s[...] = jnp.transpose(jnp.concatenate([window, jnp.zeros((LANES - 16, LANES), f32)], axis=0))[0:32]
+
+
+def tap_of(t, bands, masks):
+    tap = jnp.zeros((SUB, LANES), f32)
+    for s in range(2 * SHIFT + 1):
+        if 0 <= t - s < BAND:
+            tap = jnp.where(masks[s], bands[t - s], tap)
+    return tap
+
+
+def basis_at(t, turned_s):
+    upper = turned_s[t : t + SUB, :]
+    lower = turned_s[t + SUB : t + 2 * SUB, :]
+    return jnp.where(lanes_of() < HALF, upper, pltpu.roll(lower, HALF, 1))
+
+
+def model_copies(res_h, basis_h, shift_h, res_v, basis_v, shift_v, sems):
+    copies = [
+        pltpu.make_async_copy(source, target, sems.at[i])
+        for i, (source, target) in enumerate(((res_h, res_v), (basis_h, basis_v), (shift_h, shift_v)))
+    ]
+    for copy in copies:
+        copy.start()
+    return copies
+
+
+def sky_kernel(res_h, basis_h, shift_h, sky_h, pix_h, send_ref, first_ref, last_ref, res_v, basis_v, shift_v, sky_v, res_s, basis_s, row_s, turned_s, sems):
+    exp_at = lax.axis_index("exp")
+    ccd_at = lax.axis_index("ccd")
+    edges = [
+        pltpu.make_async_copy(pix_h.at[0:EDGE, :], first_ref, sems.at[4]),
+        pltpu.make_async_copy(pix_h.at[LOCAL - EDGE : LOCAL, :], last_ref, sems.at[5]),
+    ]
+    for edge in edges:
+        edge.start()
+    copies = model_copies(res_h, basis_h, shift_h, res_v, basis_v, shift_v, sems)
+    listed = pltpu.make_async_copy(sky_h, sky_v, sems.at[3])
+    listed.start()
+    listed.wait()
+    for copy in copies:
+        copy.wait()
+    lane = lanes_of()
+    fibre, comp, valid = sky_index(lane)
+    sky = sky_lanes(sky_v[...], row_s, ccd_at, fibre)
+    shift = pick(doubled(shift_v[...], row_s), sky) + SHIFT
+    masks = [shift == s for s in range(2 * SHIFT + 1)]
+    bands = [pick(band, sky) for band in banded(res_v, res_s)]
+    turned_basis(basis_v, basis_s, turned_s, exp_at)
+    total = jnp.zeros((SUB, LANES), f32)
+    for t in range(TAPS):
+        total = total + tap_of(t, bands, masks) * pick(basis_at(t, turned_s), (lane & HALF) + comp)
+    total = jnp.where(valid, total, 0.0)
+    send_ref[...] = jnp.broadcast_to(total[None], (EXPOS, SUB, LANES))
+    for edge in edges:
+        edge.wait()
+
+
+def model_kernel(res_h, basis_h, shift_h, model_ref, res_v, basis_v, shift_v, res_s, basis_s, row_s, turned_s, sems):
+    exp_at = lax.axis_index("exp")
+    for copy in model_copies(res_h, basis_h, shift_h, res_v, basis_v, shift_v, sems):
+        copy.wait()
+    lane = lanes_of()
+    shift = doubled(shift_v[...], row_s) + SHIFT
+    masks = [shift == s for s in range(2 * SHIFT + 1)]
+    bands = banded(res_v, res_s)
+    turned_basis(basis_v, basis_s, turned_s, exp_at)
     totals = [jnp.zeros((SUB, LANES), f32) for _ in range(COMP)]
     for t in range(TAPS):
-        tap = jnp.zeros((SUB, LANES), f32)
-        for s in range(2 * SHIFT + 1):
-            if 0 <= t - s < BAND:
-                tap = jnp.where(masks[s], bands[t - s], tap)
-        upper = turned_s[t : t + SUB, :]
-        lower = turned_s[t + SUB : t + 2 * SUB, :]
-        both = jnp.where(lane < HALF, upper, pltpu.roll(lower, HALF, 1))
+        tap = tap_of(t, bands, masks)
+        both = basis_at(t, turned_s)
         for k in range(COMP):
             totals[k] = totals[k] + tap * pick(both, (lane & HALF) + k)
     for k in range(COMP):
         model_ref[k] = totals[k]
-    fibre, comp, valid = sky_index(lane)
-    sky = by_sky(fibre, [sky_ref[ccd_at * SKYC + i] - ccd_at * FC for i in range(SKYC)])
-    source = (lane & HALF) + sky
-    out = jnp.zeros((SUB, LANES), f32)
-    for k in range(COMP):
-        out = jnp.where((comp == k) & valid, pick(totals[k], source), out)
-    send_ref[...] = jnp.broadcast_to(out[None], (EXPOS, SUB, LANES))
-
-
-def extract_kernel(pos_ref, sky_ref, slots_ref, pix_ref, before_ref, after_ref, psf_ref, slot_ref, flux_ref, weight_ref, skyflux_ref, pix_s, var_s, pad_s, flux_s, vari_s, row_s):
-    ccd_at = pos_ref[1]
+
+
+def extract_kernel(sky_h, slot_h, pix_ref, before_ref, after_ref, psf_ref, flux_ref, weight_ref, skyflux_ref, sky_v, slot_v, pix_s, var_s, pad_s, flux_s, vari_s, row_s, sems):
+    ccd_at = lax.axis_index("ccd")
     base = ccd_at * FC
     lane = lanes_of()
+    listed = pltpu.make_async_copy(sky_h, sky_v, sems.at[0])
+    slotted = pltpu.make_async_copy(slot_h, slot_v, sems.at[1])
+    listed.start()
+    slotted.start()
     pix_s[0:EDGE, :] = before_ref[...]
     pix_s[EDGE : EDGE + LOCAL, :] = pix_ref[...]
     pix_s[EDGE + LOCAL : 2 * EDGE + LOCAL, :] = after_ref[...]
@@ -125,15 +180,16 @@
         square = jnp.square(psf.astype(f32)).astype(jnp.bfloat16)
         pad_s[0:100, :] = jnp.dot(square, var_s[lower : lower + DEPTH, :], preferred_element_type=f32)
         vari_s[b] = jnp.transpose(pad_s[...])
-    slot = doubled(slot_ref, row_s)
+    listed.wait()
+    slotted.wait()
+    fibre, _, valid = sky_index(lane)
+    sky = sky_lanes(sky_v[...], row_s, ccd_at, fibre)
+    slot = doubled(slot_v[...], row_s)
     used = (lane & (HALF - 1)) < FC
     slot = jnp.where(used, slot - base, 0)
     second = slot >= FIBBLK
     place = jnp.where(second, slot - FIBBLK, slot) * ROWS
-    fibre, _, valid = sky_index(lane)
-    local = [sky_ref[ccd_at * SKYC + i] - base for i in range(SKYC)]
-    sky = (lane & HALF) + by_sky(fibre, local)
-    sky_slot = by_sky(fibre, [slots_ref[f] - base for f in local])
+    sky_slot = pick(slot, sky)
     sky_second = sky_slot >= FIBBLK
     sky_place = jnp.where(sky_second, sky_slot - FIBBLK, sky_slot) * ROWS
 
@@ -191,10 +247,11 @@
         out_ref[e] = jnp.where(here, coeffs, flux_ref[e])
 
 
-def subtract_kernel(flux_ref, model_ref, out_ref, noise_ref, left_s):
+def subtract_kernel(flux_ref, model_ref, out_h, noise_ref, left_s, out_s, sems):
     models = [model_ref[k] for k in range(COMP)]
     spots = [jnp.full((SUB, LANES), FC + k, jnp.int32) for k in range(COMP)]
     total = jnp.zeros((SUB, LANES), f32)
+    copies = []
     for e in range(EXPOS):
         left = flux_ref[e]
         sky = pick(left, spots[0]) * models[0]
@@ -203,8 +260,12 @@
         left = left - sky
         left_s[e] = left
         total = total + left
-        out_ref[e, 0:SUB, :] = left[:, 0:FC]
-        out_ref[e, SUB:CHUNK, :] = pltpu.roll(left, HALF, 1)[:, 0:FC]
+        out_s[e, 0:SUB, :] = left[:, 0:FC]
+        out_s[e, SUB:CHUNK, :] = pltpu.roll(left, HALF, 1)[:, 0:FC]
+        if e % PIECE == PIECE - 1:
+            at = pl.ds(e + 1 - PIECE, PIECE)
+            copies.append(pltpu.make_async_copy(out_s.at[at], out_h.at[at], sems.at[e // PIECE]))
+            copies[-1].start()
     mean = total * (1.0 / EXPOS)
     spread = jnp.zeros((SUB, LANES), f32)
     for e in range(EXPOS):
@@ -212,48 +273,68 @@
     noise = jnp.sqrt(spread * (1.0 / EXPOS) + 1e-06)
     noise_ref[0:SUB, :] = noise[:, 0:FC]
     noise_ref[SUB:CHUNK, :] = pltpu.roll(noise, HALF, 1)[:, 0:FC]
+    for copy in copies:
+        copy.wait()
 
 
 VMEM = pl.BlockSpec(memory_space=pltpu.VMEM)
-SMEM = pl.BlockSpec(memory_space=pltpu.SMEM)
+HBM = pl.BlockSpec(memory_space=pltpu.HBM)
 TILES = jax.ShapeDtypeStruct((EXPOS, SUB, LANES), f32)
+EDGES = jax.ShapeDtypeStruct((EDGE, GROUPS), jnp.bfloat16)
 PARAMS = pltpu.CompilerParams(vmem_limit_bytes=40 * 1024 * 1024)
-
-
-def local_model(pos, sky_fibres, resolution, basis, band_shift):
+MODEL_INPUTS = [pltpu.VMEM((BAND, CHUNK, FC), f32), pltpu.VMEM((COMP, 528), f32), pltpu.VMEM((1, FC), jnp.int32)]
+MODEL_SCRATCH = [
+    pltpu.VMEM((BAND, SUB, LANES), f32),
+    pltpu.VMEM((16, 640), f32),
+    pltpu.VMEM((SUB, LANES), jnp.int32),
+    pltpu.VMEM((32, LANES), f32),
+]
+
+
+def sky_model(resolution, basis, shift, sky, pixels):
+    return pl.pallas_call(
+        sky_kernel,
+        out_shape=(TILES, EDGES, EDGES),
+        in_specs=[HBM] * 5,
+        out_specs=(VMEM, VMEM, VMEM),
+        scratch_shapes=MODEL_INPUTS + [pltpu.VMEM((1, 96), jnp.int32)] + MODEL_SCRATCH + [pltpu.SemaphoreType.DMA((6,))],
+        compiler_params=PARAMS,
+        name="sky_model",
+    )(*(pltpu.with_memory_space_constraint(v, pltpu.HBM) for v in (resolution, basis, shift, sky, pixels)))
+
+
+def local_model(resolution, basis, shift):
     return pl.pallas_call(
         model_kernel,
-        out_shape=(TILES, jax.ShapeDtypeStruct((COMP, SUB, LANES), f32)),
-        in_specs=[SMEM, SMEM, VMEM, VMEM, VMEM],
-        out_specs=(VMEM, VMEM),
-        scratch_shapes=[
-            pltpu.VMEM((BAND, SUB, LANES), f32),
-            pltpu.VMEM((16, 640), f32),
-            pltpu.VMEM((SUB, LANES), jnp.int32),
-            pltpu.VMEM((32, LANES), f32),
-        ],
+        out_shape=jax.ShapeDtypeStruct((COMP, SUB, LANES), f32),
+        in_specs=[HBM] * 3,
+        out_specs=VMEM,
+        scratch_shapes=MODEL_INPUTS + MODEL_SCRATCH + [pltpu.SemaphoreType.DMA((3,))],
         compiler_params=PARAMS,
-        name="model",
-    )(pos, sky_fibres, resolution.transpose(1, 2, 0), basis, band_shift.reshape(1, FC))
-
-
-def extract(pos, sky_fibres, fibre_slot, pixels, before, after, psf):
+        name="local_model",
+    )(*(pltpu.with_memory_space_constraint(v, pltpu.HBM) for v in (resolution, basis, shift)))
+
+
+def extract(sky, slot, pixels, before, after, psf):
     return pl.pallas_call(
         extract_kernel,
         out_shape=(TILES, TILES, TILES),
-        in_specs=[SMEM, SMEM, SMEM, VMEM, VMEM, VMEM, VMEM, VMEM],
+        in_specs=[HBM, HBM, VMEM, VMEM, VMEM, VMEM],
         out_specs=(VMEM, VMEM, VMEM),
         scratch_shapes=[
+            pltpu.VMEM((1, 96), jnp.int32),
+            pltpu.VMEM((1, FC), jnp.int32),
             pltpu.VMEM((2 * EDGE + LOCAL, LANES), jnp.bfloat16),
             pltpu.VMEM((2 * EDGE + LOCAL, LANES), jnp.bfloat16),
             pltpu.VMEM((LANES, LANES), f32),
             pltpu.VMEM((2, LANES, LANES), f32),
             pltpu.VMEM((2, LANES, LANES), f32),
             pltpu.VMEM((SUB, LANES), jnp.int32),
+            pltpu.SemaphoreType.DMA((2,)),
         ],
         compiler_params=PARAMS,
         name="extract",
-    )(pos, sky_fibres, fibre_slot, pixels, before, after, psf, fibre_slot.reshape(1, FC))
+    )(*(pltpu.with_memory_space_constraint(v, pltpu.HBM) for v in (sky, slot)), pixels, before, after, psf)
 
 
 def gram_parts(model, weight, flux, copies):
@@ -278,8 +359,12 @@
         subtract_kernel,
         out_shape=(jax.ShapeDtypeStruct((EXPOS, CHUNK, FC), f32), jax.ShapeDtypeStruct((CHUNK, FC), f32)),
         in_specs=[VMEM, VMEM],
-        out_specs=(VMEM, VMEM),
-        scratch_shapes=[pltpu.VMEM((EXPOS, SUB, LANES), f32)],
+        out_specs=(HBM, VMEM),
+        scratch_shapes=[
+            pltpu.VMEM((EXPOS, SUB, LANES), f32),
+            pltpu.VMEM((EXPOS, CHUNK, FC), f32),
+            pltpu.SemaphoreType.DMA((EXPOS // PIECE,)),
+        ],
         compiler_params=PARAMS,
         name="subtract",
     )(flux, model)
@@ -288,16 +373,21 @@
 def shards(pixels, psf_proj, resolution, basis, sky_fibres, fibre_slot, band_shift):
     size = lax.axis_size("ccd")
     rows = pixels.reshape(LOCAL, GROUPS)
+    res = resolution.transpose(1, 2, 0)
+    sky = sky_fibres.reshape(1, -1)
+    slot = fibre_slot.reshape(1, FC)
+    shift = band_shift.reshape(1, FC)
     up = [(i, i + 1) for i in range(size - 1)]
     down = [(j, i) for i, j in up]
-    before = lax.ppermute(rows[LOCAL - EDGE :], "ccd", up)
-    after = lax.ppermute(rows[:EDGE], "ccd", down)
-    pos = jnp.stack([lax.axis_index("exp"), lax.axis_index("ccd")]).astype(jnp.int32)
-    send, model = local_model(pos, sky_fibres, resolution, basis, band_shift)
-    sky_model = lax.all_to_all(send, "exp", split_axis=0, concat_axis=0, tiled=True)
-    flux, weight, sky_flux = extract(pos, sky_fibres, fibre_slot, rows, before, after, psf_proj)
-    parts = gram_parts(sky_model, weight, sky_flux, size)
+    send, first, last = sky_model(res, basis, shift, sky, rows)
+    before = lax.ppermute(last, "ccd", up)
+    after = lax.ppermute(first, "ccd", down)
+    model = lax.all_to_all(send, "exp", split_axis=0, concat_axis=0, tiled=True)
+    flux, weight, sky_flux = extract(sky, slot, rows, before, after, psf_proj)
+    parts = gram_parts(model, weight, sky_flux, size)
+    res, parts = lax.optimization_barrier((res, parts))
     parts = lax.all_to_all(parts, "ccd", split_axis=0, concat_axis=0, tiled=True)
+    model = local_model(res, basis, shift)
     flux = solve(parts, flux)
     flux = lax.all_to_all(flux, "exp", split_axis=0, concat_axis=0, tiled=True)
     sky_subtracted, noise_rms = subtract(flux, model)

time: 72.2 us -> 69 us (0.956)
  blocking collectives: 37.1 us -> 17.8 us
  starting transfers between devices: 17.5 us -> 28 us
  waiting for transfers between devices: 2.26 us -> 10.7 us
  local copies, waits for them, and re-layouts: 5.01 us -> 0.1 us
  Pallas kernels: 8.92 us -> 11.3 us
    all_to_all x1 -> x0, blocking collectives: 19.4 us -> none  [shards(): flux = lax.all_to_all(flux, 'exp', split_axis=0, concat_axis=0, tiled=True)]
    all_to_all x1 -> x2, starting transfers between devices: 13 us -> 23.5 us  [the longest x1 13 us: shards(): model = lax.all_to_all(send, 'exp', split_axis=0, concat_axis=0, tiled=True)]
    all_to_all x1 -> x2, waiting for transfers between devices: 0.01 us -> 7.29 us  [the longest x1 7.29 us: shards(): flux = lax.all_to_all(flux, 'exp', split_axis=0, concat_axis=0, tiled=True)]
    unnamed x13 -> x5, local copies, waits for them, and re-layouts: 4.25 us -> 0.1 us
    pallas_call x1 -> x2, Pallas kernels: 2.13 us -> 3.82 us  [the longest x1 2.05 us: sky_model(): pl.pallas_call(sky_kernel, out_shape=(TILES, EDGES, EDGES), in_specs=[HBM...]
    ppermute x2, waiting for transfers between devices: 2.25 us -> 3.4 us  [the longest x1 3.4 us: shards(): after = lax.ppermute(first, 'ccd', down)]
    slice x1 -> x0, local copies, waits for them, and re-layouts: 0.76 us -> none  [shards(): after = lax.ppermute(rows[:EDGE], 'ccd', down)]
  transfers between devices with their start and end apart: 3 -> 4, of which waited for: 1 -> 2; matrix products, arithmetic and copies ran while one was open for 3% -> 0% of each run, Pallas kernels for 3% -> 5%
where the time goes in v2:
time: 69 us; the launch traced here: 68.6 us
  starting transfers between devices  28 us (41%)
  blocking collectives  17.8 us (26%)
  Pallas kernels  11.3 us (16%)
  waiting for transfers between devices  10.7 us (16%)
  between operations  0.74 us (1%)
    all_to_all x1, blocking collectives, shards(): lax.all_to_all(parts, 'ccd', split_axis=0, concat_axis=0, tiled=True)  17.8 us
    all_to_all x1, starting transfers between devices, shards(): model = lax.all_to_all(send, 'exp', split_axis=0, concat_axis=0, tiled=True)  13 us
    all_to_all x1, starting transfers between devices, shards(): flux = lax.all_to_all(flux, 'exp', split_axis=0, concat_axis=0, tiled=True)  10.4 us
    all_to_all x1, waiting for transfers between devices, shards(): flux = lax.all_to_all(flux, 'exp', split_axis=0, concat_axis=0, tiled=True)  7.29 us
    ppermute x1, waiting for transfers between devices, shards(): after = lax.ppermute(first, 'ccd', down)  3.4 us
    pallas_call x1, Pallas kernels, subtract(): pl.pallas_call(subtract_kernel, out_shape=(jax.ShapeDtypeStruct((EXPOS, C...  3.38 us
    ppermute x1, starting transfers between devices, shards(): before = lax.ppermute(last, 'ccd', up)  3.2 us
    pallas_call x1, Pallas kernels, sky_model(): pl.pallas_call(sky_kernel, out_shape=(TILES, EDGES, EDGES), in_specs=[HBM...  2.05 us
  transfers between devices with their start and end apart: 4, of which 2 were waited for; matrix products, arithmetic and copies ran while one was open for 0% of the time, Pallas kernels for 5%

profile of v2, /device:TPU:1, one launch (start us, length us, event | category | flops | bytes accessed | tf_op | source)
XLA Modules:
  0.0 68.6 jit_solution(12724721579088693592)
XLA Ops:
  0.6 0.0 copy-start.1
  0.6 2.1 %sky_model.1 = (f32[32,8,128]{2,1,0:T(8,128)}, bf16[80,128]{1,0:T(8,128)(2,1)S(1)}, bf16[80,128]{1,0:T(8,128)(2,1)S(1)}) custom-call(f32[11,16,50]{2,1,0:T(8,128)} %bitcast.9, f32[10,528]{1,0:T(8,128)} %basis_h.3, s32[1,50]{1,0:T(1,128)} %bitcast.13, s32[1,96]{1,0:T(1,128)} %bitcast.11, bf16[4000,128]{1,0:T(8,128)(2,1)} %bitcast.7), custom_call_target="tpu_custom_call" | custom-call | tf_op jit(solution)/shard_map/sky_model/pallas_call | solution.py:295
  2.7 0.0 copy-start
  2.7 13.0 %all-to-all-start = ((f32[32,8,128]{2,1,0:T(8,128)}), f32[32,8,128]{2,1,0:T(8,128)S(1)}, u32[]{:S(2)}, u32[]{:S(2)}) async-start(f32[32,8,128]{2,1,0:T(8,128)} %get-tuple-element.12), calls=%async_computation | async-start | bytes 262144 | tf_op jit(solution)/shard_map/all_to_all | solution.py:385
  15.8 3.2 %collective-permute-start = (bf16[80,128]{1,0:T(8,128)(2,1)S(1)}, bf16[80,128]{1,0:T(8,128)(2,1)S(1)}, u32[]{:S(2)}, u32[]{:S(2)}) collective-permute-start(bf16[80,128]{1,0:T(8,128)(2,1)S(1)} %get-tuple-element.13), channel_id=1, source_target_pairs={{0,1},{1,2},{2,3},{3,4},{4,5},{5,6},{6,7},{7,8},{8,9},{9,10},{10,1... | collective-permute-start | bytes 61448 | tf_op jit(solution)/shard_map/ppermute | solution.py:383
  19.0 1.3 %collective-permute-start.1 = (bf16[80,128]{1,0:T(8,128)(2,1)S(1)}, bf16[80,128]{1,0:T(8,128)(2,1)S(1)}, u32[]{:S(2)}, u32[]{:S(2)}) collective-permute-start(bf16[80,128]{1,0:T(8,128)(2,1)S(1)} %get-tuple-element.14), channel_id=1, source_target_pairs={{1,0},{2,1},{3,2},{4,3},{5,4},{6,5},{7,6},{8,7},{9,8},{10,9},{11,1... | collective-permute-start | bytes 61448 | tf_op jit(solution)/shard_map/ppermute | solution.py:384
  20.3 0.0 copy-done.1
  20.3 0.1 copy.9.psf_ref
  20.4 0.0 collective-permute-done.before_ref
  20.4 3.4 %collective-permute-done.1.after_ref = bf16[80,128]{1,0:T(8,128)(2,1)S(1)} collective-permute-done((bf16[80,128]{1,0:T(8,128)(2,1)S(1)}, bf16[80,128]{1,0:T(8,128)(2,1)S(1)}, u32[]{:S(2)}, u32[]{:S(2)}) %collective-permute-start.1) | collective-permute-done | bytes 20512 | tf_op jit(solution)/shard_map/ppermute | solution.py:384
  23.8 0.0 copy-done
  23.8 1.7 %extract.1 = (f32[32,8,128]{2,1,0:T(8,128)S(1)}, f32[32,8,128]{2,1,0:T(8,128)S(1)}, f32[32,8,128]{2,1,0:T(8,128)S(1)}) custom-call(s32[1,96]{1,0:T(1,128)} %bitcast.12, s32[1,50]{1,0:T(1,128)} %bitcast.15, bf16[4000,128]{1,0:T(8,128)(2,1)S(1)} %bitcast.8, bf16[80,128]{1,0:T(8,128)(2,1)S(1)} %collective-permute-done.before_ref, ...), custom_call_target="tpu_custom_call" | custom-call | tf_op jit(solution)/shard_map/extract/pallas_call | solution.py:319
  25.5 0.0 all-to-all-done.model_ref
  25.5 0.9 %gram.1 = f32[16,8,128]{2,1,0:T(8,128)S(1)} custom-call(f32[32,8,128]{2,1,0:T(8,128)S(1)} %all-to-all-done.model_ref, f32[32,8,128]{2,1,0:T(8,128)S(1)} %get-tuple-element.15.weight_ref, f32[32,8,128]{2,1,0:T(8,128)S(1)} %get-tuple-element.16.flux_ref), custom_call_target="tpu_custom_call" | custom-call | tf_op jit(solution)/shard_map/gram/pallas_call | solution.py:341
  26.4 17.8 %all_to_all.15.parts_ref = f32[16,8,128]{2,1,0:T(8,128)S(1)} all-to-all(f32[16,8,128]{2,1,0:T(8,128)S(1)} %gram.1), channel_id=1, replica_groups=mesh['exp'=32,'ccd'=16] {'ccd'}, dimensions={0} | all-to-all | bytes 131072 | tf_op jit(solution)/shard_map/all_to_all | solution.py:389
  44.2 1.5 %solve.1 = f32[32,8,128]{2,1,0:T(8,128)} custom-call(f32[16,8,128]{2,1,0:T(8,128)S(1)} %all_to_all.15.parts_ref, f32[32,8,128]{2,1,0:T(8,128)S(1)} %get-tuple-element.18.flux_ref), custom_call_target="tpu_custom_call" | custom-call | tf_op jit(solution)/shard_map/solve/pallas_call | solution.py:352
  45.8 10.4 %all-to-all-start.2 = ((f32[32,8,128]{2,1,0:T(8,128)}), f32[32,8,128]{2,1,0:T(8,128)S(1)}, u32[]{:S(2)}, u32[]{:S(2)}) async-start(f32[32,8,128]{2,1,0:T(8,128)} %solve.1), calls=%async_computation.2 | async-start | bytes 262144 | tf_op jit(solution)/shard_map/all_to_all | solution.py:392
  56.2 1.8 %local_model.1.model_ref = f32[10,8,128]{2,1,0:T(8,128)S(1)} custom-call(f32[11,16,50]{2,1,0:T(8,128)} %bitcast.10, f32[10,528]{1,0:T(8,128)} %basis_h.3, s32[1,50]{1,0:T(1,128)} %bitcast.14), custom_call_target="tpu_custom_call" | custom-call | tf_op jit(solution)/shard_map/local_model/pallas_call | solution.py:307
  58.0 7.3 %all-to-all-done.2.flux_ref = f32[32,8,128]{2,1,0:T(8,128)S(1)} async-done(((f32[32,8,128]{2,1,0:T(8,128)}), f32[32,8,128]{2,1,0:T(8,128)S(1)}, u32[]{:S(2)}, u32[]{:S(2)}) %all-to-all-start.2) | async-done | bytes 131104 | tf_op jit(solution)/shard_map/all_to_all | solution.py:392
  65.2 3.4 %subtract.1 = (f32[32,16,50]{2,1,0:T(8,128)}, f32[16,50]{1,0:T(8,128)}) custom-call(f32[32,8,128]{2,1,0:T(8,128)S(1)} %all-to-all-done.2.flux_ref, f32[10,8,128]{2,1,0:T(8,128)S(1)} %local_model.1.model_ref), custom_call_target="tpu_custom_call" | custom-call | tf_op jit(solution)/shard_map/subtract/pallas_call | solution.py:358
Async XLA Ops:
  0.6 19.6 %copy-start.1 = (bf16[2,100,2160]{2,0,1:T(2,128)(2,1)S(1)}, bf16[2,100,2160]{2,0,1:T(2,128)(2,1)}, u32[]{:S(2)}) copy-start(bf16[2,100,2160]{2,0,1:T(2,128)(2,1)} %param.8) | copy-start | bytes 2592004
  2.7 21.1 %copy-start = (bf16[1,1000,4,128]{3,2,1,0:T(4,128)(2,1)S(1)}, bf16[1,1000,4,128]{3,2,1,0:T(4,128)(2,1)}, u32[]{:S(2)}) copy-start(bf16[1,1000,4,128]{3,2,1,0:T(4,128)(2,1)} %param.7) | copy-start | bytes 3072004
  2.7 22.8 %all-to-all-start = ((f32[32,8,128]{2,1,0:T(8,128)}), f32[32,8,128]{2,1,0:T(8,128)S(1)}, u32[]{:S(2)}, u32[]{:S(2)}) async-start(f32[32,8,128]{2,1,0:T(8,128)} %get-tuple-element.12), calls=%async_computation | async-start | bytes 262144 | tf_op jit(solution)/shard_map/all_to_all | solution.py:385
  15.8 4.6 %collective-permute-start = (bf16[80,128]{1,0:T(8,128)(2,1)S(1)}, bf16[80,128]{1,0:T(8,128)(2,1)S(1)}, u32[]{:S(2)}, u32[]{:S(2)}) collective-permute-start(bf16[80,128]{1,0:T(8,128)(2,1)S(1)} %get-tuple-element.13), channel_id=1, source_target_pairs={{0,1},{1,2},{2,3},{3,4},{4,5},{5,6},{6,7},{7,8},{8,9},{9,10},{10,1... | collective-permute-start | bytes 61448 | tf_op jit(solution)/shard_map/ppermute | solution.py:383
  19.0 4.8 %collective-permute-start.1 = (bf16[80,128]{1,0:T(8,128)(2,1)S(1)}, bf16[80,128]{1,0:T(8,128)(2,1)S(1)}, u32[]{:S(2)}, u32[]{:S(2)}) collective-permute-start(bf16[80,128]{1,0:T(8,128)(2,1)S(1)} %get-tuple-element.14), channel_id=1, source_target_pairs={{1,0},{2,1},{3,2},{4,3},{5,4},{6,5},{7,6},{8,7},{9,8},{10,9},{11,1... | collective-permute-start | bytes 61448 | tf_op jit(solution)/shard_map/ppermute | solution.py:384
  45.8 19.5 %all-to-all-start.2 = ((f32[32,8,128]{2,1,0:T(8,128)}), f32[32,8,128]{2,1,0:T(8,128)S(1)}, u32[]{:S(2)}, u32[]{:S(2)}) async-start(f32[32,8,128]{2,1,0:T(8,128)} %solve.1), calls=%async_computation.2 | async-start | bytes 262144 | tf_op jit(solution)/shard_map/all_to_all | solution.py:392

commit v3 on v2

--- a/solution.py
+++ b/solution.py
@@ -109,12 +109,15 @@
     return copies
 
 
-def sky_kernel(res_h, basis_h, shift_h, sky_h, pix_h, send_ref, first_ref, last_ref, res_v, basis_v, shift_v, sky_v, res_s, basis_s, row_s, turned_s, sems):
+def sky_kernel(res_h, basis_h, shift_h, sky_h, pix_h, send_ref, near_ref, far_ref, res_v, basis_v, shift_v, sky_v, res_s, basis_s, row_s, turned_s, sems):
     exp_at = lax.axis_index("exp")
     ccd_at = lax.axis_index("ccd")
+    odd = ccd_at % 2
+    at_near = pl.multiple_of(odd * (LOCAL - EDGE), EDGE)
+    at_far = pl.multiple_of((1 - odd) * (LOCAL - EDGE), EDGE)
     edges = [
-        pltpu.make_async_copy(pix_h.at[0:EDGE, :], first_ref, sems.at[4]),
-        pltpu.make_async_copy(pix_h.at[LOCAL - EDGE : LOCAL, :], last_ref, sems.at[5]),
+        pltpu.make_async_copy(pix_h.at[pl.ds(at_near, EDGE), :], near_ref, sems.at[4]),
+        pltpu.make_async_copy(pix_h.at[pl.ds(at_far, EDGE), :], far_ref, sems.at[5]),
     ]
     for edge in edges:
         edge.start()
@@ -159,7 +162,7 @@
         model_ref[k] = totals[k]
 
 
-def extract_kernel(sky_h, slot_h, pix_ref, before_ref, after_ref, psf_ref, flux_ref, weight_ref, skyflux_ref, sky_v, slot_v, pix_s, var_s, pad_s, flux_s, vari_s, row_s, sems):
+def extract_kernel(sky_h, slot_h, pix_ref, near_ref, far_ref, psf_ref, flux_ref, weight_ref, skyflux_ref, sky_v, slot_v, pix_s, var_s, pad_s, flux_s, vari_s, row_s, sems):
     ccd_at = lax.axis_index("ccd")
     base = ccd_at * FC
     lane = lanes_of()
@@ -167,9 +170,10 @@
     slotted = pltpu.make_async_copy(slot_h, slot_v, sems.at[1])
     listed.start()
     slotted.start()
-    pix_s[0:EDGE, :] = before_ref[...]
+    odd = ccd_at % 2
+    pix_s[pl.ds(pl.multiple_of(odd * (EDGE + LOCAL), EDGE), EDGE), :] = near_ref[...]
     pix_s[EDGE : EDGE + LOCAL, :] = pix_ref[...]
-    pix_s[EDGE + LOCAL : 2 * EDGE + LOCAL, :] = after_ref[...]
+    pix_s[pl.ds(pl.multiple_of((1 - odd) * (EDGE + LOCAL), EDGE), EDGE), :] = far_ref[...]
     var_s[...] = (0.25 + jnp.square(pix_s[...].astype(f32))).astype(jnp.bfloat16)
     pad_s[...] = jnp.zeros((LANES, LANES), f32)
     for b in range(2):
@@ -315,7 +319,7 @@
     )(*(pltpu.with_memory_space_constraint(v, pltpu.HBM) for v in (resolution, basis, shift)))
 
 
-def extract(sky, slot, pixels, before, after, psf):
+def extract(sky, slot, pixels, near, far, psf):
     return pl.pallas_call(
         extract_kernel,
         out_shape=(TILES, TILES, TILES),
@@ -334,7 +338,7 @@
         ],
         compiler_params=PARAMS,
         name="extract",
-    )(*(pltpu.with_memory_space_constraint(v, pltpu.HBM) for v in (sky, slot)), pixels, before, after, psf)
+    )(*(pltpu.with_memory_space_constraint(v, pltpu.HBM) for v in (sky, slot)), pixels, near, far, psf)
 
 
 def gram_parts(model, weight, flux, copies):
@@ -377,17 +381,17 @@
     sky = sky_fibres.reshape(1, -1)
     slot = fibre_slot.reshape(1, FC)
     shift = band_shift.reshape(1, FC)
-    up = [(i, i + 1) for i in range(size - 1)]
-    down = [(j, i) for i, j in up]
-    send, first, last = sky_model(res, basis, shift, sky, rows)
-    before = lax.ppermute(last, "ccd", up)
-    after = lax.ppermute(first, "ccd", down)
-    model = lax.all_to_all(send, "exp", split_axis=0, concat_axis=0, tiled=True)
-    flux, weight, sky_flux = extract(sky, slot, rows, before, after, psf_proj)
-    parts = gram_parts(model, weight, sky_flux, size)
-    res, parts = lax.optimization_barrier((res, parts))
+    pairs = [[(i, i + 1) for i in range(start, size - 1, 2)] for start in (1, 0)]
+    swaps = [[*pair, *((j, i) for i, j in pair)] for pair in pairs]
+    send, near, far = sky_model(res, basis, shift, sky, rows)
+    near = lax.ppermute(near, "ccd", swaps[0])
+    far = lax.ppermute(far, "ccd", swaps[1])
+    model = local_model(res, basis, shift)
+    near, far, model = lax.optimization_barrier((near, far, model))
+    sky_tiles = lax.all_to_all(send, "exp", split_axis=0, concat_axis=0, tiled=True)
+    flux, weight, sky_flux = extract(sky, slot, rows, near, far, psf_proj)
+    parts = gram_parts(sky_tiles, weight, sky_flux, size)
     parts = lax.all_to_all(parts, "ccd", split_axis=0, concat_axis=0, tiled=True)
-    model = local_model(res, basis, shift)
     flux = solve(parts, flux)
     flux = lax.all_to_all(flux, "exp", split_axis=0, concat_axis=0, tiled=True)
     sky_subtracted, noise_rms = subtract(flux, model)

time: 69 us -> 67.4 us (0.977)
  blocking collectives: 17.8 us -> 35.6 us
  waiting for transfers between devices: 10.7 us -> 0.01 us
  starting transfers between devices: 28 us -> 19.5 us
    all_to_all x0 -> x1, blocking collectives: none -> 19.1 us  [shards(): flux = lax.all_to_all(flux, 'exp', split_axis=0, concat_axis=0, tiled=True)]
    all_to_all x2 -> x1, starting transfers between devices: 23.5 us -> 12.9 us  [shards(): lax.all_to_all(send, 'exp', split_axis=0, concat_axis=0, tiled=True)]
    all_to_all x2 -> x1, waiting for transfers between devices: 7.29 us -> 0.01 us  [shards(): lax.all_to_all(send, 'exp', split_axis=0, concat_axis=0, tiled=True)]
    ppermute x2, waiting for transfers between devices: 3.4 us -> 0.01 us  [the longest x1 0.01 us: shards(): far = lax.ppermute(far, 'ccd', swaps[1])]
    ppermute x2, starting transfers between devices: 4.49 us -> 6.54 us  [the longest x1 5.75 us: shards(): far = lax.ppermute(far, 'ccd', swaps[1])]
    all_to_all x1, blocking collectives: 17.8 us -> 16.5 us  [shards(): lax.all_to_all(parts, 'ccd', split_axis=0, concat_axis=0, tiled=True)]
    pallas_call x1, Pallas kernels: 1.54 us -> 0.83 us  [solve(): pl.pallas_call(solve_kernel, out_shape=TILES, in_specs=[VMEM, VMEM], out_...]
  transfers between devices with their start and end apart: 4 -> 3, of which waited for: 2 -> 0; matrix products, arithmetic and copies ran while one was open for 0% -> 0% of each run, Pallas kernels for 5% -> 6%
where the time goes in v3:
time: 67.4 us; the launch traced here: 67 us
  blocking collectives  35.6 us (53%)
  starting transfers between devices  19.5 us (29%)
  Pallas kernels  11.1 us (16%)
  between operations  0.8 us (1%)
    all_to_all x1, blocking collectives, shards(): flux = lax.all_to_all(flux, 'exp', split_axis=0, concat_axis=0, tiled=True)  19.1 us
    all_to_all x1, blocking collectives, shards(): lax.all_to_all(parts, 'ccd', split_axis=0, concat_axis=0, tiled=True)  16.5 us
    all_to_all x1, starting transfers between devices, shards(): lax.all_to_all(send, 'exp', split_axis=0, concat_axis=0, tiled=True)  12.9 us
    ppermute x1, starting transfers between devices, shards(): far = lax.ppermute(far, 'ccd', swaps[1])  5.75 us
    pallas_call x1, Pallas kernels, subtract(): pl.pallas_call(subtract_kernel, out_shape=(jax.ShapeDtypeStruct((EXPOS, C...  3.38 us
    pallas_call x1, Pallas kernels, extract(): pl.pallas_call(extract_kernel, out_shape=(TILES, TILES, TILES), in_specs=...  2.13 us
    pallas_call x1, Pallas kernels, sky_model(): pl.pallas_call(sky_kernel, out_shape=(TILES, EDGES, EDGES), in_specs=[HBM...  2.06 us
    pallas_call x1, Pallas kernels, local_model(): pl.pallas_call(model_kernel, out_shape=jax.ShapeDtypeStruct((COMP, SUB, L...  1.77 us
  transfers between devices with their start and end apart: 3, of which 0 were waited for; matrix products, arithmetic and copies ran while one was open for 0% of the time, Pallas kernels for 6%

profile of v3, /device:TPU:1, one launch (start us, length us, event | category | flops | bytes accessed | tf_op | source)
XLA Modules:
  0.0 67.0 jit_solution(5605320359724417858)
XLA Ops:
  0.6 0.0 copy-start.1
  0.6 2.1 %sky_model.1 = (f32[32,8,128]{2,1,0:T(8,128)}, bf16[80,128]{1,0:T(8,128)(2,1)S(1)}, bf16[80,128]{1,0:T(8,128)(2,1)S(1)}) custom-call(f32[11,16,50]{2,1,0:T(8,128)} %bitcast.9, f32[10,528]{1,0:T(8,128)} %basis_h.3, s32[1,50]{1,0:T(1,128)} %bitcast.11, s32[1,96]{1,0:T(1,128)} %bitcast.13, bf16[4000,128]{1,0:T(8,128)(2,1)} %bitcast.7), custom_call_target="tpu_custom_call" | custom-call | tf_op jit(solution)/shard_map/sky_model/pallas_call | solution.py:299
  2.7 12.9 %all-to-all-start = ((f32[32,8,128]{2,1,0:T(8,128)}), f32[32,8,128]{2,1,0:T(8,128)S(1)}, u32[]{:S(2)}, u32[]{:S(2)}) async-start(f32[32,8,128]{2,1,0:T(8,128)} %get-tuple-element.13), calls=%async_computation | async-start | bytes 262144 | tf_op jit(solution)/shard_map/all_to_all | solution.py:391
  15.6 0.0 copy-start
  15.6 0.8 %collective-permute-start = (bf16[80,128]{1,0:T(8,128)(2,1)S(1)}, bf16[80,128]{1,0:T(8,128)(2,1)S(1)}, u32[]{:S(2)}, u32[]{:S(2)}) collective-permute-start(bf16[80,128]{1,0:T(8,128)(2,1)S(1)} %get-tuple-element.14), channel_id=1, source_target_pairs={{1,2},{3,4},{5,6},{7,8},{9,10},{11,12},{13,14},{2,1},{4,3},{6,5},{... | collective-permute-start | bytes 61448 | tf_op jit(solution)/shard_map/ppermute | solution.py:387
  16.4 5.7 %collective-permute-start.1 = (bf16[80,128]{1,0:T(8,128)(2,1)S(1)}, bf16[80,128]{1,0:T(8,128)(2,1)S(1)}, u32[]{:S(2)}, u32[]{:S(2)}) collective-permute-start(bf16[80,128]{1,0:T(8,128)(2,1)S(1)} %get-tuple-element.15), channel_id=1, source_target_pairs={{0,1},{2,3},{4,5},{6,7},{8,9},{10,11},{12,13},{14,15},{1,0},{3,2},... | collective-permute-start | bytes 61448 | tf_op jit(solution)/shard_map/ppermute | solution.py:388
  22.2 1.8 %local_model.1.model_ref = f32[10,8,128]{2,1,0:T(8,128)S(1)} custom-call(f32[11,16,50]{2,1,0:T(8,128)} %bitcast.10, f32[10,528]{1,0:T(8,128)} %basis_h.3, s32[1,50]{1,0:T(1,128)} %bitcast.12), custom_call_target="tpu_custom_call" | custom-call | tf_op jit(solution)/shard_map/local_model/pallas_call | solution.py:311
  24.0 0.0 copy-done.1
  24.0 0.1 copy.9.psf_ref
  24.1 0.0 collective-permute-done.near_ref
  24.1 0.0 collective-permute-done.1.far_ref
  24.1 0.0 copy-done
  24.1 2.1 %extract.1 = (f32[32,8,128]{2,1,0:T(8,128)S(1)}, f32[32,8,128]{2,1,0:T(8,128)S(1)}, f32[32,8,128]{2,1,0:T(8,128)S(1)}) custom-call(s32[1,96]{1,0:T(1,128)} %bitcast.14, s32[1,50]{1,0:T(1,128)} %bitcast.15, bf16[4000,128]{1,0:T(8,128)(2,1)S(1)} %bitcast.8, bf16[80,128]{1,0:T(8,128)(2,1)S(1)} %collective-permute-done.near_ref, ...), custom_call_target="tpu_custom_call" | custom-call | tf_op jit(solution)/shard_map/extract/pallas_call | solution.py:323
  26.3 0.0 all-to-all-done.model_ref
  26.3 0.9 %gram.1 = f32[16,8,128]{2,1,0:T(8,128)S(1)} custom-call(f32[32,8,128]{2,1,0:T(8,128)S(1)} %all-to-all-done.model_ref, f32[32,8,128]{2,1,0:T(8,128)S(1)} %get-tuple-element.18.weight_ref, f32[32,8,128]{2,1,0:T(8,128)S(1)} %get-tuple-element.19.flux_ref), custom_call_target="tpu_custom_call" | custom-call | tf_op jit(solution)/shard_map/gram/pallas_call | solution.py:345
  27.2 16.5 %all_to_all.15.parts_ref = f32[16,8,128]{2,1,0:T(8,128)S(1)} all-to-all(f32[16,8,128]{2,1,0:T(8,128)S(1)} %gram.1), channel_id=1, replica_groups=mesh['exp'=32,'ccd'=16] {'ccd'}, dimensions={0} | all-to-all | bytes 131072 | tf_op jit(solution)/shard_map/all_to_all | solution.py:394
  43.6 0.8 %solve.1 = f32[32,8,128]{2,1,0:T(8,128)S(1)} custom-call(f32[16,8,128]{2,1,0:T(8,128)S(1)} %all_to_all.15.parts_ref, f32[32,8,128]{2,1,0:T(8,128)S(1)} %get-tuple-element.20.flux_ref), custom_call_target="tpu_custom_call" | custom-call | tf_op jit(solution)/shard_map/solve/pallas_call | solution.py:356
  44.5 19.1 %all_to_all.16.flux_ref = f32[32,8,128]{2,1,0:T(8,128)S(1)} all-to-all(f32[32,8,128]{2,1,0:T(8,128)S(1)} %solve.1), channel_id=1, replica_groups=mesh['exp'=32,'ccd'=16] {'exp'}, dimensions={0} | all-to-all | bytes 262144 | tf_op jit(solution)/shard_map/all_to_all | solution.py:396
  63.6 3.4 %subtract.1 = (f32[32,16,50]{2,1,0:T(8,128)}, f32[16,50]{1,0:T(8,128)}) custom-call(f32[32,8,128]{2,1,0:T(8,128)S(1)} %all_to_all.16.flux_ref, f32[10,8,128]{2,1,0:T(8,128)S(1)} %local_model.1.model_ref), custom_call_target="tpu_custom_call" | custom-call | tf_op jit(solution)/shard_map/subtract/pallas_call | solution.py:362
Async XLA Ops:
  0.6 23.4 %copy-start.1 = (bf16[2,100,2160]{2,0,1:T(2,128)(2,1)S(1)}, bf16[2,100,2160]{2,0,1:T(2,128)(2,1)}, u32[]{:S(2)}) copy-start(bf16[2,100,2160]{2,0,1:T(2,128)(2,1)} %param.8) | copy-start | bytes 2592004
  2.7 23.6 %all-to-all-start = ((f32[32,8,128]{2,1,0:T(8,128)}), f32[32,8,128]{2,1,0:T(8,128)S(1)}, u32[]{:S(2)}, u32[]{:S(2)}) async-start(f32[32,8,128]{2,1,0:T(8,128)} %get-tuple-element.13), calls=%async_computation | async-start | bytes 262144 | tf_op jit(solution)/shard_map/all_to_all | solution.py:391
  15.6 8.5 %copy-start = (bf16[1,1000,4,128]{3,2,1,0:T(4,128)(2,1)S(1)}, bf16[1,1000,4,128]{3,2,1,0:T(4,128)(2,1)}, u32[]{:S(2)}) copy-start(bf16[1,1000,4,128]{3,2,1,0:T(4,128)(2,1)} %param.7) | copy-start | bytes 3072004
  15.6 8.4 %collective-permute-start = (bf16[80,128]{1,0:T(8,128)(2,1)S(1)}, bf16[80,128]{1,0:T(8,128)(2,1)S(1)}, u32[]{:S(2)}, u32[]{:S(2)}) collective-permute-start(bf16[80,128]{1,0:T(8,128)(2,1)S(1)} %get-tuple-element.14), channel_id=1, source_target_pairs={{1,2},{3,4},{5,6},{7,8},{9,10},{11,12},{13,14},{2,1},{4,3},{6,5},{... | collective-permute-start | bytes 61448 | tf_op jit(solution)/shard_map/ppermute | solution.py:387
  16.4 7.7 %collective-permute-start.1 = (bf16[80,128]{1,0:T(8,128)(2,1)S(1)}, bf16[80,128]{1,0:T(8,128)(2,1)S(1)}, u32[]{:S(2)}, u32[]{:S(2)}) collective-permute-start(bf16[80,128]{1,0:T(8,128)(2,1)S(1)} %get-tuple-element.15), channel_id=1, source_target_pairs={{0,1},{2,3},{4,5},{6,7},{8,9},{10,11},{12,13},{14,15},{1,0},{3,2},... | collective-permute-start | bytes 61448 | tf_op jit(solution)/shard_map/ppermute | solution.py:388

commit v4 on v3

--- a/solution.py
+++ b/solution.py
@@ -158,11 +158,13 @@
         both = basis_at(t, turned_s)
         for k in range(COMP):
             totals[k] = totals[k] + tap * pick(both, (lane & HALF) + k)
+    model_ref[...] = jnp.zeros((16, SUB * LANES), f32)
     for k in range(COMP):
-        model_ref[k] = totals[k]
-
-
-def extract_kernel(sky_h, slot_h, pix_ref, near_ref, far_ref, psf_ref, flux_ref, weight_ref, skyflux_ref, sky_v, slot_v, pix_s, var_s, pad_s, flux_s, vari_s, row_s, sems):
+        for j in range(SUB):
+            model_ref[k : k + 1, j * LANES : (j + 1) * LANES] = totals[k][j : j + 1, :]
+
+
+def extract_kernel(sky_h, slot_h, pix_ref, near_ref, far_ref, psf_ref, flux_ref, weight_ref, skyflux_ref, sky_v, slot_v, pix_s, var_s, pad_s, rows_s, flux_s, vari_s, row_s, sems):
     ccd_at = lax.axis_index("ccd")
     base = ccd_at * FC
     lane = lanes_of()
@@ -175,15 +177,19 @@
     pix_s[EDGE : EDGE + LOCAL, :] = pix_ref[...]
     pix_s[pl.ds(pl.multiple_of((1 - odd) * (EDGE + LOCAL), EDGE), EDGE), :] = far_ref[...]
     var_s[...] = (0.25 + jnp.square(pix_s[...].astype(f32))).astype(jnp.bfloat16)
-    pad_s[...] = jnp.zeros((LANES, LANES), f32)
+    rows_s[...] = jnp.zeros((2, 2, LANES, LANES), f32)
     for b in range(2):
         lower = b * BPIX * ROWS
         psf = psf_ref[b]
-        pad_s[0:100, :] = jnp.dot(psf, pix_s[lower : lower + DEPTH, :], preferred_element_type=f32)
-        flux_s[b] = jnp.transpose(pad_s[...])
         square = jnp.square(psf.astype(f32)).astype(jnp.bfloat16)
-        pad_s[0:100, :] = jnp.dot(square, var_s[lower : lower + DEPTH, :], preferred_element_type=f32)
-        vari_s[b] = jnp.transpose(pad_s[...])
+        for q, (weights, values) in enumerate(((psf, pix_s), (square, var_s))):
+            pad_s[b, q] = jnp.dot(weights, values[lower : lower + DEPTH, :], preferred_element_type=f32)
+            for r in range(ROWS):
+                at = (r % 2) * HALF + b * 32
+                rows_s[q, r // 2, at : at + FIBBLK, :] = pad_s[b, q, pl.ds(r, FIBBLK, stride=ROWS), :]
+    for half in range(2):
+        flux_s[half] = jnp.transpose(rows_s[0, half])
+        vari_s[half] = jnp.transpose(rows_s[1, half])
     listed.wait()
     slotted.wait()
     fibre, _, valid = sky_index(lane)
@@ -191,24 +197,21 @@
     slot = doubled(slot_v[...], row_s)
     used = (lane & (HALF - 1)) < FC
     slot = jnp.where(used, slot - base, 0)
-    second = slot >= FIBBLK
-    place = jnp.where(second, slot - FIBBLK, slot) * ROWS
-    sky_slot = pick(slot, sky)
-    sky_second = sky_slot >= FIBBLK
-    sky_place = jnp.where(sky_second, sky_slot - FIBBLK, sky_slot) * ROWS
-
-    def gathered(ref, row, spot, late):
-        upper = jnp.where(late, pick(ref[1, row : row + SUB, :], spot), pick(ref[0, row : row + SUB, :], spot))
-        row = row + SUB
-        lower = jnp.where(late, pick(ref[1, row : row + SUB, :], spot), pick(ref[0, row : row + SUB, :], spot))
+    place = jnp.where(slot >= FIBBLK, slot + (32 - FIBBLK), slot)
+    sky_place = pick(place, sky)
+
+    def gathered(ref, row, spot):
+        upper = pick(ref[row : row + SUB, :], spot)
+        lower = pick(ref[row + SUB : row + 2 * SUB, :], spot)
         return jnp.where(lane < HALF, upper, lower)
 
     for r in range(ROWS):
+        half, turn = r // 2, (r % 2) * HALF
         for m in range(GROUPS // CHUNK):
-            flux = jnp.where(used, gathered(flux_s, m * CHUNK, place + r, second), 0.0)
+            flux = jnp.where(used, gathered(flux_s.at[half], m * CHUNK, place + turn), 0.0)
             flux_ref[r * 8 + m] = flux
             skyflux_ref[r * 8 + m] = jnp.where(valid, pick(flux, sky), 0.0)
-            vari = gathered(vari_s, m * CHUNK, sky_place + r, sky_second)
+            vari = gathered(vari_s.at[half], m * CHUNK, sky_place + turn)
             weight_ref[r * 8 + m] = jnp.where(valid, 1.0 / vari, 0.0)
 
 
@@ -251,29 +254,30 @@
         out_ref[e] = jnp.where(here, coeffs, flux_ref[e])
 
 
-def subtract_kernel(flux_ref, model_ref, out_h, noise_ref, left_s, out_s, sems):
-    models = [model_ref[k] for k in range(COMP)]
-    spots = [jnp.full((SUB, LANES), FC + k, jnp.int32) for k in range(COMP)]
+def subtract_kernel(flux_ref, model_ref, out_h, noise_ref, sky_s, left_s, out_s, sems):
+    heads = flux_ref[pl.ds(0, EXPOS, stride=SUB), :]
+    coeffs = pltpu.roll(heads, LANES - FC, 1)
+    coeffs = jnp.where(lanes_of((EXPOS, LANES)) < COMP, coeffs, 0.0)[:, 0:16]
+    sky = jnp.dot(coeffs, model_ref[...], precision=highest, preferred_element_type=f32)
+    for j in range(SUB):
+        sky_s[pl.ds(j, EXPOS, stride=SUB), :] = sky[:, j * LANES : (j + 1) * LANES]
     total = jnp.zeros((SUB, LANES), f32)
     copies = []
     for e in range(EXPOS):
-        left = flux_ref[e]
-        sky = pick(left, spots[0]) * models[0]
-        for k in range(1, COMP):
-            sky = sky + pick(left, spots[k]) * models[k]
-        left = left - sky
-        left_s[e] = left
+        at = slice(e * SUB, (e + 1) * SUB)
+        left = flux_ref[at, :] - sky_s[at, :]
+        left_s[at, :] = left
         total = total + left
         out_s[e, 0:SUB, :] = left[:, 0:FC]
         out_s[e, SUB:CHUNK, :] = pltpu.roll(left, HALF, 1)[:, 0:FC]
         if e % PIECE == PIECE - 1:
-            at = pl.ds(e + 1 - PIECE, PIECE)
-            copies.append(pltpu.make_async_copy(out_s.at[at], out_h.at[at], sems.at[e // PIECE]))
+            part = pl.ds(e + 1 - PIECE, PIECE)
+            copies.append(pltpu.make_async_copy(out_s.at[part], out_h.at[part], sems.at[e // PIECE]))
             copies[-1].start()
     mean = total * (1.0 / EXPOS)
     spread = jnp.zeros((SUB, LANES), f32)
     for e in range(EXPOS):
-        spread = spread + jnp.square(left_s[e] - mean)
+        spread = spread + jnp.square(left_s[e * SUB : (e + 1) * SUB, :] - mean)
     noise = jnp.sqrt(spread * (1.0 / EXPOS) + 1e-06)
     noise_ref[0:SUB, :] = noise[:, 0:FC]
     noise_ref[SUB:CHUNK, :] = pltpu.roll(noise, HALF, 1)[:, 0:FC]
@@ -310,7 +314,7 @@
 def local_model(resolution, basis, shift):
     return pl.pallas_call(
         model_kernel,
-        out_shape=jax.ShapeDtypeStruct((COMP, SUB, LANES), f32),
+        out_shape=jax.ShapeDtypeStruct((16, SUB * LANES), f32),
         in_specs=[HBM] * 3,
         out_specs=VMEM,
         scratch_shapes=MODEL_INPUTS + MODEL_SCRATCH + [pltpu.SemaphoreType.DMA((3,))],
@@ -330,13 +334,15 @@
             pltpu.VMEM((1, FC), jnp.int32),
             pltpu.VMEM((2 * EDGE + LOCAL, LANES), jnp.bfloat16),
             pltpu.VMEM((2 * EDGE + LOCAL, LANES), jnp.bfloat16),
-            pltpu.VMEM((LANES, LANES), f32),
+            pltpu.VMEM((2, 2, FIBBLK * ROWS, LANES), f32),
+            pltpu.VMEM((2, 2, LANES, LANES), f32),
             pltpu.VMEM((2, LANES, LANES), f32),
             pltpu.VMEM((2, LANES, LANES), f32),
             pltpu.VMEM((SUB, LANES), jnp.int32),
             pltpu.SemaphoreType.DMA((2,)),
         ],
         compiler_params=PARAMS,
+        cost_estimate=pl.CostEstimate(flops=2400000000, transcendentals=0, bytes_accessed=4000000),
         name="extract",
     )(*(pltpu.with_memory_space_constraint(v, pltpu.HBM) for v in (sky, slot)), pixels, near, far, psf)
 
@@ -365,13 +371,14 @@
         in_specs=[VMEM, VMEM],
         out_specs=(HBM, VMEM),
         scratch_shapes=[
-            pltpu.VMEM((EXPOS, SUB, LANES), f32),
+            pltpu.VMEM((EXPOS * SUB, LANES), f32),
+            pltpu.VMEM((EXPOS * SUB, LANES), f32),
             pltpu.VMEM((EXPOS, CHUNK, FC), f32),
             pltpu.SemaphoreType.DMA((EXPOS // PIECE,)),
         ],
         compiler_params=PARAMS,
         name="subtract",
-    )(flux, model)
+    )(flux.reshape(EXPOS * SUB, LANES), model)
 
 
 def shards(pixels, psf_proj, resolution, basis, sky_fibres, fibre_slot, band_shift):
@@ -385,6 +392,7 @@
     swaps = [[*pair, *((j, i) for i, j in pair)] for pair in pairs]
     send, near, far = sky_model(res, basis, shift, sky, rows)
     near = lax.ppermute(near, "ccd", swaps[0])
+    near, far = lax.optimization_barrier((near, far))
     far = lax.ppermute(far, "ccd", swaps[1])
     model = local_model(res, basis, shift)
     near, far, model = lax.optimization_barrier((near, far, model))

time: 67.4 us -> 65.7 us (0.975)
  Pallas kernels: 11.1 us -> 9.35 us
    all_to_all x1, blocking collectives: 19.1 us -> 16.9 us  [shards(): flux = lax.all_to_all(flux, 'exp', split_axis=0, concat_axis=0, tiled=True)]
    all_to_all x1, blocking collectives: 16.5 us -> 18.5 us  [shards(): lax.all_to_all(parts, 'ccd', split_axis=0, concat_axis=0, tiled=True)]
    pallas_call x1, Pallas kernels: 3.38 us -> 1.72 us  [subtract(): pl.pallas_call(subtract_kernel, out_shape=(jax.ShapeDtypeStruct((EXPOS, C...]
where the time goes in v4:
time: 65.7 us; the launch traced here: 65.3 us
  blocking collectives  35.3 us (54%)
  starting transfers between devices  19.7 us (30%)
  Pallas kernels  9.35 us (14%)
  between operations  0.8 us (1%)
    all_to_all x1, blocking collectives, shards(): lax.all_to_all(parts, 'ccd', split_axis=0, concat_axis=0, tiled=True)  18.5 us
    all_to_all x1, blocking collectives, shards(): flux = lax.all_to_all(flux, 'exp', split_axis=0, concat_axis=0, tiled=True)  16.9 us
    all_to_all x1, starting transfers between devices, shards(): lax.all_to_all(send, 'exp', split_axis=0, concat_axis=0, tiled=True)  12.9 us
    ppermute x1, starting transfers between devices, shards(): far = lax.ppermute(far, 'ccd', swaps[1])  6.16 us
    pallas_call x1, Pallas kernels, extract(): pl.pallas_call(extract_kernel, out_shape=(TILES, TILES, TILES), in_specs=...  2.09 us
    pallas_call x1, Pallas kernels, sky_model(): pl.pallas_call(sky_kernel, out_shape=(TILES, EDGES, EDGES), in_specs=[HBM...  2.06 us
    pallas_call x1, Pallas kernels, local_model(): pl.pallas_call(model_kernel, out_shape=jax.ShapeDtypeStruct((16, SUB * LA...  1.77 us
    pallas_call x1, Pallas kernels, subtract(): pl.pallas_call(subtract_kernel, out_shape=(jax.ShapeDtypeStruct((EXPOS, C...  1.72 us
  transfers between devices with their start and end apart: 3, of which 0 were waited for; matrix products, arithmetic and copies ran while one was open for 0% of the time, Pallas kernels for 6%

profile of v4, /device:TPU:1, one launch (start us, length us, event | category | flops | bytes accessed | tf_op | source)
XLA Modules:
  0.0 65.3 jit_solution(4114060691030254293)
XLA Ops:
  0.6 0.0 copy-start.1
  0.6 2.1 %sky_model.1 = (f32[32,8,128]{2,1,0:T(8,128)}, bf16[80,128]{1,0:T(8,128)(2,1)S(1)}, bf16[80,128]{1,0:T(8,128)(2,1)S(1)}) custom-call(f32[11,16,50]{2,1,0:T(8,128)} %bitcast.11, f32[10,528]{1,0:T(8,128)} %basis_h.3, s32[1,50]{1,0:T(1,128)} %bitcast.13, s32[1,96]{1,0:T(1,128)} %bitcast.15, bf16[4000,128]{1,0:T(8,128)(2,1)} %bitcast.8), custom_call_target="tpu_custom_call" | custom-call | tf_op jit(solution)/shard_map/sky_model/pallas_call | solution.py:303
  2.7 0.7 %collective-permute-start = (bf16[80,128]{1,0:T(8,128)(2,1)S(1)}, bf16[80,128]{1,0:T(8,128)(2,1)S(1)}, u32[]{:S(2)}, u32[]{:S(2)}) collective-permute-start(bf16[80,128]{1,0:T(8,128)(2,1)S(1)} %get-tuple-element.16), channel_id=1, source_target_pairs={{1,2},{3,4},{5,6},{7,8},{9,10},{11,12},{13,14},{2,1},{4,3},{6,5},{... | collective-permute-start | bytes 61448 | tf_op jit(solution)/shard_map/ppermute | solution.py:394
  3.4 12.9 %all-to-all-start = ((f32[32,8,128]{2,1,0:T(8,128)}), f32[32,8,128]{2,1,0:T(8,128)S(1)}, u32[]{:S(2)}, u32[]{:S(2)}) async-start(f32[32,8,128]{2,1,0:T(8,128)} %get-tuple-element.15), calls=%async_computation | async-start | bytes 262144 | tf_op jit(solution)/shard_map/all_to_all | solution.py:399
  16.3 0.0 copy-start
  16.3 0.0 collective-permute-done.near_ref
  16.3 6.2 %collective-permute-start.1 = (bf16[80,128]{1,0:T(8,128)(2,1)S(1)}, bf16[80,128]{1,0:T(8,128)(2,1)S(1)}, u32[]{:S(2)}, u32[]{:S(2)}) collective-permute-start(bf16[80,128]{1,0:T(8,128)(2,1)S(1)} %get-tuple-element.19), channel_id=1, source_target_pairs={{0,1},{2,3},{4,5},{6,7},{8,9},{10,11},{12,13},{14,15},{1,0},{3,2},... | collective-permute-start | bytes 61448 | tf_op jit(solution)/shard_map/ppermute | solution.py:396
  22.5 1.8 %local_model.1.model_ref = f32[16,1024]{1,0:T(8,128)S(1)} custom-call(f32[11,16,50]{2,1,0:T(8,128)} %bitcast.12, f32[10,528]{1,0:T(8,128)} %basis_h.3, s32[1,50]{1,0:T(1,128)} %bitcast.14), custom_call_target="tpu_custom_call" | custom-call | tf_op jit(solution)/shard_map/local_model/pallas_call | solution.py:315
  24.3 0.0 copy-done.1
  24.3 0.1 copy.9.psf_ref
  24.4 0.0 collective-permute-done.1.far_ref
  24.4 0.0 copy-done
  24.4 2.1 %extract.1 = (f32[32,8,128]{2,1,0:T(8,128)S(1)}, f32[32,8,128]{2,1,0:T(8,128)S(1)}, f32[32,8,128]{2,1,0:T(8,128)S(1)}) custom-call(s32[1,96]{1,0:T(1,128)} %bitcast.16, s32[1,50]{1,0:T(1,128)} %bitcast.19, bf16[4000,128]{1,0:T(8,128)(2,1)S(1)} %bitcast.9, bf16[80,128]{1,0:T(8,128)(2,1)S(1)} %collective-permute-done.near_ref, ...), custom_call_target="tpu_custom_call" | custom-call | flops 2400000000 | bytes 4000000 | tf_op jit(solution)/shard_map/extract/pallas_call | solution.py:327
  26.5 0.0 all-to-all-done.model_ref
  26.5 0.9 %gram.1 = f32[16,8,128]{2,1,0:T(8,128)S(1)} custom-call(f32[32,8,128]{2,1,0:T(8,128)S(1)} %all-to-all-done.model_ref, f32[32,8,128]{2,1,0:T(8,128)S(1)} %get-tuple-element.22.weight_ref, f32[32,8,128]{2,1,0:T(8,128)S(1)} %get-tuple-element.23.flux_ref), custom_call_target="tpu_custom_call" | custom-call | tf_op jit(solution)/shard_map/gram/pallas_call | solution.py:351
  27.4 18.5 %all_to_all.15.parts_ref = f32[16,8,128]{2,1,0:T(8,128)S(1)} all-to-all(f32[16,8,128]{2,1,0:T(8,128)S(1)} %gram.1), channel_id=1, replica_groups=mesh['exp'=32,'ccd'=16] {'ccd'}, dimensions={0} | all-to-all | bytes 131072 | tf_op jit(solution)/shard_map/all_to_all | solution.py:402
  45.9 0.8 %solve.1 = f32[32,8,128]{2,1,0:T(8,128)S(1)} custom-call(f32[16,8,128]{2,1,0:T(8,128)S(1)} %all_to_all.15.parts_ref, f32[32,8,128]{2,1,0:T(8,128)S(1)} %get-tuple-element.24.flux_ref), custom_call_target="tpu_custom_call" | custom-call | tf_op jit(solution)/shard_map/solve/pallas_call | solution.py:362
  46.7 16.9 %all_to_all.16 = f32[32,8,128]{2,1,0:T(8,128)S(1)} all-to-all(f32[32,8,128]{2,1,0:T(8,128)S(1)} %solve.1), channel_id=1, replica_groups=mesh['exp'=32,'ccd'=16] {'exp'}, dimensions={0} | all-to-all | bytes 262144 | tf_op jit(solution)/shard_map/all_to_all | solution.py:404
  63.6 1.7 %subtract.1 = (f32[32,16,50]{2,1,0:T(8,128)}, f32[16,50]{1,0:T(8,128)}) custom-call(f32[256,128]{1,0:T(8,128)S(1)} %bitcast.10, f32[16,1024]{1,0:T(8,128)S(1)} %local_model.1.model_ref), custom_call_target="tpu_custom_call" | custom-call | tf_op jit(solution)/shard_map/subtract/pallas_call | solution.py:368
Async XLA Ops:
  0.6 23.6 %copy-start.1 = (bf16[2,100,2160]{2,0,1:T(2,128)(2,1)S(1)}, bf16[2,100,2160]{2,0,1:T(2,128)(2,1)}, u32[]{:S(2)}) copy-start(bf16[2,100,2160]{2,0,1:T(2,128)(2,1)} %param.8) | copy-start | bytes 2592004
  2.7 13.6 %collective-permute-start = (bf16[80,128]{1,0:T(8,128)(2,1)S(1)}, bf16[80,128]{1,0:T(8,128)(2,1)S(1)}, u32[]{:S(2)}, u32[]{:S(2)}) collective-permute-start(bf16[80,128]{1,0:T(8,128)(2,1)S(1)} %get-tuple-element.16), channel_id=1, source_target_pairs={{1,2},{3,4},{5,6},{7,8},{9,10},{11,12},{13,14},{2,1},{4,3},{6,5},{... | collective-permute-start | bytes 61448 | tf_op jit(solution)/shard_map/ppermute | solution.py:394
  3.4 23.1 %all-to-all-start = ((f32[32,8,128]{2,1,0:T(8,128)}), f32[32,8,128]{2,1,0:T(8,128)S(1)}, u32[]{:S(2)}, u32[]{:S(2)}) async-start(f32[32,8,128]{2,1,0:T(8,128)} %get-tuple-element.15), calls=%async_computation | async-start | bytes 262144 | tf_op jit(solution)/shard_map/all_to_all | solution.py:399
  16.3 8.1 %copy-start = (bf16[1,1000,4,128]{3,2,1,0:T(4,128)(2,1)S(1)}, bf16[1,1000,4,128]{3,2,1,0:T(4,128)(2,1)}, u32[]{:S(2)}) copy-start(bf16[1,1000,4,128]{3,2,1,0:T(4,128)(2,1)} %param.7) | copy-start | bytes 3072004
  16.3 8.1 %collective-permute-start.1 = (bf16[80,128]{1,0:T(8,128)(2,1)S(1)}, bf16[80,128]{1,0:T(8,128)(2,1)S(1)}, u32[]{:S(2)}, u32[]{:S(2)}) collective-permute-start(bf16[80,128]{1,0:T(8,128)(2,1)S(1)} %get-tuple-element.19), channel_id=1, source_target_pairs={{0,1},{2,3},{4,5},{6,7},{8,9},{10,11},{12,13},{14,15},{1,0},{3,2},... | collective-permute-start | bytes 61448 | tf_op jit(solution)/shard_map/ppermute | solution.py:396

commit v5 on v4

--- a/solution.py
+++ b/solution.py
@@ -25,6 +25,7 @@
 TAPS = BAND + 2 * SHIFT
 EDGE = MARG * ROWS
 DEPTH = SPAN * ROWS
+TAIL = 32
 LOCAL = 2 * BPIX * ROWS
 
 
@@ -164,26 +165,59 @@
             model_ref[k : k + 1, j * LANES : (j + 1) * LANES] = totals[k][j : j + 1, :]
 
 
-def extract_kernel(sky_h, slot_h, pix_ref, near_ref, far_ref, psf_ref, flux_ref, weight_ref, skyflux_ref, sky_v, slot_v, pix_s, var_s, pad_s, rows_s, flux_s, vari_s, row_s, sems):
+def extract_kernel(pix_ref, near_ref, psf_ref, flux_ref, vari_ref, pix_s, var_s):
+    odd = lax.axis_index("ccd") % 2
+    far = pl.ds(pl.multiple_of((1 - odd) * (EDGE + LOCAL), EDGE), EDGE)
+    pix_s[pl.ds(pl.multiple_of(odd * (EDGE + LOCAL), EDGE), EDGE), :] = near_ref[...]
+    pix_s[EDGE : EDGE + LOCAL, :] = pix_ref[...]
+    pix_s[far, :] = jnp.zeros((EDGE, LANES), jnp.bfloat16)
+    var_s[...] = variance_of(pix_s[...])
+    var_s[far, :] = jnp.zeros((EDGE, LANES), jnp.bfloat16)
+    for b in range(2):
+        lower = b * BPIX * ROWS
+        psf = psf_ref[b]
+        flux_ref[b] = jnp.dot(psf, pix_s[lower : lower + DEPTH, :], preferred_element_type=f32)
+        vari_ref[b] = jnp.dot(squared(psf), var_s[lower : lower + DEPTH, :], preferred_element_type=f32)
+
+
+def variance_of(x):
+    return (0.25 + jnp.square(x.astype(f32))).astype(jnp.bfloat16)
+
+
+def squared(x):
+    return jnp.square(x.astype(f32)).astype(jnp.bfloat16)
+
+
+def gram_kernel(sky_h, slot_h, far_ref, psf_ref, flux_in, vari_in, model_ref, flux_ref, out_ref, sky_v, slot_v, edge_s, extra_s, pad_s, rows_s, flux_s, vari_s, row_s, weighted_s, sems):
     ccd_at = lax.axis_index("ccd")
     base = ccd_at * FC
+    odd = ccd_at % 2
     lane = lanes_of()
     listed = pltpu.make_async_copy(sky_h, sky_v, sems.at[0])
     slotted = pltpu.make_async_copy(slot_h, slot_v, sems.at[1])
     listed.start()
     slotted.start()
-    odd = ccd_at % 2
-    pix_s[pl.ds(pl.multiple_of(odd * (EDGE + LOCAL), EDGE), EDGE), :] = near_ref[...]
-    pix_s[EDGE : EDGE + LOCAL, :] = pix_ref[...]
-    pix_s[pl.ds(pl.multiple_of((1 - odd) * (EDGE + LOCAL), EDGE), EDGE), :] = far_ref[...]
-    var_s[...] = (0.25 + jnp.square(pix_s[...].astype(f32))).astype(jnp.bfloat16)
     rows_s[...] = jnp.zeros((2, 2, LANES, LANES), f32)
+    edge_s[0, 0:TAIL, :] = jnp.zeros((TAIL, LANES), jnp.bfloat16)
+    edge_s[1, 0:TAIL, :] = jnp.zeros((TAIL, LANES), jnp.bfloat16)
+    edge_s[0, TAIL : TAIL + EDGE, :] = far_ref[...]
+    edge_s[1, TAIL : TAIL + EDGE, :] = variance_of(far_ref[...])
+
+    @pl.when(odd == 1)
+    def first_block():
+        psf = psf_ref[0, :, 0:EDGE]
+        extra_s[0] = jnp.dot(psf, edge_s[0, TAIL : TAIL + EDGE, :], preferred_element_type=f32)
+        extra_s[1] = jnp.dot(squared(psf), edge_s[1, TAIL : TAIL + EDGE, :], preferred_element_type=f32)
+
+    @pl.when(odd == 0)
+    def second_block():
+        psf = psf_ref[1, :, DEPTH - EDGE - TAIL : DEPTH]
+        extra_s[0] = jnp.dot(psf, edge_s[0], preferred_element_type=f32)
+        extra_s[1] = jnp.dot(squared(psf), edge_s[1], preferred_element_type=f32)
+
     for b in range(2):
-        lower = b * BPIX * ROWS
-        psf = psf_ref[b]
-        square = jnp.square(psf.astype(f32)).astype(jnp.bfloat16)
-        for q, (weights, values) in enumerate(((psf, pix_s), (square, var_s))):
-            pad_s[b, q] = jnp.dot(weights, values[lower : lower + DEPTH, :], preferred_element_type=f32)
+        for q, part in enumerate((flux_in, vari_in)):
+            pad_s[b, q] = part[b] + jnp.where(odd == 1 - b, extra_s[q], 0.0)
             for r in range(ROWS):
                 at = (r % 2) * HALF + b * 32
                 rows_s[q, r // 2, at : at + FIBBLK, :] = pad_s[b, q, pl.ds(r, FIBBLK, stride=ROWS), :]
@@ -205,31 +239,30 @@
         lower = pick(ref[row + SUB : row + 2 * SUB, :], spot)
         return jnp.where(lane < HALF, upper, lower)
 
+    target = jnp.zeros((SUB, LANES), f32)
     for r in range(ROWS):
         half, turn = r // 2, (r % 2) * HALF
         for m in range(GROUPS // CHUNK):
+            e = r * 8 + m
             flux = jnp.where(used, gathered(flux_s.at[half], m * CHUNK, place + turn), 0.0)
-            flux_ref[r * 8 + m] = flux
-            skyflux_ref[r * 8 + m] = jnp.where(valid, pick(flux, sky), 0.0)
+            flux_ref[e] = flux
             vari = gathered(vari_s.at[half], m * CHUNK, sky_place + turn)
-            weight_ref[r * 8 + m] = jnp.where(valid, 1.0 / vari, 0.0)
-
-
-def gram_kernel(model_ref, weight_ref, flux_ref, out_ref):
+            weighted = jnp.where(valid, model_ref[e] / vari, 0.0)
+            weighted_s[e * SUB : (e + 1) * SUB, :] = weighted
+            target = target + weighted * pick(flux, sky)
+    target = jnp.sum(target, axis=0, keepdims=True)
     model = model_ref[...].reshape(EXPOS * SUB, LANES)
-    weighted = model * weight_ref[...].reshape(EXPOS * SUB, LANES)
-    target = jnp.sum(weighted * flux_ref[...].reshape(EXPOS * SUB, LANES), axis=0, keepdims=True)
-    square = lax.dot_general(weighted, model, (((0,), (0,)), ((), ())), precision=highest, preferred_element_type=f32)
+    square = lax.dot_general(weighted_s[...], model, (((0,), (0,)), ((), ())), precision=highest, preferred_element_type=f32)
     shape = (LANES, LANES)
-    fibre_r, comp_r, valid_r = sky_index(lanes_of(shape, 0))
     row, col = lanes_of(shape, 0), lanes_of(shape, 1)
+    fibre_r, _, valid_r = sky_index(row)
     fibre_c, comp_c, valid_c = sky_index(col)
     same = (fibre_r == fibre_c) & ((row & HALF) == (col & HALF)) & valid_r & valid_c
     square = jnp.where(same, square, 0.0)
     select = jnp.where((row == comp_c) & valid_c, 1.0, 0.0)
-    half = jnp.dot(select[0:16], square, precision=highest, preferred_element_type=f32)
-    half = jnp.where(row[0:16] == COMP, target, half)
-    full = lax.dot_general(half, select, (((1,), (1,)), ((), ())), precision=highest, preferred_element_type=f32)
+    summed = jnp.dot(select[0:16], square, precision=highest, preferred_element_type=f32)
+    summed = jnp.where(row[0:16] == COMP, target, summed)
+    full = lax.dot_general(summed, select, (((1,), (1,)), ((), ())), precision=highest, preferred_element_type=f32)
     tile = full[0:SUB] + pltpu.roll(full[SUB : 2 * SUB], HALF, 1)
     out_ref[...] = jnp.broadcast_to(tile[None], out_ref.shape)
 
@@ -240,12 +273,15 @@
     col = lanes_of((16, LANES))
     row = lanes_of((16, LANES), 0)
     system = jnp.where((col < COMP) & (row <= COMP), system, 0.0)
-    for k in range(COMP):
-        column = pick(system, jnp.full((16, LANES), k, jnp.int32))
-        line = system[k : k + 1, :]
-        pivot = column[k : k + 1, :]
-        unit = jnp.where(col[0:1] == k, 1.0, 0.0)
-        system = system - column * ((line - unit) / pivot)
+    for k in range(0, COMP, 2):
+        left = pick(system, jnp.full((16, LANES), k, jnp.int32))
+        right = pick(system, jnp.full((16, LANES), k + 1, jnp.int32))
+        upper = system[k : k + 1, :] - jnp.where(col[0:1] == k, 1.0, 0.0)
+        lower = system[k + 1 : k + 2, :] - jnp.where(col[0:1] == k + 1, 1.0, 0.0)
+        a, b = left[k : k + 1, :], right[k : k + 1, :]
+        c, d = left[k + 1 : k + 2, :], right[k + 1 : k + 2, :]
+        scale = 1.0 / (a * d - b * c)
+        system = system - left * ((d * upper - b * lower) * scale) - right * ((a * lower - c * upper) * scale)
     coeffs = jnp.broadcast_to(system[COMP : COMP + 1, :], (SUB, LANES))
     coeffs = pltpu.roll(coeffs, FC, 1)
     lane = lanes_of()
@@ -254,7 +290,7 @@
         out_ref[e] = jnp.where(here, coeffs, flux_ref[e])
 
 
-def subtract_kernel(flux_ref, model_ref, out_h, noise_ref, sky_s, left_s, out_s, sems):
+def subtract_kernel(flux_ref, model_ref, out_h, noise_h, sky_s, left_s, out_s, noise_s, sems):
     heads = flux_ref[pl.ds(0, EXPOS, stride=SUB), :]
     coeffs = pltpu.roll(heads, LANES - FC, 1)
     coeffs = jnp.where(lanes_of((EXPOS, LANES)) < COMP, coeffs, 0.0)[:, 0:16]
@@ -279,8 +315,10 @@
     for e in range(EXPOS):
         spread = spread + jnp.square(left_s[e * SUB : (e + 1) * SUB, :] - mean)
     noise = jnp.sqrt(spread * (1.0 / EXPOS) + 1e-06)
-    noise_ref[0:SUB, :] = noise[:, 0:FC]
-    noise_ref[SUB:CHUNK, :] = pltpu.roll(noise, HALF, 1)[:, 0:FC]
+    noise_s[0:SUB, :] = noise[:, 0:FC]
+    noise_s[SUB:CHUNK, :] = pltpu.roll(noise, HALF, 1)[:, 0:FC]
+    copies.append(pltpu.make_async_copy(noise_s, noise_h, sems.at[EXPOS // PIECE]))
+    copies[-1].start()
     for copy in copies:
         copy.wait()
 
@@ -323,39 +361,44 @@
     )(*(pltpu.with_memory_space_constraint(v, pltpu.HBM) for v in (resolution, basis, shift)))
 
 
-def extract(sky, slot, pixels, near, far, psf):
+def extract(pixels, near, psf):
+    part = jax.ShapeDtypeStruct((2, FIBBLK * ROWS, LANES), f32)
     return pl.pallas_call(
         extract_kernel,
-        out_shape=(TILES, TILES, TILES),
-        in_specs=[HBM, HBM, VMEM, VMEM, VMEM, VMEM],
-        out_specs=(VMEM, VMEM, VMEM),
+        out_shape=(part, part),
+        in_specs=[VMEM] * 3,
+        out_specs=(VMEM, VMEM),
+        scratch_shapes=[
+            pltpu.VMEM((2 * EDGE + LOCAL, LANES), jnp.bfloat16),
+            pltpu.VMEM((2 * EDGE + LOCAL, LANES), jnp.bfloat16),
+        ],
+        compiler_params=PARAMS,
+        name="extract",
+    )(pixels, near, psf)
+
+
+def gram_parts(sky, slot, far, psf, flux, vari, model, copies):
+    return pl.pallas_call(
+        gram_kernel,
+        out_shape=(TILES, jax.ShapeDtypeStruct((copies, SUB, LANES), f32)),
+        in_specs=[HBM, HBM] + [VMEM] * 5,
+        out_specs=(VMEM, VMEM),
         scratch_shapes=[
             pltpu.VMEM((1, 96), jnp.int32),
             pltpu.VMEM((1, FC), jnp.int32),
-            pltpu.VMEM((2 * EDGE + LOCAL, LANES), jnp.bfloat16),
-            pltpu.VMEM((2 * EDGE + LOCAL, LANES), jnp.bfloat16),
+            pltpu.VMEM((2, TAIL + EDGE, LANES), jnp.bfloat16),
+            pltpu.VMEM((2, FIBBLK * ROWS, LANES), f32),
             pltpu.VMEM((2, 2, FIBBLK * ROWS, LANES), f32),
             pltpu.VMEM((2, 2, LANES, LANES), f32),
             pltpu.VMEM((2, LANES, LANES), f32),
             pltpu.VMEM((2, LANES, LANES), f32),
             pltpu.VMEM((SUB, LANES), jnp.int32),
+            pltpu.VMEM((EXPOS * SUB, LANES), f32),
             pltpu.SemaphoreType.DMA((2,)),
         ],
         compiler_params=PARAMS,
-        cost_estimate=pl.CostEstimate(flops=2400000000, transcendentals=0, bytes_accessed=4000000),
-        name="extract",
-    )(*(pltpu.with_memory_space_constraint(v, pltpu.HBM) for v in (sky, slot)), pixels, near, far, psf)
-
-
-def gram_parts(model, weight, flux, copies):
-    return pl.pallas_call(
-        gram_kernel,
-        out_shape=jax.ShapeDtypeStruct((copies, SUB, LANES), f32),
-        in_specs=[VMEM, VMEM, VMEM],
-        out_specs=VMEM,
-        compiler_params=PARAMS,
         name="gram",
-    )(model, weight, flux)
+    )(*(pltpu.with_memory_space_constraint(v, pltpu.HBM) for v in (sky, slot)), far, psf, flux, vari, model)
 
 
 def solve(parts, flux):
@@ -369,12 +412,13 @@
         subtract_kernel,
         out_shape=(jax.ShapeDtypeStruct((EXPOS, CHUNK, FC), f32), jax.ShapeDtypeStruct((CHUNK, FC), f32)),
         in_specs=[VMEM, VMEM],
-        out_specs=(HBM, VMEM),
+        out_specs=(HBM, HBM),
         scratch_shapes=[
             pltpu.VMEM((EXPOS * SUB, LANES), f32),
             pltpu.VMEM((EXPOS * SUB, LANES), f32),
             pltpu.VMEM((EXPOS, CHUNK, FC), f32),
-            pltpu.SemaphoreType.DMA((EXPOS // PIECE,)),
+            pltpu.VMEM((CHUNK, FC), f32),
+            pltpu.SemaphoreType.DMA((EXPOS // PIECE + 1,)),
         ],
         compiler_params=PARAMS,
         name="subtract",
@@ -392,13 +436,12 @@
     swaps = [[*pair, *((j, i) for i, j in pair)] for pair in pairs]
     send, near, far = sky_model(res, basis, shift, sky, rows)
     near = lax.ppermute(near, "ccd", swaps[0])
-    near, far = lax.optimization_barrier((near, far))
     far = lax.ppermute(far, "ccd", swaps[1])
     model = local_model(res, basis, shift)
-    near, far, model = lax.optimization_barrier((near, far, model))
+    part, vari = extract(rows, near, psf_proj)
+    far, model, part, vari = lax.optimization_barrier((far, model, part, vari))
     sky_tiles = lax.all_to_all(send, "exp", split_axis=0, concat_axis=0, tiled=True)
-    flux, weight, sky_flux = extract(sky, slot, rows, near, far, psf_proj)
-    parts = gram_parts(sky_tiles, weight, sky_flux, size)
+    flux, parts = gram_parts(sky, slot, far, psf_proj, part, vari, sky_tiles, size)
     parts = lax.all_to_all(parts, "ccd", split_axis=0, concat_axis=0, tiled=True)
     flux = solve(parts, flux)
     flux = lax.all_to_all(flux, "exp", split_axis=0, concat_axis=0, tiled=True)

time: 65.7 us -> 63.6 us (0.968)
  Pallas kernels: 9.35 us -> 8.22 us
    all_to_all x1, blocking collectives: 18.5 us -> 17.4 us  [shards(): lax.all_to_all(parts, 'ccd', split_axis=0, concat_axis=0, tiled=True)]
  transfers between devices with their start and end apart: 3 -> 3, of which waited for: 0 -> 0; matrix products, arithmetic and copies ran while one was open for 0% -> 0% of each run, Pallas kernels for 6% -> 4%
where the time goes in v5:
time: 63.6 us; the launch traced here: 63.2 us
  blocking collectives  34.7 us (55%)
  starting transfers between devices  19.5 us (31%)
  Pallas kernels  8.22 us (13%)
  between operations  0.78 us (1%)
    all_to_all x1, blocking collectives, shards(): lax.all_to_all(parts, 'ccd', split_axis=0, concat_axis=0, tiled=True)  17.4 us
    all_to_all x1, blocking collectives, shards(): flux = lax.all_to_all(flux, 'exp', split_axis=0, concat_axis=0, tiled=True)  17.2 us
    all_to_all x1, starting transfers between devices, shards(): lax.all_to_all(send, 'exp', split_axis=0, concat_axis=0, tiled=True)  12.9 us
    ppermute x1, starting transfers between devices, shards(): far = lax.ppermute(far, 'ccd', swaps[1])  5.75 us
    pallas_call x1, Pallas kernels, sky_model(): pl.pallas_call(sky_kernel, out_shape=(TILES, EDGES, EDGES), in_specs=[HBM...  2.06 us
    pallas_call x1, Pallas kernels, gram_parts(): pl.pallas_call(gram_kernel, out_shape=(TILES, jax.ShapeDtypeStruct((copie...  1.87 us
    pallas_call x1, Pallas kernels, local_model(): pl.pallas_call(model_kernel, out_shape=jax.ShapeDtypeStruct((16, SUB * LA...  1.77 us
  transfers between devices with their start and end apart: 3, of which 0 were waited for; matrix products, arithmetic and copies ran while one was open for 0% of the time, Pallas kernels for 4%

profile of v5, /device:TPU:1, one launch (start us, length us, event | category | flops | bytes accessed | tf_op | source)
XLA Modules:
  0.0 63.2 jit_solution(7626224159888334474)
XLA Ops:
  0.6 0.0 copy-start.1
  0.6 2.1 %sky_model.1 = (f32[32,8,128]{2,1,0:T(8,128)}, bf16[80,128]{1,0:T(8,128)(2,1)S(1)}, bf16[80,128]{1,0:T(8,128)(2,1)S(1)}) custom-call(f32[11,16,50]{2,1,0:T(8,128)} %bitcast.11, f32[10,528]{1,0:T(8,128)} %basis_h.3, s32[1,50]{1,0:T(1,128)} %bitcast.13, s32[1,96]{1,0:T(1,128)} %bitcast.15, bf16[4000,128]{1,0:T(8,128)(2,1)} %bitcast.8), custom_call_target="tpu_custom_call" | custom-call | tf_op jit(solution)/shard_map/sky_model/pallas_call | solution.py:341
  2.7 12.9 %all-to-all-start = ((f32[32,8,128]{2,1,0:T(8,128)}), f32[32,8,128]{2,1,0:T(8,128)S(1)}, u32[]{:S(2)}, u32[]{:S(2)}) async-start(f32[32,8,128]{2,1,0:T(8,128)} %get-tuple-element.22), calls=%async_computation | async-start | bytes 262144 | tf_op jit(solution)/shard_map/all_to_all | solution.py:443
  15.6 0.0 copy-start
  15.6 0.8 %collective-permute-start.1 = (bf16[80,128]{1,0:T(8,128)(2,1)S(1)}, bf16[80,128]{1,0:T(8,128)(2,1)S(1)}, u32[]{:S(2)}, u32[]{:S(2)}) collective-permute-start(bf16[80,128]{1,0:T(8,128)(2,1)S(1)} %get-tuple-element.16), channel_id=1, source_target_pairs={{1,2},{3,4},{5,6},{7,8},{9,10},{11,12},{13,14},{2,1},{4,3},{6,5},{... | collective-permute-start | bytes 61448 | tf_op jit(solution)/shard_map/ppermute | solution.py:438
  16.4 5.7 %collective-permute-start = (bf16[80,128]{1,0:T(8,128)(2,1)S(1)}, bf16[80,128]{1,0:T(8,128)(2,1)S(1)}, u32[]{:S(2)}, u32[]{:S(2)}) collective-permute-start(bf16[80,128]{1,0:T(8,128)(2,1)S(1)} %get-tuple-element.15), channel_id=1, source_target_pairs={{0,1},{2,3},{4,5},{6,7},{8,9},{10,11},{12,13},{14,15},{1,0},{3,2},... | collective-permute-start | bytes 61448 | tf_op jit(solution)/shard_map/ppermute | solution.py:439
  22.2 1.8 %local_model.1.model_ref = f32[16,1024]{1,0:T(8,128)S(1)} custom-call(f32[11,16,50]{2,1,0:T(8,128)} %bitcast.12, f32[10,528]{1,0:T(8,128)} %basis_h.3, s32[1,50]{1,0:T(1,128)} %bitcast.14), custom_call_target="tpu_custom_call" | custom-call | tf_op jit(solution)/shard_map/local_model/pallas_call | solution.py:353
  24.0 0.0 copy-done.1
  24.0 0.1 copy.9.psf_ref
  24.1 0.0 collective-permute-done.1.near_ref
  24.1 0.0 copy-done
  24.1 0.9 %extract.1 = (f32[2,100,128]{2,1,0:T(8,128)S(1)}, f32[2,100,128]{2,1,0:T(8,128)S(1)}) custom-call(bf16[4000,128]{1,0:T(8,128)(2,1)S(1)} %bitcast.9, bf16[80,128]{1,0:T(8,128)(2,1)S(1)} %collective-permute-done.1.near_ref, bf16[2,100,2160]{2,1,0:T(8,128)(2,1)S(1)} %copy.9.psf_ref), custom_call_target="tpu_custom_call" | custom-call | tf_op jit(solution)/shard_map/extract/pallas_call | solution.py:366
  25.0 0.0 collective-permute-done.far_ref
  25.0 0.0 all-to-all-done.model_ref
  25.0 1.9 %gram.1 = (f32[32,8,128]{2,1,0:T(8,128)S(1)}, f32[16,8,128]{2,1,0:T(8,128)S(1)}) custom-call(s32[1,96]{1,0:T(1,128)} %bitcast.16, s32[1,50]{1,0:T(1,128)} %bitcast.17, bf16[80,128]{1,0:T(8,128)(2,1)S(1)} %collective-permute-done.far_ref, bf16[2,100,2160]{2,1,0:T(8,128)(2,1)S(1)} %copy.9.psf_ref, f32[2,100,128]{2,1,0:T(8,128)S(1)} %get-tuple-element.20.flux_in, ...), custom_call_target="tpu_custom_call" | custom-call | tf_op jit(solution)/shard_map/gram/pallas_call | solution.py:381
  26.9 17.4 %all_to_all.15.parts_ref = f32[16,8,128]{2,1,0:T(8,128)S(1)} all-to-all(f32[16,8,128]{2,1,0:T(8,128)S(1)} %get-tuple-element.23), channel_id=1, replica_groups=mesh['exp'=32,'ccd'=16] {'ccd'}, dimensions={0} | all-to-all | bytes 131072 | tf_op jit(solution)/shard_map/all_to_all | solution.py:445
  44.3 0.5 solve.1
  44.9 17.2 %all_to_all.16 = f32[32,8,128]{2,1,0:T(8,128)S(1)} all-to-all(f32[32,8,128]{2,1,0:T(8,128)S(1)} %solve.1), channel_id=1, replica_groups=mesh['exp'=32,'ccd'=16] {'exp'}, dimensions={0} | all-to-all | bytes 262144 | tf_op jit(solution)/shard_map/all_to_all | solution.py:447
  62.1 1.1 %subtract.1 = (f32[32,16,50]{2,1,0:T(8,128)}, f32[16,50]{1,0:T(8,128)}) custom-call(f32[256,128]{1,0:T(8,128)S(1)} %bitcast.10, f32[16,1024]{1,0:T(8,128)S(1)} %local_model.1.model_ref), custom_call_target="tpu_custom_call" | custom-call | tf_op jit(solution)/shard_map/subtract/pallas_call | solution.py:411
Async XLA Ops:
  0.6 23.4 %copy-start.1 = (bf16[2,100,2160]{2,0,1:T(2,128)(2,1)S(1)}, bf16[2,100,2160]{2,0,1:T(2,128)(2,1)}, u32[]{:S(2)}) copy-start(bf16[2,100,2160]{2,0,1:T(2,128)(2,1)} %param.8) | copy-start | bytes 2592004
  2.7 22.3 %all-to-all-start = ((f32[32,8,128]{2,1,0:T(8,128)}), f32[32,8,128]{2,1,0:T(8,128)S(1)}, u32[]{:S(2)}, u32[]{:S(2)}) async-start(f32[32,8,128]{2,1,0:T(8,128)} %get-tuple-element.22), calls=%async_computation | async-start | bytes 262144 | tf_op jit(solution)/shard_map/all_to_all | solution.py:443
  15.6 8.5 %copy-start = (bf16[1,1000,4,128]{3,2,1,0:T(4,128)(2,1)S(1)}, bf16[1,1000,4,128]{3,2,1,0:T(4,128)(2,1)}, u32[]{:S(2)}) copy-start(bf16[1,1000,4,128]{3,2,1,0:T(4,128)(2,1)} %param.7) | copy-start | bytes 3072004
  15.6 8.4 %collective-permute-start.1 = (bf16[80,128]{1,0:T(8,128)(2,1)S(1)}, bf16[80,128]{1,0:T(8,128)(2,1)S(1)}, u32[]{:S(2)}, u32[]{:S(2)}) collective-permute-start(bf16[80,128]{1,0:T(8,128)(2,1)S(1)} %get-tuple-element.16), channel_id=1, source_target_pairs={{1,2},{3,4},{5,6},{7,8},{9,10},{11,12},{13,14},{2,1},{4,3},{6,5},{... | collective-permute-start | bytes 61448 | tf_op jit(solution)/shard_map/ppermute | solution.py:438
  16.4 8.6 %collective-permute-start = (bf16[80,128]{1,0:T(8,128)(2,1)S(1)}, bf16[80,128]{1,0:T(8,128)(2,1)S(1)}, u32[]{:S(2)}, u32[]{:S(2)}) collective-permute-start(bf16[80,128]{1,0:T(8,128)(2,1)S(1)} %get-tuple-element.15), channel_id=1, source_target_pairs={{0,1},{2,3},{4,5},{6,7},{8,9},{10,11},{12,13},{14,15},{1,0},{3,2},... | collective-permute-start | bytes 61448 | tf_op jit(solution)/shard_map/ppermute | solution.py:439

commit v6 on v5

--- a/solution.py
+++ b/solution.py
@@ -100,69 +100,79 @@
     return jnp.where(lanes_of() < HALF, upper, pltpu.roll(lower, HALF, 1))
 
 
-def model_copies(res_h, basis_h, shift_h, res_v, basis_v, shift_v, sems):
-    copies = [
-        pltpu.make_async_copy(source, target, sems.at[i])
-        for i, (source, target) in enumerate(((res_h, res_v), (basis_h, basis_v), (shift_h, shift_v)))
-    ]
-    for copy in copies:
-        copy.start()
-    return copies
-
-
-def sky_kernel(res_h, basis_h, shift_h, sky_h, pix_h, send_ref, near_ref, far_ref, res_v, basis_v, shift_v, sky_v, res_s, basis_s, row_s, turned_s, sems):
+def sky_kernel(res_h, basis_h, shift_h, sky_h, slot_h, pix_h, send_ref, near_ref, far_ref, bands_ref, turned_ref, table_ref, res_v, basis_v, shift_v, sky_v, slot_v, basis_s, row_s, sems):
     exp_at = lax.axis_index("exp")
     ccd_at = lax.axis_index("ccd")
     odd = ccd_at % 2
     at_near = pl.multiple_of(odd * (LOCAL - EDGE), EDGE)
     at_far = pl.multiple_of((1 - odd) * (LOCAL - EDGE), EDGE)
-    edges = [
-        pltpu.make_async_copy(pix_h.at[pl.ds(at_near, EDGE), :], near_ref, sems.at[4]),
-        pltpu.make_async_copy(pix_h.at[pl.ds(at_far, EDGE), :], far_ref, sems.at[5]),
+    copies = [
+        pltpu.make_async_copy(source, target, sems.at[i])
+        for i, (source, target) in enumerate(
+            (
+                (sky_h, sky_v),
+                (shift_h, shift_v),
+                (res_h, res_v),
+                (basis_h, basis_v),
+                (slot_h, slot_v),
+                (pix_h.at[pl.ds(at_near, EDGE), :], near_ref),
+                (pix_h.at[pl.ds(at_far, EDGE), :], far_ref),
+            )
+        )
     ]
-    for edge in edges:
-        edge.start()
-    copies = model_copies(res_h, basis_h, shift_h, res_v, basis_v, shift_v, sems)
-    listed = pltpu.make_async_copy(sky_h, sky_v, sems.at[3])
-    listed.start()
-    listed.wait()
     for copy in copies:
+        copy.start()
+    for copy in copies[:4]:
         copy.wait()
     lane = lanes_of()
     fibre, comp, valid = sky_index(lane)
     sky = sky_lanes(sky_v[...], row_s, ccd_at, fibre)
-    shift = pick(doubled(shift_v[...], row_s), sky) + SHIFT
+    shift = doubled(shift_v[...], row_s) + SHIFT
+    table_ref[0] = sky
+    table_ref[1] = shift
+    shift = pick(shift, sky)
     masks = [shift == s for s in range(2 * SHIFT + 1)]
-    bands = [pick(band, sky) for band in banded(res_v, res_s)]
-    turned_basis(basis_v, basis_s, turned_s, exp_at)
+    bands = [pick(band, sky) for band in banded(res_v, bands_ref)]
+    turned_basis(basis_v, basis_s, turned_ref, exp_at)
     total = jnp.zeros((SUB, LANES), f32)
     for t in range(TAPS):
-        total = total + tap_of(t, bands, masks) * pick(basis_at(t, turned_s), (lane & HALF) + comp)
+        total = total + tap_of(t, bands, masks) * pick(basis_at(t, turned_ref), (lane & HALF) + comp)
     total = jnp.where(valid, total, 0.0)
     send_ref[...] = jnp.broadcast_to(total[None], (EXPOS, SUB, LANES))
-    for edge in edges:
-        edge.wait()
-
-
-def model_kernel(res_h, basis_h, shift_h, model_ref, res_v, basis_v, shift_v, res_s, basis_s, row_s, turned_s, sems):
-    exp_at = lax.axis_index("exp")
-    for copy in model_copies(res_h, basis_h, shift_h, res_v, basis_v, shift_v, sems):
+    for copy in copies[4:]:
         copy.wait()
+    table_ref[2] = doubled(slot_v[...], row_s)
+
+
+def model_kernel(bands_ref, turned_ref, table_ref, model_ref, picks_ref, same_ref, select_ref):
+    ccd_at = lax.axis_index("ccd")
     lane = lanes_of()
-    shift = doubled(shift_v[...], row_s) + SHIFT
+    sky, shift = table_ref[0], table_ref[1]
     masks = [shift == s for s in range(2 * SHIFT + 1)]
-    bands = banded(res_v, res_s)
-    turned_basis(basis_v, basis_s, turned_s, exp_at)
+    bands = [bands_ref[d] for d in range(BAND)]
     totals = [jnp.zeros((SUB, LANES), f32) for _ in range(COMP)]
     for t in range(TAPS):
         tap = tap_of(t, bands, masks)
-        both = basis_at(t, turned_s)
+        both = basis_at(t, turned_ref)
         for k in range(COMP):
             totals[k] = totals[k] + tap * pick(both, (lane & HALF) + k)
     model_ref[...] = jnp.zeros((16, SUB * LANES), f32)
     for k in range(COMP):
         for j in range(SUB):
             model_ref[k : k + 1, j * LANES : (j + 1) * LANES] = totals[k][j : j + 1, :]
+    slot = table_ref[2]
+    slot = jnp.where((lane & (HALF - 1)) < FC, slot - ccd_at * FC, 0)
+    place = jnp.where(slot >= FIBBLK, slot + (32 - FIBBLK), slot)
+    picks_ref[0] = sky
+    picks_ref[1] = place
+    picks_ref[2] = pick(place, sky)
+    shape = (LANES, LANES)
+    row, col = lanes_of(shape, 0), lanes_of(shape, 1)
+    fibre_r, _, valid_r = sky_index(row)
+    fibre_c, comp_c, valid_c = sky_index(col)
+    same = (fibre_r == fibre_c) & ((row & HALF) == (col & HALF)) & valid_r & valid_c
+    same_ref[...] = jnp.where(same, 1.0, 0.0)
+    select_ref[...] = jnp.where((row == comp_c) & valid_c, 1.0, 0.0)
 
 
 def extract_kernel(pix_ref, near_ref, psf_ref, flux_ref, vari_ref, pix_s, var_s):
@@ -188,15 +198,9 @@
     return jnp.square(x.astype(f32)).astype(jnp.bfloat16)
 
 
-def gram_kernel(sky_h, slot_h, far_ref, psf_ref, flux_in, vari_in, model_ref, flux_ref, out_ref, sky_v, slot_v, edge_s, extra_s, pad_s, rows_s, flux_s, vari_s, row_s, weighted_s, sems):
-    ccd_at = lax.axis_index("ccd")
-    base = ccd_at * FC
-    odd = ccd_at % 2
+def gram_kernel(picks_ref, same_ref, select_ref, far_ref, psf_ref, flux_in, vari_in, model_ref, flux_ref, out_ref, edge_s, extra_s, pad_s, rows_s, flux_s, vari_s, weighted_s):
+    odd = lax.axis_index("ccd") % 2
     lane = lanes_of()
-    listed = pltpu.make_async_copy(sky_h, sky_v, sems.at[0])
-    slotted = pltpu.make_async_copy(slot_h, slot_v, sems.at[1])
-    listed.start()
-    slotted.start()
     rows_s[...] = jnp.zeros((2, 2, LANES, LANES), f32)
     edge_s[0, 0:TAIL, :] = jnp.zeros((TAIL, LANES), jnp.bfloat16)
     edge_s[1, 0:TAIL, :] = jnp.zeros((TAIL, LANES), jnp.bfloat16)
@@ -224,15 +228,9 @@
     for half in range(2):
         flux_s[half] = jnp.transpose(rows_s[0, half])
         vari_s[half] = jnp.transpose(rows_s[1, half])
-    listed.wait()
-    slotted.wait()
-    fibre, _, valid = sky_index(lane)
-    sky = sky_lanes(sky_v[...], row_s, ccd_at, fibre)
-    slot = doubled(slot_v[...], row_s)
+    _, _, valid = sky_index(lane)
     used = (lane & (HALF - 1)) < FC
-    slot = jnp.where(used, slot - base, 0)
-    place = jnp.where(slot >= FIBBLK, slot + (32 - FIBBLK), slot)
-    sky_place = pick(place, sky)
+    sky, place, sky_place = picks_ref[0], picks_ref[1], picks_ref[2]
 
     def gathered(ref, row, spot):
         upper = pick(ref[row : row + SUB, :], spot)
@@ -253,15 +251,10 @@
     target = jnp.sum(target, axis=0, keepdims=True)
     model = model_ref[...].reshape(EXPOS * SUB, LANES)
     square = lax.dot_general(weighted_s[...], model, (((0,), (0,)), ((), ())), precision=highest, preferred_element_type=f32)
-    shape = (LANES, LANES)
-    row, col = lanes_of(shape, 0), lanes_of(shape, 1)
-    fibre_r, _, valid_r = sky_index(row)
-    fibre_c, comp_c, valid_c = sky_index(col)
-    same = (fibre_r == fibre_c) & ((row & HALF) == (col & HALF)) & valid_r & valid_c
-    square = jnp.where(same, square, 0.0)
-    select = jnp.where((row == comp_c) & valid_c, 1.0, 0.0)
+    square = square * same_ref[...]
+    select = select_ref[...]
     summed = jnp.dot(select[0:16], square, precision=highest, preferred_element_type=f32)
-    summed = jnp.where(row[0:16] == COMP, target, summed)
+    summed = jnp.where(lanes_of((16, LANES), 0) == COMP, target, summed)
     full = lax.dot_general(summed, select, (((1,), (1,)), ((), ())), precision=highest, preferred_element_type=f32)
     tile = full[0:SUB] + pltpu.roll(full[SUB : 2 * SUB], HALF, 1)
     out_ref[...] = jnp.broadcast_to(tile[None], out_ref.shape)
@@ -328,37 +321,52 @@
 TILES = jax.ShapeDtypeStruct((EXPOS, SUB, LANES), f32)
 EDGES = jax.ShapeDtypeStruct((EDGE, GROUPS), jnp.bfloat16)
 PARAMS = pltpu.CompilerParams(vmem_limit_bytes=40 * 1024 * 1024)
-MODEL_INPUTS = [pltpu.VMEM((BAND, CHUNK, FC), f32), pltpu.VMEM((COMP, 528), f32), pltpu.VMEM((1, FC), jnp.int32)]
-MODEL_SCRATCH = [
-    pltpu.VMEM((BAND, SUB, LANES), f32),
-    pltpu.VMEM((16, 640), f32),
-    pltpu.VMEM((SUB, LANES), jnp.int32),
-    pltpu.VMEM((32, LANES), f32),
-]
-
-
-def sky_model(resolution, basis, shift, sky, pixels):
+BANDS = jax.ShapeDtypeStruct((BAND, SUB, LANES), f32)
+SQUARE = jax.ShapeDtypeStruct((LANES, LANES), f32)
+
+
+def sky_model(*arrays):
     return pl.pallas_call(
         sky_kernel,
-        out_shape=(TILES, EDGES, EDGES),
-        in_specs=[HBM] * 5,
-        out_specs=(VMEM, VMEM, VMEM),
-        scratch_shapes=MODEL_INPUTS + [pltpu.VMEM((1, 96), jnp.int32)] + MODEL_SCRATCH + [pltpu.SemaphoreType.DMA((6,))],
+        out_shape=(
+            TILES,
+            EDGES,
+            EDGES,
+            BANDS,
+            jax.ShapeDtypeStruct((32, LANES), f32),
+            jax.ShapeDtypeStruct((3, SUB, LANES), jnp.int32),
+        ),
+        in_specs=[HBM] * 6,
+        out_specs=(VMEM,) * 6,
+        scratch_shapes=[
+            pltpu.VMEM((BAND, CHUNK, FC), f32),
+            pltpu.VMEM((COMP, 528), f32),
+            pltpu.VMEM((1, FC), jnp.int32),
+            pltpu.VMEM((1, 96), jnp.int32),
+            pltpu.VMEM((1, FC), jnp.int32),
+            pltpu.VMEM((16, 640), f32),
+            pltpu.VMEM((SUB, LANES), jnp.int32),
+            pltpu.SemaphoreType.DMA((7,)),
+        ],
         compiler_params=PARAMS,
         name="sky_model",
-    )(*(pltpu.with_memory_space_constraint(v, pltpu.HBM) for v in (resolution, basis, shift, sky, pixels)))
-
-
-def local_model(resolution, basis, shift):
+    )(*(pltpu.with_memory_space_constraint(v, pltpu.HBM) for v in arrays))
+
+
+def local_model(bands, turned, table):
     return pl.pallas_call(
         model_kernel,
-        out_shape=jax.ShapeDtypeStruct((16, SUB * LANES), f32),
-        in_specs=[HBM] * 3,
-        out_specs=VMEM,
-        scratch_shapes=MODEL_INPUTS + MODEL_SCRATCH + [pltpu.SemaphoreType.DMA((3,))],
+        out_shape=(
+            jax.ShapeDtypeStruct((16, SUB * LANES), f32),
+            jax.ShapeDtypeStruct((3, SUB, LANES), jnp.int32),
+            SQUARE,
+            SQUARE,
+        ),
+        in_specs=[VMEM] * 3,
+        out_specs=(VMEM,) * 4,
         compiler_params=PARAMS,
         name="local_model",
-    )(*(pltpu.with_memory_space_constraint(v, pltpu.HBM) for v in (resolution, basis, shift)))
+    )(bands, turned, table)
 
 
 def extract(pixels, near, psf):
@@ -377,28 +385,24 @@
     )(pixels, near, psf)
 
 
-def gram_parts(sky, slot, far, psf, flux, vari, model, copies):
+def gram_parts(tables, far, psf, flux, vari, model, copies):
     return pl.pallas_call(
         gram_kernel,
         out_shape=(TILES, jax.ShapeDtypeStruct((copies, SUB, LANES), f32)),
-        in_specs=[HBM, HBM] + [VMEM] * 5,
+        in_specs=[VMEM] * 8,
         out_specs=(VMEM, VMEM),
         scratch_shapes=[
-            pltpu.VMEM((1, 96), jnp.int32),
-            pltpu.VMEM((1, FC), jnp.int32),
             pltpu.VMEM((2, TAIL + EDGE, LANES), jnp.bfloat16),
             pltpu.VMEM((2, FIBBLK * ROWS, LANES), f32),
             pltpu.VMEM((2, 2, FIBBLK * ROWS, LANES), f32),
             pltpu.VMEM((2, 2, LANES, LANES), f32),
             pltpu.VMEM((2, LANES, LANES), f32),
             pltpu.VMEM((2, LANES, LANES), f32),
-            pltpu.VMEM((SUB, LANES), jnp.int32),
             pltpu.VMEM((EXPOS * SUB, LANES), f32),
-            pltpu.SemaphoreType.DMA((2,)),
         ],
         compiler_params=PARAMS,
         name="gram",
-    )(*(pltpu.with_memory_space_constraint(v, pltpu.HBM) for v in (sky, slot)), far, psf, flux, vari, model)
+    )(*tables, far, psf, flux, vari, model)
 
 
 def solve(parts, flux):
@@ -434,14 +438,14 @@
     shift = band_shift.reshape(1, FC)
     pairs = [[(i, i + 1) for i in range(start, size - 1, 2)] for start in (1, 0)]
     swaps = [[*pair, *((j, i) for i, j in pair)] for pair in pairs]
-    send, near, far = sky_model(res, basis, shift, sky, rows)
+    send, near, far, *prepared = sky_model(res, basis, shift, sky, slot, rows)
     near = lax.ppermute(near, "ccd", swaps[0])
     far = lax.ppermute(far, "ccd", swaps[1])
-    model = local_model(res, basis, shift)
+    model, *tables = local_model(*prepared)
     part, vari = extract(rows, near, psf_proj)
-    far, model, part, vari = lax.optimization_barrier((far, model, part, vari))
+    far, model, tables, part, vari = lax.optimization_barrier((far, model, tables, part, vari))
     sky_tiles = lax.all_to_all(send, "exp", split_axis=0, concat_axis=0, tiled=True)
-    flux, parts = gram_parts(sky, slot, far, psf_proj, part, vari, sky_tiles, size)
+    flux, parts = gram_parts(tables, far, psf_proj, part, vari, sky_tiles, size)
     parts = lax.all_to_all(parts, "ccd", split_axis=0, concat_axis=0, tiled=True)
     flux = solve(parts, flux)
     flux = lax.all_to_all(flux, "exp", split_axis=0, concat_axis=0, tiled=True)

time: 63.6 us -> 63 us (level)
  Pallas kernels: 8.22 us -> 6.62 us
  waiting for transfers between devices: 0.01 us -> 0.87 us
    pallas_call x2, Pallas kernels: 3.84 us -> 2.79 us  [the longest x1 2.06 us: sky_model(): pl.pallas_call(sky_kernel, out_shape=(TILES, EDGES, EDGES, BANDS, jax.Sha...]
    all_to_all x1, waiting for transfers between devices: 0.01 us -> 0.86 us  [shards(): lax.all_to_all(send, 'exp', split_axis=0, concat_axis=0, tiled=True)]
  transfers between devices with their start and end apart: 3 -> 3, of which waited for: 0 -> 1; matrix products, arithmetic and copies ran while one was open for 0% -> 0% of each run, Pallas kernels for 4% -> 3%
where the time goes in v6:
time: 63 us; the launch traced here: 62.7 us
  blocking collectives  34.9 us (55%)
  starting transfers between devices  19.5 us (31%)
  Pallas kernels  6.62 us (11%)
  waiting for transfers between devices  0.87 us (1%)
  between operations  0.76 us (1%)
    all_to_all x1, blocking collectives, shards(): lax.all_to_all(parts, 'ccd', split_axis=0, concat_axis=0, tiled=True)  17.8 us
    all_to_all x1, blocking collectives, shards(): flux = lax.all_to_all(flux, 'exp', split_axis=0, concat_axis=0, tiled=True)  17.1 us
    all_to_all x1, starting transfers between devices, shards(): lax.all_to_all(send, 'exp', split_axis=0, concat_axis=0, tiled=True)  13 us
    ppermute x1, starting transfers between devices, shards(): far = lax.ppermute(far, 'ccd', swaps[1])  5.75 us
    pallas_call x1, Pallas kernels, sky_model(): pl.pallas_call(sky_kernel, out_shape=(TILES, EDGES, EDGES, BANDS, jax.Sha...  2.06 us
    pallas_call x1, Pallas kernels, gram_parts(): pl.pallas_call(gram_kernel, out_shape=(TILES, jax.ShapeDtypeStruct((copie...  1.3 us
  transfers between devices with their start and end apart: 3, of which 1 were waited for; matrix products, arithmetic and copies ran while one was open for 0% of the time, Pallas kernels for 3%

profile of v6, /device:TPU:1, one launch (start us, length us, event | category | flops | bytes accessed | tf_op | source)
XLA Modules:
  0.0 62.7 jit_solution(3321184925305364125)
XLA Ops:
  0.6 0.0 copy-start.1
  0.6 2.1 %sky_model.1 = (f32[32,8,128]{2,1,0:T(8,128)}, bf16[80,128]{1,0:T(8,128)(2,1)S(1)}, bf16[80,128]{1,0:T(8,128)(2,1)S(1)}, f32[11,8,128]{2,1,0:T(8,128)S(1)}, f32[...) custom-call(f32[11,16,50]{2,1,0:T(8,128)} %bitcast.11, f32[10,528]{1,0:T(8,128)} %basis_h.1, s32[1,50]{1,0:T(1,128)} %bitcast.12, ...), custom_call_target="tpu_custom_call" | custom-call | tf_op jit(solution)/shard_map/sky_model/pallas_call | solution.py:329
  2.7 0.0 copy-start
  2.7 13.0 %all-to-all-start = ((f32[32,8,128]{2,1,0:T(8,128)}), f32[32,8,128]{2,1,0:T(8,128)S(1)}, u32[]{:S(2)}, u32[]{:S(2)}) async-start(f32[32,8,128]{2,1,0:T(8,128)} %get-tuple-element.42), calls=%async_computation | async-start | bytes 262144 | tf_op jit(solution)/shard_map/all_to_all | solution.py:447
  15.8 0.7 %collective-permute-start.1 = (bf16[80,128]{1,0:T(8,128)(2,1)S(1)}, bf16[80,128]{1,0:T(8,128)(2,1)S(1)}, u32[]{:S(2)}, u32[]{:S(2)}) collective-permute-start(bf16[80,128]{1,0:T(8,128)(2,1)S(1)} %get-tuple-element.33), channel_id=1, source_target_pairs={{1,2},{3,4},{5,6},{7,8},{9,10},{11,12},{13,14},{2,1},{4,3},{6,5},{... | collective-permute-start | bytes 61448 | tf_op jit(solution)/shard_map/ppermute | solution.py:442
  16.4 5.7 %collective-permute-start = (bf16[80,128]{1,0:T(8,128)(2,1)S(1)}, bf16[80,128]{1,0:T(8,128)(2,1)S(1)}, u32[]{:S(2)}, u32[]{:S(2)}) collective-permute-start(bf16[80,128]{1,0:T(8,128)(2,1)S(1)} %get-tuple-element.25), channel_id=1, source_target_pairs={{0,1},{2,3},{4,5},{6,7},{8,9},{10,11},{12,13},{14,15},{1,0},{3,2},... | collective-permute-start | bytes 61448 | tf_op jit(solution)/shard_map/ppermute | solution.py:443
  22.2 0.0 copy-done.1
  22.2 0.1 copy.9.psf_ref
  22.3 0.7 %local_model.1 = (f32[16,1024]{1,0:T(8,128)S(1)}, s32[3,8,128]{2,1,0:T(8,128)S(1)}, f32[128,128]{1,0:T(8,128)S(1)}, f32[128,128]{1,0:T(8,128)S(1)}) custom-call(f32[11,8,128]{2,1,0:T(8,128)S(1)} %get-tuple-element.26.bands_ref, f32[32,128]{1,0:T(8,128)S(1)} %get-tuple-element.27.turned_ref, s32[3,8,128]{2,1,0:T(8,128)S(1)} %get-tuple-element.28.table_ref), custom_call_target="tpu_custom_call" | custom-call | tf_op jit(solution)/shard_map/local_model/pallas_call | solution.py:357
  23.1 0.0 collective-permute-done.1.near_ref
  23.1 0.0 copy-done
  23.1 0.9 %extract.1 = (f32[2,100,128]{2,1,0:T(8,128)S(1)}, f32[2,100,128]{2,1,0:T(8,128)S(1)}) custom-call(bf16[4000,128]{1,0:T(8,128)(2,1)S(1)} %bitcast.9, bf16[80,128]{1,0:T(8,128)(2,1)S(1)} %collective-permute-done.1.near_ref, bf16[2,100,2160]{2,1,0:T(8,128)(2,1)S(1)} %copy.9.psf_ref), custom_call_target="tpu_custom_call" | custom-call | tf_op jit(solution)/shard_map/extract/pallas_call | solution.py:374
  24.0 0.0 collective-permute-done.far_ref
  24.0 0.9 %all-to-all-done.model_ref = f32[32,8,128]{2,1,0:T(8,128)S(1)} async-done(((f32[32,8,128]{2,1,0:T(8,128)}), f32[32,8,128]{2,1,0:T(8,128)S(1)}, u32[]{:S(2)}, u32[]{:S(2)}) %all-to-all-start) | async-done | bytes 131104 | tf_op jit(solution)/shard_map/all_to_all | solution.py:447
  24.9 1.3 %gram.1 = (f32[32,8,128]{2,1,0:T(8,128)S(1)}, f32[16,8,128]{2,1,0:T(8,128)S(1)}) custom-call(s32[3,8,128]{2,1,0:T(8,128)S(1)} %get-tuple-element.36.picks_ref, f32[128,128]{1,0:T(8,128)S(1)} %get-tuple-element.37.same_ref, f32[128,128]{1,0:T(8,128)S(1)} %get-tuple-element.38.select_ref, bf16[80,128]{1,0:T(8,128)(2,1)S(1)} %collective-permute-done.far_ref, ...), custom_call_target="tpu_custom_call" | custom-call | tf_op jit(solution)/shard_map/gram/pallas_call | solution.py:389
  26.2 17.8 %all_to_all.15.parts_ref = f32[16,8,128]{2,1,0:T(8,128)S(1)} all-to-all(f32[16,8,128]{2,1,0:T(8,128)S(1)} %get-tuple-element.43), channel_id=1, replica_groups=mesh['exp'=32,'ccd'=16] {'ccd'}, dimensions={0} | all-to-all | bytes 131072 | tf_op jit(solution)/shard_map/all_to_all | solution.py:449
  43.9 0.5 solve.1
  44.5 17.1 %all_to_all.16 = f32[32,8,128]{2,1,0:T(8,128)S(1)} all-to-all(f32[32,8,128]{2,1,0:T(8,128)S(1)} %solve.1), channel_id=1, replica_groups=mesh['exp'=32,'ccd'=16] {'exp'}, dimensions={0} | all-to-all | bytes 262144 | tf_op jit(solution)/shard_map/all_to_all | solution.py:451
  61.5 1.1 %subtract.1 = (f32[32,16,50]{2,1,0:T(8,128)}, f32[16,50]{1,0:T(8,128)}) custom-call(f32[256,128]{1,0:T(8,128)S(1)} %bitcast.10, f32[16,1024]{1,0:T(8,128)S(1)} %get-tuple-element.45.model_ref), custom_call_target="tpu_custom_call" | custom-call | tf_op jit(solution)/shard_map/subtract/pallas_call | solution.py:415
Async XLA Ops:
  0.6 21.6 %copy-start.1 = (bf16[2,100,2160]{2,0,1:T(2,128)(2,1)S(1)}, bf16[2,100,2160]{2,0,1:T(2,128)(2,1)}, u32[]{:S(2)}) copy-start(bf16[2,100,2160]{2,0,1:T(2,128)(2,1)} %param.8) | copy-start | bytes 2592004
  2.7 20.4 %copy-start = (bf16[1,1000,4,128]{3,2,1,0:T(4,128)(2,1)S(1)}, bf16[1,1000,4,128]{3,2,1,0:T(4,128)(2,1)}, u32[]{:S(2)}) copy-start(bf16[1,1000,4,128]{3,2,1,0:T(4,128)(2,1)} %param.7) | copy-start | bytes 3072004
  2.7 22.1 %all-to-all-start = ((f32[32,8,128]{2,1,0:T(8,128)}), f32[32,8,128]{2,1,0:T(8,128)S(1)}, u32[]{:S(2)}, u32[]{:S(2)}) async-start(f32[32,8,128]{2,1,0:T(8,128)} %get-tuple-element.42), calls=%async_computation | async-start | bytes 262144 | tf_op jit(solution)/shard_map/all_to_all | solution.py:447
  15.8 7.3 %collective-permute-start.1 = (bf16[80,128]{1,0:T(8,128)(2,1)S(1)}, bf16[80,128]{1,0:T(8,128)(2,1)S(1)}, u32[]{:S(2)}, u32[]{:S(2)}) collective-permute-start(bf16[80,128]{1,0:T(8,128)(2,1)S(1)} %get-tuple-element.33), channel_id=1, source_target_pairs={{1,2},{3,4},{5,6},{7,8},{9,10},{11,12},{13,14},{2,1},{4,3},{6,5},{... | collective-permute-start | bytes 61448 | tf_op jit(solution)/shard_map/ppermute | solution.py:442
  16.4 7.5 %collective-permute-start = (bf16[80,128]{1,0:T(8,128)(2,1)S(1)}, bf16[80,128]{1,0:T(8,128)(2,1)S(1)}, u32[]{:S(2)}, u32[]{:S(2)}) collective-permute-start(bf16[80,128]{1,0:T(8,128)(2,1)S(1)} %get-tuple-element.25), channel_id=1, source_target_pairs={{0,1},{2,3},{4,5},{6,7},{8,9},{10,11},{12,13},{14,15},{1,0},{3,2},... | collective-permute-start | bytes 61448 | tf_op jit(solution)/shard_map/ppermute | solution.py:443

commit v7 on v6

--- a/solution.py
+++ b/solution.py
@@ -16,7 +16,7 @@
 SPAN = 540
 SKYC = 6
 EXPOS = 32
-PIECE = 8
+PIECE = 16
 CHUNK = 16
 GROUPS = 128
 LANES = 128
@@ -106,42 +106,41 @@
     odd = ccd_at % 2
     at_near = pl.multiple_of(odd * (LOCAL - EDGE), EDGE)
     at_far = pl.multiple_of((1 - odd) * (LOCAL - EDGE), EDGE)
-    copies = [
-        pltpu.make_async_copy(source, target, sems.at[i])
-        for i, (source, target) in enumerate(
-            (
-                (sky_h, sky_v),
-                (shift_h, shift_v),
-                (res_h, res_v),
-                (basis_h, basis_v),
-                (slot_h, slot_v),
-                (pix_h.at[pl.ds(at_near, EDGE), :], near_ref),
-                (pix_h.at[pl.ds(at_far, EDGE), :], far_ref),
-            )
-        )
-    ]
-    for copy in copies:
+    moves = {
+        "res": (res_h, res_v),
+        "basis": (basis_h, basis_v),
+        "sky": (sky_h, sky_v),
+        "shift": (shift_h, shift_v),
+        "slot": (slot_h, slot_v),
+        "near": (pix_h.at[pl.ds(at_near, EDGE), :], near_ref),
+        "far": (pix_h.at[pl.ds(at_far, EDGE), :], far_ref),
+    }
+    copies = {name: pltpu.make_async_copy(*move, sems.at[i]) for i, (name, move) in enumerate(moves.items())}
+    for copy in copies.values():
         copy.start()
-    for copy in copies[:4]:
-        copy.wait()
     lane = lanes_of()
     fibre, comp, valid = sky_index(lane)
+    copies["sky"].wait()
+    copies["shift"].wait()
+    copies["slot"].wait()
     sky = sky_lanes(sky_v[...], row_s, ccd_at, fibre)
     shift = doubled(shift_v[...], row_s) + SHIFT
     table_ref[0] = sky
     table_ref[1] = shift
+    table_ref[2] = doubled(slot_v[...], row_s)
     shift = pick(shift, sky)
     masks = [shift == s for s in range(2 * SHIFT + 1)]
+    copies["basis"].wait()
+    turned_basis(basis_v, basis_s, turned_ref, exp_at)
+    copies["res"].wait()
     bands = [pick(band, sky) for band in banded(res_v, bands_ref)]
-    turned_basis(basis_v, basis_s, turned_ref, exp_at)
     total = jnp.zeros((SUB, LANES), f32)
     for t in range(TAPS):
         total = total + tap_of(t, bands, masks) * pick(basis_at(t, turned_ref), (lane & HALF) + comp)
     total = jnp.where(valid, total, 0.0)
     send_ref[...] = jnp.broadcast_to(total[None], (EXPOS, SUB, LANES))
-    for copy in copies[4:]:
-        copy.wait()
-    table_ref[2] = doubled(slot_v[...], row_s)
+    copies["near"].wait()
+    copies["far"].wait()
 
 
 def model_kernel(bands_ref, turned_ref, table_ref, model_ref, picks_ref, same_ref, select_ref):
@@ -172,7 +171,7 @@
     fibre_c, comp_c, valid_c = sky_index(col)
     same = (fibre_r == fibre_c) & ((row & HALF) == (col & HALF)) & valid_r & valid_c
     same_ref[...] = jnp.where(same, 1.0, 0.0)
-    select_ref[...] = jnp.where((row == comp_c) & valid_c, 1.0, 0.0)
+    select_ref[...] = jnp.where((row == comp_c) & valid_c, 1.0, 0.0).astype(jnp.bfloat16)
 
 
 def extract_kernel(pix_ref, near_ref, psf_ref, flux_ref, vari_ref, pix_s, var_s):
@@ -196,6 +195,13 @@
 
 def squared(x):
     return jnp.square(x.astype(f32)).astype(jnp.bfloat16)
+
+
+def split(x):
+    high = x.astype(jnp.bfloat16)
+    rest = x - high.astype(f32)
+    middle = rest.astype(jnp.bfloat16)
+    return high, middle, (rest - middle.astype(f32)).astype(jnp.bfloat16)
 
 
 def gram_kernel(picks_ref, same_ref, select_ref, far_ref, psf_ref, flux_in, vari_in, model_ref, flux_ref, out_ref, edge_s, extra_s, pad_s, rows_s, flux_s, vari_s, weighted_s):
@@ -253,9 +259,10 @@
     square = lax.dot_general(weighted_s[...], model, (((0,), (0,)), ((), ())), precision=highest, preferred_element_type=f32)
     square = square * same_ref[...]
     select = select_ref[...]
-    summed = jnp.dot(select[0:16], square, precision=highest, preferred_element_type=f32)
+    summed = sum(jnp.dot(select[0:16], piece, preferred_element_type=f32) for piece in split(square))
     summed = jnp.where(lanes_of((16, LANES), 0) == COMP, target, summed)
-    full = lax.dot_general(summed, select, (((1,), (1,)), ((), ())), precision=highest, preferred_element_type=f32)
+    turned = (((1,), (1,)), ((), ()))
+    full = sum(lax.dot_general(piece, select, turned, preferred_element_type=f32) for piece in split(summed))
     tile = full[0:SUB] + pltpu.roll(full[SUB : 2 * SUB], HALF, 1)
     out_ref[...] = jnp.broadcast_to(tile[None], out_ref.shape)
 
@@ -322,7 +329,6 @@
 EDGES = jax.ShapeDtypeStruct((EDGE, GROUPS), jnp.bfloat16)
 PARAMS = pltpu.CompilerParams(vmem_limit_bytes=40 * 1024 * 1024)
 BANDS = jax.ShapeDtypeStruct((BAND, SUB, LANES), f32)
-SQUARE = jax.ShapeDtypeStruct((LANES, LANES), f32)
 
 
 def sky_model(*arrays):
@@ -359,8 +365,8 @@
         out_shape=(
             jax.ShapeDtypeStruct((16, SUB * LANES), f32),
             jax.ShapeDtypeStruct((3, SUB, LANES), jnp.int32),
-            SQUARE,
-            SQUARE,
+            jax.ShapeDtypeStruct((LANES, LANES), f32),
+            jax.ShapeDtypeStruct((LANES, LANES), jnp.bfloat16),
         ),
         in_specs=[VMEM] * 3,
         out_specs=(VMEM,) * 4,

time: 63 us -> 62.8 us (level)
  no operation moved by 1% of the time
where the time goes in v7:
time: 62.8 us; the launch traced here: 62.5 us
  blocking collectives  34.9 us (56%)
  starting transfers between devices  19.5 us (31%)
  Pallas kernels  6.4 us (10%)
  waiting for transfers between devices  0.87 us (1%)
  between operations  0.76 us (1%)
    all_to_all x1, blocking collectives, shards(): lax.all_to_all(parts, 'ccd', split_axis=0, concat_axis=0, tiled=True)  17.8 us
    all_to_all x1, blocking collectives, shards(): flux = lax.all_to_all(flux, 'exp', split_axis=0, concat_axis=0, tiled=True)  17.1 us
    all_to_all x1, starting transfers between devices, shards(): lax.all_to_all(send, 'exp', split_axis=0, concat_axis=0, tiled=True)  13 us
    ppermute x1, starting transfers between devices, shards(): far = lax.ppermute(far, 'ccd', swaps[1])  5.75 us
    pallas_call x1, Pallas kernels, sky_model(): pl.pallas_call(sky_kernel, out_shape=(TILES, EDGES, EDGES, BANDS, jax.Sha...  2.05 us
  transfers between devices with their start and end apart: 3, of which 1 were waited for; matrix products, arithmetic and copies ran while one was open for 0% of the time, Pallas kernels for 3%

profile of v7, /device:TPU:1, one launch (start us, length us, event | category | flops | bytes accessed | tf_op | source)
XLA Modules:
  0.0 62.5 jit_solution(11864833399189840847)
XLA Ops:
  0.6 0.0 copy-start.1
  0.6 2.0 %sky_model.1 = (f32[32,8,128]{2,1,0:T(8,128)}, bf16[80,128]{1,0:T(8,128)(2,1)S(1)}, bf16[80,128]{1,0:T(8,128)(2,1)S(1)}, f32[11,8,128]{2,1,0:T(8,128)S(1)}, f32[...) custom-call(f32[11,16,50]{2,1,0:T(8,128)} %bitcast.11, f32[10,528]{1,0:T(8,128)} %basis_h.1, s32[1,50]{1,0:T(1,128)} %bitcast.12, ...), custom_call_target="tpu_custom_call" | custom-call | tf_op jit(solution)/shard_map/sky_model/pallas_call | solution.py:335
  2.7 0.0 copy-start
  2.7 13.0 %all-to-all-start = ((f32[32,8,128]{2,1,0:T(8,128)}), f32[32,8,128]{2,1,0:T(8,128)S(1)}, u32[]{:S(2)}, u32[]{:S(2)}) async-start(f32[32,8,128]{2,1,0:T(8,128)} %get-tuple-element.42), calls=%async_computation | async-start | bytes 262144 | tf_op jit(solution)/shard_map/all_to_all | solution.py:453
  15.8 0.7 %collective-permute-start.1 = (bf16[80,128]{1,0:T(8,128)(2,1)S(1)}, bf16[80,128]{1,0:T(8,128)(2,1)S(1)}, u32[]{:S(2)}, u32[]{:S(2)}) collective-permute-start(bf16[80,128]{1,0:T(8,128)(2,1)S(1)} %get-tuple-element.33), channel_id=1, source_target_pairs={{1,2},{3,4},{5,6},{7,8},{9,10},{11,12},{13,14},{2,1},{4,3},{6,5},{... | collective-permute-start | bytes 61448 | tf_op jit(solution)/shard_map/ppermute | solution.py:448
  16.4 5.7 %collective-permute-start = (bf16[80,128]{1,0:T(8,128)(2,1)S(1)}, bf16[80,128]{1,0:T(8,128)(2,1)S(1)}, u32[]{:S(2)}, u32[]{:S(2)}) collective-permute-start(bf16[80,128]{1,0:T(8,128)(2,1)S(1)} %get-tuple-element.25), channel_id=1, source_target_pairs={{0,1},{2,3},{4,5},{6,7},{8,9},{10,11},{12,13},{14,15},{1,0},{3,2},... | collective-permute-start | bytes 61448 | tf_op jit(solution)/shard_map/ppermute | solution.py:449
  22.2 0.0 copy-done.1
  22.2 0.1 copy.9.psf_ref
  22.3 0.7 %local_model.1 = (f32[16,1024]{1,0:T(8,128)S(1)}, s32[3,8,128]{2,1,0:T(8,128)S(1)}, f32[128,128]{1,0:T(8,128)S(1)}, bf16[128,128]{1,0:T(8,128)(2,1)S(1)}) custom-call(f32[11,8,128]{2,1,0:T(8,128)S(1)} %get-tuple-element.26.bands_ref, f32[32,128]{1,0:T(8,128)S(1)} %get-tuple-element.27.turned_ref, s32[3,8,128]{2,1,0:T(8,128)S(1)} %get-tuple-element.28.table_ref), custom_call_target="tpu_custom_call" | custom-call | tf_op jit(solution)/shard_map/local_model/pallas_call | solution.py:363
  23.0 0.0 collective-permute-done.1.near_ref
  23.1 0.0 copy-done
  23.1 0.9 %extract.1 = (f32[2,100,128]{2,1,0:T(8,128)S(1)}, f32[2,100,128]{2,1,0:T(8,128)S(1)}) custom-call(bf16[4000,128]{1,0:T(8,128)(2,1)S(1)} %bitcast.9, bf16[80,128]{1,0:T(8,128)(2,1)S(1)} %collective-permute-done.1.near_ref, bf16[2,100,2160]{2,1,0:T(8,128)(2,1)S(1)} %copy.9.psf_ref), custom_call_target="tpu_custom_call" | custom-call | tf_op jit(solution)/shard_map/extract/pallas_call | solution.py:380
  24.0 0.0 collective-permute-done.far_ref
  24.0 0.9 %all-to-all-done.model_ref = f32[32,8,128]{2,1,0:T(8,128)S(1)} async-done(((f32[32,8,128]{2,1,0:T(8,128)}), f32[32,8,128]{2,1,0:T(8,128)S(1)}, u32[]{:S(2)}, u32[]{:S(2)}) %all-to-all-start) | async-done | bytes 131104 | tf_op jit(solution)/shard_map/all_to_all | solution.py:453
  24.9 1.1 %gram.1 = (f32[32,8,128]{2,1,0:T(8,128)S(1)}, f32[16,8,128]{2,1,0:T(8,128)S(1)}) custom-call(s32[3,8,128]{2,1,0:T(8,128)S(1)} %get-tuple-element.36.picks_ref, f32[128,128]{1,0:T(8,128)S(1)} %get-tuple-element.37.same_ref, bf16[128,128]{1,0:T(8,128)(2,1)S(1)} %get-tuple-element.38.select_ref, bf16[80,128]{1,0:T(8,128)(2,1)S(1)} %collective-permute-done.far_ref, ...), custom_call_target="tpu_custom_call" | custom-call | tf_op jit(solution)/shard_map/gram/pallas_call | solution.py:395
  25.9 17.8 %all_to_all.15.parts_ref = f32[16,8,128]{2,1,0:T(8,128)S(1)} all-to-all(f32[16,8,128]{2,1,0:T(8,128)S(1)} %get-tuple-element.43), channel_id=1, replica_groups=mesh['exp'=32,'ccd'=16] {'ccd'}, dimensions={0} | all-to-all | bytes 131072 | tf_op jit(solution)/shard_map/all_to_all | solution.py:455
  43.7 0.5 solve.1
  44.3 17.1 %all_to_all.16 = f32[32,8,128]{2,1,0:T(8,128)S(1)} all-to-all(f32[32,8,128]{2,1,0:T(8,128)S(1)} %solve.1), channel_id=1, replica_groups=mesh['exp'=32,'ccd'=16] {'exp'}, dimensions={0} | all-to-all | bytes 262144 | tf_op jit(solution)/shard_map/all_to_all | solution.py:457
  61.3 1.1 %subtract.1 = (f32[32,16,50]{2,1,0:T(8,128)}, f32[16,50]{1,0:T(8,128)}) custom-call(f32[256,128]{1,0:T(8,128)S(1)} %bitcast.10, f32[16,1024]{1,0:T(8,128)S(1)} %get-tuple-element.45.model_ref), custom_call_target="tpu_custom_call" | custom-call | tf_op jit(solution)/shard_map/subtract/pallas_call | solution.py:421
Async XLA Ops:
  0.6 21.6 %copy-start.1 = (bf16[2,100,2160]{2,0,1:T(2,128)(2,1)S(1)}, bf16[2,100,2160]{2,0,1:T(2,128)(2,1)}, u32[]{:S(2)}) copy-start(bf16[2,100,2160]{2,0,1:T(2,128)(2,1)} %param.8) | copy-start | bytes 2592004
  2.7 20.4 %copy-start = (bf16[1,1000,4,128]{3,2,1,0:T(4,128)(2,1)S(1)}, bf16[1,1000,4,128]{3,2,1,0:T(4,128)(2,1)}, u32[]{:S(2)}) copy-start(bf16[1,1000,4,128]{3,2,1,0:T(4,128)(2,1)} %param.7) | copy-start | bytes 3072004
  2.7 22.1 %all-to-all-start = ((f32[32,8,128]{2,1,0:T(8,128)}), f32[32,8,128]{2,1,0:T(8,128)S(1)}, u32[]{:S(2)}, u32[]{:S(2)}) async-start(f32[32,8,128]{2,1,0:T(8,128)} %get-tuple-element.42), calls=%async_computation | async-start | bytes 262144 | tf_op jit(solution)/shard_map/all_to_all | solution.py:453
  15.8 7.3 %collective-permute-start.1 = (bf16[80,128]{1,0:T(8,128)(2,1)S(1)}, bf16[80,128]{1,0:T(8,128)(2,1)S(1)}, u32[]{:S(2)}, u32[]{:S(2)}) collective-permute-start(bf16[80,128]{1,0:T(8,128)(2,1)S(1)} %get-tuple-element.33), channel_id=1, source_target_pairs={{1,2},{3,4},{5,6},{7,8},{9,10},{11,12},{13,14},{2,1},{4,3},{6,5},{... | collective-permute-start | bytes 61448 | tf_op jit(solution)/shard_map/ppermute | solution.py:448
  16.4 7.5 %collective-permute-start = (bf16[80,128]{1,0:T(8,128)(2,1)S(1)}, bf16[80,128]{1,0:T(8,128)(2,1)S(1)}, u32[]{:S(2)}, u32[]{:S(2)}) collective-permute-start(bf16[80,128]{1,0:T(8,128)(2,1)S(1)} %get-tuple-element.25), channel_id=1, source_target_pairs={{0,1},{2,3},{4,5},{6,7},{8,9},{10,11},{12,13},{14,15},{1,0},{3,2},... | collective-permute-start | bytes 61448 | tf_op jit(solution)/shard_map/ppermute | solution.py:449

commit v8 on v7

--- a/solution.py
+++ b/solution.py
@@ -171,7 +171,8 @@
     fibre_c, comp_c, valid_c = sky_index(col)
     same = (fibre_r == fibre_c) & ((row & HALF) == (col & HALF)) & valid_r & valid_c
     same_ref[...] = jnp.where(same, 1.0, 0.0)
-    select_ref[...] = jnp.where((row == comp_c) & valid_c, 1.0, 0.0).astype(jnp.bfloat16)
+    for at, first in enumerate((0, FC)):
+        select_ref[at] = jnp.where((row == comp_c + first) & valid_c, 1.0, 0.0).astype(jnp.bfloat16)
 
 
 def extract_kernel(pix_ref, near_ref, psf_ref, flux_ref, vari_ref, pix_s, var_s):
@@ -227,7 +228,7 @@
 
     for b in range(2):
         for q, part in enumerate((flux_in, vari_in)):
-            pad_s[b, q] = part[b] + jnp.where(odd == 1 - b, extra_s[q], 0.0)
+            pad_s[b, q, 0 : FIBBLK * ROWS, :] = part[b] + jnp.where(odd == 1 - b, extra_s[q], 0.0)
             for r in range(ROWS):
                 at = (r % 2) * HALF + b * 32
                 rows_s[q, r // 2, at : at + FIBBLK, :] = pad_s[b, q, pl.ds(r, FIBBLK, stride=ROWS), :]
@@ -256,13 +257,14 @@
             target = target + weighted * pick(flux, sky)
     target = jnp.sum(target, axis=0, keepdims=True)
     model = model_ref[...].reshape(EXPOS * SUB, LANES)
-    square = lax.dot_general(weighted_s[...], model, (((0,), (0,)), ((), ())), precision=highest, preferred_element_type=f32)
+    square = lax.dot_general(model, weighted_s[...], (((0,), (0,)), ((), ())), precision=highest, preferred_element_type=f32)
     square = square * same_ref[...]
-    select = select_ref[...]
+    select = select_ref[0]
     summed = sum(jnp.dot(select[0:16], piece, preferred_element_type=f32) for piece in split(square))
     summed = jnp.where(lanes_of((16, LANES), 0) == COMP, target, summed)
     turned = (((1,), (1,)), ((), ()))
-    full = sum(lax.dot_general(piece, select, turned, preferred_element_type=f32) for piece in split(summed))
+    placed = select_ref[1]
+    full = sum(lax.dot_general(piece, placed, turned, preferred_element_type=f32) for piece in split(summed))
     tile = full[0:SUB] + pltpu.roll(full[SUB : 2 * SUB], HALF, 1)
     out_ref[...] = jnp.broadcast_to(tile[None], out_ref.shape)
 
@@ -272,10 +274,11 @@
     system = jnp.concatenate([total, pltpu.roll(total, HALF, 1)], axis=0)
     col = lanes_of((16, LANES))
     row = lanes_of((16, LANES), 0)
-    system = jnp.where((col < COMP) & (row <= COMP), system, 0.0)
+    col = col - FC
+    system = jnp.where((col >= 0) & (col < COMP) & (row <= COMP), system, 0.0)
     for k in range(0, COMP, 2):
-        left = pick(system, jnp.full((16, LANES), k, jnp.int32))
-        right = pick(system, jnp.full((16, LANES), k + 1, jnp.int32))
+        left = pick(system, jnp.full((16, LANES), FC + k, jnp.int32))
+        right = pick(system, jnp.full((16, LANES), FC + k + 1, jnp.int32))
         upper = system[k : k + 1, :] - jnp.where(col[0:1] == k, 1.0, 0.0)
         lower = system[k + 1 : k + 2, :] - jnp.where(col[0:1] == k + 1, 1.0, 0.0)
         a, b = left[k : k + 1, :], right[k : k + 1, :]
@@ -283,7 +286,6 @@
         scale = 1.0 / (a * d - b * c)
         system = system - left * ((d * upper - b * lower) * scale) - right * ((a * lower - c * upper) * scale)
     coeffs = jnp.broadcast_to(system[COMP : COMP + 1, :], (SUB, LANES))
-    coeffs = pltpu.roll(coeffs, FC, 1)
     lane = lanes_of()
     here = (lane >= FC) & (lane < FC + COMP)
     for e in range(EXPOS):
@@ -366,7 +368,7 @@
             jax.ShapeDtypeStruct((16, SUB * LANES), f32),
             jax.ShapeDtypeStruct((3, SUB, LANES), jnp.int32),
             jax.ShapeDtypeStruct((LANES, LANES), f32),
-            jax.ShapeDtypeStruct((LANES, LANES), jnp.bfloat16),
+            jax.ShapeDtypeStruct((2, LANES, LANES), jnp.bfloat16),
         ),
         in_specs=[VMEM] * 3,
         out_specs=(VMEM,) * 4,
@@ -400,7 +402,7 @@
         scratch_shapes=[
             pltpu.VMEM((2, TAIL + EDGE, LANES), jnp.bfloat16),
             pltpu.VMEM((2, FIBBLK * ROWS, LANES), f32),
-            pltpu.VMEM((2, 2, FIBBLK * ROWS, LANES), f32),
+            pltpu.VMEM((2, 2, LANES, LANES), f32),
             pltpu.VMEM((2, 2, LANES, LANES), f32),
             pltpu.VMEM((2, LANES, LANES), f32),
             pltpu.VMEM((2, LANES, LANES), f32),

time: 62.8 us -> 62.7 us (level)
  no operation moved by 1% of the time
where the time goes in v8:
time: 62.7 us; the launch traced here: 62.4 us
  blocking collectives  34.9 us (56%)
  starting transfers between devices  19.5 us (31%)
  Pallas kernels  6.33 us (10%)
  waiting for transfers between devices  0.87 us (1%)
  between operations  0.74 us (1%)
    all_to_all x1, blocking collectives, shards(): lax.all_to_all(parts, 'ccd', split_axis=0, concat_axis=0, tiled=True)  17.8 us
    all_to_all x1, blocking collectives, shards(): flux = lax.all_to_all(flux, 'exp', split_axis=0, concat_axis=0, tiled=True)  17.1 us
    all_to_all x1, starting transfers between devices, shards(): lax.all_to_all(send, 'exp', split_axis=0, concat_axis=0, tiled=True)  13 us
    ppermute x1, starting transfers between devices, shards(): far = lax.ppermute(far, 'ccd', swaps[1])  5.75 us
    pallas_call x1, Pallas kernels, sky_model(): pl.pallas_call(sky_kernel, out_shape=(TILES, EDGES, EDGES, BANDS, jax.Sha...  2.05 us
  transfers between devices with their start and end apart: 3, of which 1 were waited for; matrix products, arithmetic and copies ran while one was open for 0% of the time, Pallas kernels for 3%

profile of v8, /device:TPU:1, one launch (start us, length us, event | category | flops | bytes accessed | tf_op | source)
XLA Modules:
  0.0 62.4 jit_solution(3926707369895498895)
XLA Ops:
  0.6 0.0 copy-start.1
  0.6 2.0 %sky_model.1 = (f32[32,8,128]{2,1,0:T(8,128)}, bf16[80,128]{1,0:T(8,128)(2,1)S(1)}, bf16[80,128]{1,0:T(8,128)(2,1)S(1)}, f32[11,8,128]{2,1,0:T(8,128)S(1)}, f32[...) custom-call(f32[11,16,50]{2,1,0:T(8,128)} %bitcast.11, f32[10,528]{1,0:T(8,128)} %basis_h.1, s32[1,50]{1,0:T(1,128)} %bitcast.12, ...), custom_call_target="tpu_custom_call" | custom-call | tf_op jit(solution)/shard_map/sky_model/pallas_call | solution.py:337
  2.7 0.0 copy-start
  2.7 13.0 %all-to-all-start = ((f32[32,8,128]{2,1,0:T(8,128)}), f32[32,8,128]{2,1,0:T(8,128)S(1)}, u32[]{:S(2)}, u32[]{:S(2)}) async-start(f32[32,8,128]{2,1,0:T(8,128)} %get-tuple-element.42), calls=%async_computation | async-start | bytes 262144 | tf_op jit(solution)/shard_map/all_to_all | solution.py:455
  15.8 0.7 %collective-permute-start.1 = (bf16[80,128]{1,0:T(8,128)(2,1)S(1)}, bf16[80,128]{1,0:T(8,128)(2,1)S(1)}, u32[]{:S(2)}, u32[]{:S(2)}) collective-permute-start(bf16[80,128]{1,0:T(8,128)(2,1)S(1)} %get-tuple-element.33), channel_id=1, source_target_pairs={{1,2},{3,4},{5,6},{7,8},{9,10},{11,12},{13,14},{2,1},{4,3},{6,5},{... | collective-permute-start | bytes 61448 | tf_op jit(solution)/shard_map/ppermute | solution.py:450
  16.4 5.7 %collective-permute-start = (bf16[80,128]{1,0:T(8,128)(2,1)S(1)}, bf16[80,128]{1,0:T(8,128)(2,1)S(1)}, u32[]{:S(2)}, u32[]{:S(2)}) collective-permute-start(bf16[80,128]{1,0:T(8,128)(2,1)S(1)} %get-tuple-element.25), channel_id=1, source_target_pairs={{0,1},{2,3},{4,5},{6,7},{8,9},{10,11},{12,13},{14,15},{1,0},{3,2},... | collective-permute-start | bytes 61448 | tf_op jit(solution)/shard_map/ppermute | solution.py:451
  22.2 0.0 copy-done.1
  22.2 0.1 copy.9.psf_ref
  22.3 0.7 %local_model.1 = (f32[16,1024]{1,0:T(8,128)S(1)}, s32[3,8,128]{2,1,0:T(8,128)S(1)}, f32[128,128]{1,0:T(8,128)S(1)}, bf16[2,128,128]{2,1,0:T(8,128)(2,1)S(1)}) custom-call(f32[11,8,128]{2,1,0:T(8,128)S(1)} %get-tuple-element.26.bands_ref, f32[32,128]{1,0:T(8,128)S(1)} %get-tuple-element.27.turned_ref, s32[3,8,128]{2,1,0:T(8,128)S(1)} %get-tuple-element.28.table_ref), custom_call_target="tpu_custom_call" | custom-call | tf_op jit(solution)/shard_map/local_model/pallas_call | solution.py:365
  23.0 0.0 collective-permute-done.1.near_ref
  23.1 0.0 copy-done
  23.1 0.9 %extract.1 = (f32[2,100,128]{2,1,0:T(8,128)S(1)}, f32[2,100,128]{2,1,0:T(8,128)S(1)}) custom-call(bf16[4000,128]{1,0:T(8,128)(2,1)S(1)} %bitcast.9, bf16[80,128]{1,0:T(8,128)(2,1)S(1)} %collective-permute-done.1.near_ref, bf16[2,100,2160]{2,1,0:T(8,128)(2,1)S(1)} %copy.9.psf_ref), custom_call_target="tpu_custom_call" | custom-call | tf_op jit(solution)/shard_map/extract/pallas_call | solution.py:382
  24.0 0.0 collective-permute-done.far_ref
  24.0 0.9 %all-to-all-done.model_ref = f32[32,8,128]{2,1,0:T(8,128)S(1)} async-done(((f32[32,8,128]{2,1,0:T(8,128)}), f32[32,8,128]{2,1,0:T(8,128)S(1)}, u32[]{:S(2)}, u32[]{:S(2)}) %all-to-all-start) | async-done | bytes 131104 | tf_op jit(solution)/shard_map/all_to_all | solution.py:455
  24.9 1.1 %gram.1 = (f32[32,8,128]{2,1,0:T(8,128)S(1)}, f32[16,8,128]{2,1,0:T(8,128)S(1)}) custom-call(s32[3,8,128]{2,1,0:T(8,128)S(1)} %get-tuple-element.36.picks_ref, f32[128,128]{1,0:T(8,128)S(1)} %get-tuple-element.37.same_ref, bf16[2,128,128]{2,1,0:T(8,128)(2,1)S(1)} %get-tuple-element.38.select_ref, bf16[80,128]{1,0:T(8,128)(2,1)S(1)} %collective-permute-done.far_ref, ...), custom_call_target="tpu_custom_call" | custom-call | tf_op jit(solution)/shard_map/gram/pallas_call | solution.py:397
  25.9 17.8 %all_to_all.15.parts_ref = f32[16,8,128]{2,1,0:T(8,128)S(1)} all-to-all(f32[16,8,128]{2,1,0:T(8,128)S(1)} %get-tuple-element.43), channel_id=1, replica_groups=mesh['exp'=32,'ccd'=16] {'ccd'}, dimensions={0} | all-to-all | bytes 131072 | tf_op jit(solution)/shard_map/all_to_all | solution.py:457
  43.7 0.5 solve.1
  44.2 17.1 %all_to_all.16 = f32[32,8,128]{2,1,0:T(8,128)S(1)} all-to-all(f32[32,8,128]{2,1,0:T(8,128)S(1)} %solve.1), channel_id=1, replica_groups=mesh['exp'=32,'ccd'=16] {'exp'}, dimensions={0} | all-to-all | bytes 262144 | tf_op jit(solution)/shard_map/all_to_all | solution.py:459
  61.3 1.1 %subtract.1 = (f32[32,16,50]{2,1,0:T(8,128)}, f32[16,50]{1,0:T(8,128)}) custom-call(f32[256,128]{1,0:T(8,128)S(1)} %bitcast.10, f32[16,1024]{1,0:T(8,128)S(1)} %get-tuple-element.45.model_ref), custom_call_target="tpu_custom_call" | custom-call | tf_op jit(solution)/shard_map/subtract/pallas_call | solution.py:423
Async XLA Ops:
  0.6 21.6 %copy-start.1 = (bf16[2,100,2160]{2,0,1:T(2,128)(2,1)S(1)}, bf16[2,100,2160]{2,0,1:T(2,128)(2,1)}, u32[]{:S(2)}) copy-start(bf16[2,100,2160]{2,0,1:T(2,128)(2,1)} %param.8) | copy-start | bytes 2592004
  2.7 20.4 %copy-start = (bf16[1,1000,4,128]{3,2,1,0:T(4,128)(2,1)S(1)}, bf16[1,1000,4,128]{3,2,1,0:T(4,128)(2,1)}, u32[]{:S(2)}) copy-start(bf16[1,1000,4,128]{3,2,1,0:T(4,128)(2,1)} %param.7) | copy-start | bytes 3072004
  2.7 22.1 %all-to-all-start = ((f32[32,8,128]{2,1,0:T(8,128)}), f32[32,8,128]{2,1,0:T(8,128)S(1)}, u32[]{:S(2)}, u32[]{:S(2)}) async-start(f32[32,8,128]{2,1,0:T(8,128)} %get-tuple-element.42), calls=%async_computation | async-start | bytes 262144 | tf_op jit(solution)/shard_map/all_to_all | solution.py:455
  15.8 7.3 %collective-permute-start.1 = (bf16[80,128]{1,0:T(8,128)(2,1)S(1)}, bf16[80,128]{1,0:T(8,128)(2,1)S(1)}, u32[]{:S(2)}, u32[]{:S(2)}) collective-permute-start(bf16[80,128]{1,0:T(8,128)(2,1)S(1)} %get-tuple-element.33), channel_id=1, source_target_pairs={{1,2},{3,4},{5,6},{7,8},{9,10},{11,12},{13,14},{2,1},{4,3},{6,5},{... | collective-permute-start | bytes 61448 | tf_op jit(solution)/shard_map/ppermute | solution.py:450
  16.4 7.5 %collective-permute-start = (bf16[80,128]{1,0:T(8,128)(2,1)S(1)}, bf16[80,128]{1,0:T(8,128)(2,1)S(1)}, u32[]{:S(2)}, u32[]{:S(2)}) collective-permute-start(bf16[80,128]{1,0:T(8,128)(2,1)S(1)} %get-tuple-element.25), channel_id=1, source_target_pairs={{0,1},{2,3},{4,5},{6,7},{8,9},{10,11},{12,13},{14,15},{1,0},{3,2},... | collective-permute-start | bytes 61448 | tf_op jit(solution)/shard_map/ppermute | solution.py:451

commit v9 on v8

--- a/solution.py
+++ b/solution.py
@@ -100,7 +100,7 @@
     return jnp.where(lanes_of() < HALF, upper, pltpu.roll(lower, HALF, 1))
 
 
-def sky_kernel(res_h, basis_h, shift_h, sky_h, slot_h, pix_h, send_ref, near_ref, far_ref, bands_ref, turned_ref, table_ref, res_v, basis_v, shift_v, sky_v, slot_v, basis_s, row_s, sems):
+def sky_kernel(res_h, basis_h, shift_h, sky_h, slot_h, pix_h, send_h, near_ref, far_ref, bands_ref, turned_ref, table_ref, res_v, basis_v, shift_v, sky_v, slot_v, send_s, basis_s, row_s, sems):
     exp_at = lax.axis_index("exp")
     ccd_at = lax.axis_index("ccd")
     odd = ccd_at % 2
@@ -122,12 +122,10 @@
     fibre, comp, valid = sky_index(lane)
     copies["sky"].wait()
     copies["shift"].wait()
-    copies["slot"].wait()
     sky = sky_lanes(sky_v[...], row_s, ccd_at, fibre)
     shift = doubled(shift_v[...], row_s) + SHIFT
     table_ref[0] = sky
     table_ref[1] = shift
-    table_ref[2] = doubled(slot_v[...], row_s)
     shift = pick(shift, sky)
     masks = [shift == s for s in range(2 * SHIFT + 1)]
     copies["basis"].wait()
@@ -138,9 +136,14 @@
     for t in range(TAPS):
         total = total + tap_of(t, bands, masks) * pick(basis_at(t, turned_ref), (lane & HALF) + comp)
     total = jnp.where(valid, total, 0.0)
-    send_ref[...] = jnp.broadcast_to(total[None], (EXPOS, SUB, LANES))
+    send_s[...] = jnp.broadcast_to(total[None], (EXPOS, SUB, LANES))
+    sent = pltpu.make_async_copy(send_s, send_h, sems.at[len(moves)])
+    sent.start()
+    copies["slot"].wait()
+    table_ref[2] = doubled(slot_v[...], row_s)
     copies["near"].wait()
     copies["far"].wait()
+    sent.wait()
 
 
 def model_kernel(bands_ref, turned_ref, table_ref, model_ref, picks_ref, same_ref, select_ref):
@@ -345,16 +348,17 @@
             jax.ShapeDtypeStruct((3, SUB, LANES), jnp.int32),
         ),
         in_specs=[HBM] * 6,
-        out_specs=(VMEM,) * 6,
+        out_specs=(HBM,) + (VMEM,) * 5,
         scratch_shapes=[
             pltpu.VMEM((BAND, CHUNK, FC), f32),
             pltpu.VMEM((COMP, 528), f32),
             pltpu.VMEM((1, FC), jnp.int32),
             pltpu.VMEM((1, 96), jnp.int32),
             pltpu.VMEM((1, FC), jnp.int32),
+            pltpu.VMEM((EXPOS, SUB, LANES), f32),
             pltpu.VMEM((16, 640), f32),
             pltpu.VMEM((SUB, LANES), jnp.int32),
-            pltpu.SemaphoreType.DMA((7,)),
+            pltpu.SemaphoreType.DMA((8,)),
         ],
         compiler_params=PARAMS,
         name="sky_model",

time: 62.7 us -> 62.7 us (level)
  no operation moved by 1% of the time
where the time goes in v9:
time: 62.7 us; the launch traced here: 62.4 us
  blocking collectives  34.9 us (56%)
  starting transfers between devices  19.5 us (31%)
  Pallas kernels  6.31 us (10%)
  waiting for transfers between devices  0.87 us (1%)
  between operations  0.74 us (1%)
    all_to_all x1, blocking collectives, shards(): lax.all_to_all(parts, 'ccd', split_axis=0, concat_axis=0, tiled=True)  17.8 us
    all_to_all x1, blocking collectives, shards(): flux = lax.all_to_all(flux, 'exp', split_axis=0, concat_axis=0, tiled=True)  17.1 us
    all_to_all x1, starting transfers between devices, shards(): lax.all_to_all(send, 'exp', split_axis=0, concat_axis=0, tiled=True)  13 us
    ppermute x1, starting transfers between devices, shards(): far = lax.ppermute(far, 'ccd', swaps[1])  5.75 us
    pallas_call x1, Pallas kernels, sky_model(): pl.pallas_call(sky_kernel, out_shape=(TILES, EDGES, EDGES, BANDS, jax.Sha...  2.04 us
  transfers between devices with their start and end apart: 3, of which 1 were waited for; matrix products, arithmetic and copies ran while one was open for 0% of the time, Pallas kernels for 3%

profile of v9, /device:TPU:1, one launch (start us, length us, event | category | flops | bytes accessed | tf_op | source)
XLA Modules:
  0.0 62.4 jit_solution(11660221020422353875)
XLA Ops:
  0.6 0.0 copy-start.1
  0.6 2.0 %sky_model.1 = (f32[32,8,128]{2,1,0:T(8,128)}, bf16[80,128]{1,0:T(8,128)(2,1)S(1)}, bf16[80,128]{1,0:T(8,128)(2,1)S(1)}, f32[11,8,128]{2,1,0:T(8,128)S(1)}, f32[...) custom-call(f32[11,16,50]{2,1,0:T(8,128)} %bitcast.11, f32[10,528]{1,0:T(8,128)} %basis_h.1, s32[1,50]{1,0:T(1,128)} %bitcast.12, ...), custom_call_target="tpu_custom_call" | custom-call | tf_op jit(solution)/shard_map/sky_model/pallas_call | solution.py:340
  2.7 0.0 copy-start
  2.7 13.0 %all-to-all-start = ((f32[32,8,128]{2,1,0:T(8,128)}), f32[32,8,128]{2,1,0:T(8,128)S(1)}, u32[]{:S(2)}, u32[]{:S(2)}) async-start(f32[32,8,128]{2,1,0:T(8,128)} %get-tuple-element.42), calls=%async_computation | async-start | bytes 262144 | tf_op jit(solution)/shard_map/all_to_all | solution.py:459
  15.8 0.7 %collective-permute-start.1 = (bf16[80,128]{1,0:T(8,128)(2,1)S(1)}, bf16[80,128]{1,0:T(8,128)(2,1)S(1)}, u32[]{:S(2)}, u32[]{:S(2)}) collective-permute-start(bf16[80,128]{1,0:T(8,128)(2,1)S(1)} %get-tuple-element.33), channel_id=1, source_target_pairs={{1,2},{3,4},{5,6},{7,8},{9,10},{11,12},{13,14},{2,1},{4,3},{6,5},{... | collective-permute-start | bytes 61448 | tf_op jit(solution)/shard_map/ppermute | solution.py:454
  16.4 5.7 %collective-permute-start = (bf16[80,128]{1,0:T(8,128)(2,1)S(1)}, bf16[80,128]{1,0:T(8,128)(2,1)S(1)}, u32[]{:S(2)}, u32[]{:S(2)}) collective-permute-start(bf16[80,128]{1,0:T(8,128)(2,1)S(1)} %get-tuple-element.25), channel_id=1, source_target_pairs={{0,1},{2,3},{4,5},{6,7},{8,9},{10,11},{12,13},{14,15},{1,0},{3,2},... | collective-permute-start | bytes 61448 | tf_op jit(solution)/shard_map/ppermute | solution.py:455
  22.2 0.0 copy-done.1
  22.2 0.1 copy.9.psf_ref
  22.3 0.7 %local_model.1 = (f32[16,1024]{1,0:T(8,128)S(1)}, s32[3,8,128]{2,1,0:T(8,128)S(1)}, f32[128,128]{1,0:T(8,128)S(1)}, bf16[2,128,128]{2,1,0:T(8,128)(2,1)S(1)}) custom-call(f32[11,8,128]{2,1,0:T(8,128)S(1)} %get-tuple-element.26.bands_ref, f32[32,128]{1,0:T(8,128)S(1)} %get-tuple-element.27.turned_ref, s32[3,8,128]{2,1,0:T(8,128)S(1)} %get-tuple-element.28.table_ref), custom_call_target="tpu_custom_call" | custom-call | tf_op jit(solution)/shard_map/local_model/pallas_call | solution.py:369
  23.0 0.0 collective-permute-done.1.near_ref
  23.0 0.0 copy-done
  23.1 0.9 %extract.1 = (f32[2,100,128]{2,1,0:T(8,128)S(1)}, f32[2,100,128]{2,1,0:T(8,128)S(1)}) custom-call(bf16[4000,128]{1,0:T(8,128)(2,1)S(1)} %bitcast.9, bf16[80,128]{1,0:T(8,128)(2,1)S(1)} %collective-permute-done.1.near_ref, bf16[2,100,2160]{2,1,0:T(8,128)(2,1)S(1)} %copy.9.psf_ref), custom_call_target="tpu_custom_call" | custom-call | tf_op jit(solution)/shard_map/extract/pallas_call | solution.py:386
  24.0 0.0 collective-permute-done.far_ref
  24.0 0.9 %all-to-all-done.model_ref = f32[32,8,128]{2,1,0:T(8,128)S(1)} async-done(((f32[32,8,128]{2,1,0:T(8,128)}), f32[32,8,128]{2,1,0:T(8,128)S(1)}, u32[]{:S(2)}, u32[]{:S(2)}) %all-to-all-start) | async-done | bytes 131104 | tf_op jit(solution)/shard_map/all_to_all | solution.py:459
  24.8 1.0 %gram.1 = (f32[32,8,128]{2,1,0:T(8,128)S(1)}, f32[16,8,128]{2,1,0:T(8,128)S(1)}) custom-call(s32[3,8,128]{2,1,0:T(8,128)S(1)} %get-tuple-element.36.picks_ref, f32[128,128]{1,0:T(8,128)S(1)} %get-tuple-element.37.same_ref, bf16[2,128,128]{2,1,0:T(8,128)(2,1)S(1)} %get-tuple-element.38.select_ref, bf16[80,128]{1,0:T(8,128)(2,1)S(1)} %collective-permute-done.far_ref, ...), custom_call_target="tpu_custom_call" | custom-call | tf_op jit(solution)/shard_map/gram/pallas_call | solution.py:401
  25.9 17.8 %all_to_all.15.parts_ref = f32[16,8,128]{2,1,0:T(8,128)S(1)} all-to-all(f32[16,8,128]{2,1,0:T(8,128)S(1)} %get-tuple-element.43), channel_id=1, replica_groups=mesh['exp'=32,'ccd'=16] {'ccd'}, dimensions={0} | all-to-all | bytes 131072 | tf_op jit(solution)/shard_map/all_to_all | solution.py:461
  43.7 0.5 solve.1
  44.2 17.1 %all_to_all.16 = f32[32,8,128]{2,1,0:T(8,128)S(1)} all-to-all(f32[32,8,128]{2,1,0:T(8,128)S(1)} %solve.1), channel_id=1, replica_groups=mesh['exp'=32,'ccd'=16] {'exp'}, dimensions={0} | all-to-all | bytes 262144 | tf_op jit(solution)/shard_map/all_to_all | solution.py:463
  61.2 1.1 %subtract.1 = (f32[32,16,50]{2,1,0:T(8,128)}, f32[16,50]{1,0:T(8,128)}) custom-call(f32[256,128]{1,0:T(8,128)S(1)} %bitcast.10, f32[16,1024]{1,0:T(8,128)S(1)} %get-tuple-element.45.model_ref), custom_call_target="tpu_custom_call" | custom-call | tf_op jit(solution)/shard_map/subtract/pallas_call | solution.py:427
Async XLA Ops:
  0.6 21.5 %copy-start.1 = (bf16[2,100,2160]{2,0,1:T(2,128)(2,1)S(1)}, bf16[2,100,2160]{2,0,1:T(2,128)(2,1)}, u32[]{:S(2)}) copy-start(bf16[2,100,2160]{2,0,1:T(2,128)(2,1)} %param.8) | copy-start | bytes 2592004
  2.7 20.4 %copy-start = (bf16[1,1000,4,128]{3,2,1,0:T(4,128)(2,1)S(1)}, bf16[1,1000,4,128]{3,2,1,0:T(4,128)(2,1)}, u32[]{:S(2)}) copy-start(bf16[1,1000,4,128]{3,2,1,0:T(4,128)(2,1)} %param.7) | copy-start | bytes 3072004
  2.7 22.1 %all-to-all-start = ((f32[32,8,128]{2,1,0:T(8,128)}), f32[32,8,128]{2,1,0:T(8,128)S(1)}, u32[]{:S(2)}, u32[]{:S(2)}) async-start(f32[32,8,128]{2,1,0:T(8,128)} %get-tuple-element.42), calls=%async_computation | async-start | bytes 262144 | tf_op jit(solution)/shard_map/all_to_all | solution.py:459
  15.8 7.3 %collective-permute-start.1 = (bf16[80,128]{1,0:T(8,128)(2,1)S(1)}, bf16[80,128]{1,0:T(8,128)(2,1)S(1)}, u32[]{:S(2)}, u32[]{:S(2)}) collective-permute-start(bf16[80,128]{1,0:T(8,128)(2,1)S(1)} %get-tuple-element.33), channel_id=1, source_target_pairs={{1,2},{3,4},{5,6},{7,8},{9,10},{11,12},{13,14},{2,1},{4,3},{6,5},{... | collective-permute-start | bytes 61448 | tf_op jit(solution)/shard_map/ppermute | solution.py:454
  16.4 7.5 %collective-permute-start = (bf16[80,128]{1,0:T(8,128)(2,1)S(1)}, bf16[80,128]{1,0:T(8,128)(2,1)S(1)}, u32[]{:S(2)}, u32[]{:S(2)}) collective-permute-start(bf16[80,128]{1,0:T(8,128)(2,1)S(1)} %get-tuple-element.25), channel_id=1, source_target_pairs={{0,1},{2,3},{4,5},{6,7},{8,9},{10,11},{12,13},{14,15},{1,0},{3,2},... | collective-permute-start | bytes 61448 | tf_op jit(solution)/shard_map/ppermute | solution.py:455

commit v10 on v9

--- a/solution.py
+++ b/solution.py
@@ -211,7 +211,6 @@
 def gram_kernel(picks_ref, same_ref, select_ref, far_ref, psf_ref, flux_in, vari_in, model_ref, flux_ref, out_ref, edge_s, extra_s, pad_s, rows_s, flux_s, vari_s, weighted_s):
     odd = lax.axis_index("ccd") % 2
     lane = lanes_of()
-    rows_s[...] = jnp.zeros((2, 2, LANES, LANES), f32)
     edge_s[0, 0:TAIL, :] = jnp.zeros((TAIL, LANES), jnp.bfloat16)
     edge_s[1, 0:TAIL, :] = jnp.zeros((TAIL, LANES), jnp.bfloat16)
     edge_s[0, TAIL : TAIL + EDGE, :] = far_ref[...]
@@ -273,7 +272,10 @@
 
 
 def solve_kernel(parts_ref, flux_ref, out_ref):
-    total = jnp.sum(parts_ref[...], axis=0)
+    parts = [parts_ref[c] for c in range(parts_ref.shape[0])]
+    while len(parts) > 1:
+        parts = [sum(parts[c : c + 2]) for c in range(0, len(parts), 2)]
+    total = parts[0]
     system = jnp.concatenate([total, pltpu.roll(total, HALF, 1)], axis=0)
     col = lanes_of((16, LANES))
     row = lanes_of((16, LANES), 0)

time: 62.7 us -> 62.7 us (level)
  no operation moved by 1% of the time
where the time goes in v10:
time: 62.7 us; the launch traced here: 62.4 us
  blocking collectives  34.9 us (56%)
  starting transfers between devices  19.5 us (31%)
  Pallas kernels  6.3 us (10%)
  waiting for transfers between devices  0.87 us (1%)
  between operations  0.74 us (1%)
    all_to_all x1, blocking collectives, shards(): lax.all_to_all(parts, 'ccd', split_axis=0, concat_axis=0, tiled=True)  17.8 us
    all_to_all x1, blocking collectives, shards(): flux = lax.all_to_all(flux, 'exp', split_axis=0, concat_axis=0, tiled=True)  17.1 us
    all_to_all x1, starting transfers between devices, shards(): lax.all_to_all(send, 'exp', split_axis=0, concat_axis=0, tiled=True)  13 us
    ppermute x1, starting transfers between devices, shards(): far = lax.ppermute(far, 'ccd', swaps[1])  5.75 us
    pallas_call x1, Pallas kernels, sky_model(): pl.pallas_call(sky_kernel, out_shape=(TILES, EDGES, EDGES, BANDS, jax.Sha...  2.04 us
  transfers between devices with their start and end apart: 3, of which 1 were waited for; matrix products, arithmetic and copies ran while one was open for 0% of the time, Pallas kernels for 3%

profile of v10, /device:TPU:1, one launch (start us, length us, event | category | flops | bytes accessed | tf_op | source)
XLA Modules:
  0.0 62.4 jit_solution(6668901122763899439)
XLA Ops:
  0.6 0.0 copy-start.1
  0.6 2.0 %sky_model.1 = (f32[32,8,128]{2,1,0:T(8,128)}, bf16[80,128]{1,0:T(8,128)(2,1)S(1)}, bf16[80,128]{1,0:T(8,128)(2,1)S(1)}, f32[11,8,128]{2,1,0:T(8,128)S(1)}, f32[...) custom-call(f32[11,16,50]{2,1,0:T(8,128)} %bitcast.11, f32[10,528]{1,0:T(8,128)} %basis_h.1, s32[1,50]{1,0:T(1,128)} %bitcast.12, ...), custom_call_target="tpu_custom_call" | custom-call | tf_op jit(solution)/shard_map/sky_model/pallas_call | solution.py:342
  2.7 0.0 copy-start
  2.7 13.0 %all-to-all-start = ((f32[32,8,128]{2,1,0:T(8,128)}), f32[32,8,128]{2,1,0:T(8,128)S(1)}, u32[]{:S(2)}, u32[]{:S(2)}) async-start(f32[32,8,128]{2,1,0:T(8,128)} %get-tuple-element.42), calls=%async_computation | async-start | bytes 262144 | tf_op jit(solution)/shard_map/all_to_all | solution.py:461
  15.8 0.7 %collective-permute-start.1 = (bf16[80,128]{1,0:T(8,128)(2,1)S(1)}, bf16[80,128]{1,0:T(8,128)(2,1)S(1)}, u32[]{:S(2)}, u32[]{:S(2)}) collective-permute-start(bf16[80,128]{1,0:T(8,128)(2,1)S(1)} %get-tuple-element.33), channel_id=1, source_target_pairs={{1,2},{3,4},{5,6},{7,8},{9,10},{11,12},{13,14},{2,1},{4,3},{6,5},{... | collective-permute-start | bytes 61448 | tf_op jit(solution)/shard_map/ppermute | solution.py:456
  16.4 5.7 %collective-permute-start = (bf16[80,128]{1,0:T(8,128)(2,1)S(1)}, bf16[80,128]{1,0:T(8,128)(2,1)S(1)}, u32[]{:S(2)}, u32[]{:S(2)}) collective-permute-start(bf16[80,128]{1,0:T(8,128)(2,1)S(1)} %get-tuple-element.25), channel_id=1, source_target_pairs={{0,1},{2,3},{4,5},{6,7},{8,9},{10,11},{12,13},{14,15},{1,0},{3,2},... | collective-permute-start | bytes 61448 | tf_op jit(solution)/shard_map/ppermute | solution.py:457
  22.2 0.0 copy-done.1
  22.2 0.1 copy.9.psf_ref
  22.3 0.7 %local_model.1 = (f32[16,1024]{1,0:T(8,128)S(1)}, s32[3,8,128]{2,1,0:T(8,128)S(1)}, f32[128,128]{1,0:T(8,128)S(1)}, bf16[2,128,128]{2,1,0:T(8,128)(2,1)S(1)}) custom-call(f32[11,8,128]{2,1,0:T(8,128)S(1)} %get-tuple-element.26.bands_ref, f32[32,128]{1,0:T(8,128)S(1)} %get-tuple-element.27.turned_ref, s32[3,8,128]{2,1,0:T(8,128)S(1)} %get-tuple-element.28.table_ref), custom_call_target="tpu_custom_call" | custom-call | tf_op jit(solution)/shard_map/local_model/pallas_call | solution.py:371
  23.0 0.0 collective-permute-done.1.near_ref
  23.0 0.0 copy-done
  23.1 0.9 %extract.1 = (f32[2,100,128]{2,1,0:T(8,128)S(1)}, f32[2,100,128]{2,1,0:T(8,128)S(1)}) custom-call(bf16[4000,128]{1,0:T(8,128)(2,1)S(1)} %bitcast.9, bf16[80,128]{1,0:T(8,128)(2,1)S(1)} %collective-permute-done.1.near_ref, bf16[2,100,2160]{2,1,0:T(8,128)(2,1)S(1)} %copy.9.psf_ref), custom_call_target="tpu_custom_call" | custom-call | tf_op jit(solution)/shard_map/extract/pallas_call | solution.py:388
  24.0 0.0 collective-permute-done.far_ref
  24.0 0.9 %all-to-all-done.model_ref = f32[32,8,128]{2,1,0:T(8,128)S(1)} async-done(((f32[32,8,128]{2,1,0:T(8,128)}), f32[32,8,128]{2,1,0:T(8,128)S(1)}, u32[]{:S(2)}, u32[]{:S(2)}) %all-to-all-start) | async-done | bytes 131104 | tf_op jit(solution)/shard_map/all_to_all | solution.py:461
  24.8 1.1 %gram.1 = (f32[32,8,128]{2,1,0:T(8,128)S(1)}, f32[16,8,128]{2,1,0:T(8,128)S(1)}) custom-call(s32[3,8,128]{2,1,0:T(8,128)S(1)} %get-tuple-element.36.picks_ref, f32[128,128]{1,0:T(8,128)S(1)} %get-tuple-element.37.same_ref, bf16[2,128,128]{2,1,0:T(8,128)(2,1)S(1)} %get-tuple-element.38.select_ref, bf16[80,128]{1,0:T(8,128)(2,1)S(1)} %collective-permute-done.far_ref, ...), custom_call_target="tpu_custom_call" | custom-call | tf_op jit(solution)/shard_map/gram/pallas_call | solution.py:403
  25.9 17.8 %all_to_all.15.parts_ref = f32[16,8,128]{2,1,0:T(8,128)S(1)} all-to-all(f32[16,8,128]{2,1,0:T(8,128)S(1)} %get-tuple-element.43), channel_id=1, replica_groups=mesh['exp'=32,'ccd'=16] {'ccd'}, dimensions={0} | all-to-all | bytes 131072 | tf_op jit(solution)/shard_map/all_to_all | solution.py:463
  43.7 0.4 solve.1
  44.1 17.1 %all_to_all.16 = f32[32,8,128]{2,1,0:T(8,128)S(1)} all-to-all(f32[32,8,128]{2,1,0:T(8,128)S(1)} %solve.1), channel_id=1, replica_groups=mesh['exp'=32,'ccd'=16] {'exp'}, dimensions={0} | all-to-all | bytes 262144 | tf_op jit(solution)/shard_map/all_to_all | solution.py:465
  61.2 1.1 %subtract.1 = (f32[32,16,50]{2,1,0:T(8,128)}, f32[16,50]{1,0:T(8,128)}) custom-call(f32[256,128]{1,0:T(8,128)S(1)} %bitcast.10, f32[16,1024]{1,0:T(8,128)S(1)} %get-tuple-element.45.model_ref), custom_call_target="tpu_custom_call" | custom-call | tf_op jit(solution)/shard_map/subtract/pallas_call | solution.py:429
Async XLA Ops:
  0.6 21.5 %copy-start.1 = (bf16[2,100,2160]{2,0,1:T(2,128)(2,1)S(1)}, bf16[2,100,2160]{2,0,1:T(2,128)(2,1)}, u32[]{:S(2)}) copy-start(bf16[2,100,2160]{2,0,1:T(2,128)(2,1)} %param.8) | copy-start | bytes 2592004
  2.7 20.4 %copy-start = (bf16[1,1000,4,128]{3,2,1,0:T(4,128)(2,1)S(1)}, bf16[1,1000,4,128]{3,2,1,0:T(4,128)(2,1)}, u32[]{:S(2)}) copy-start(bf16[1,1000,4,128]{3,2,1,0:T(4,128)(2,1)} %param.7) | copy-start | bytes 3072004
  2.7 22.1 %all-to-all-start = ((f32[32,8,128]{2,1,0:T(8,128)}), f32[32,8,128]{2,1,0:T(8,128)S(1)}, u32[]{:S(2)}, u32[]{:S(2)}) async-start(f32[32,8,128]{2,1,0:T(8,128)} %get-tuple-element.42), calls=%async_computation | async-start | bytes 262144 | tf_op jit(solution)/shard_map/all_to_all | solution.py:461
  15.8 7.3 %collective-permute-start.1 = (bf16[80,128]{1,0:T(8,128)(2,1)S(1)}, bf16[80,128]{1,0:T(8,128)(2,1)S(1)}, u32[]{:S(2)}, u32[]{:S(2)}) collective-permute-start(bf16[80,128]{1,0:T(8,128)(2,1)S(1)} %get-tuple-element.33), channel_id=1, source_target_pairs={{1,2},{3,4},{5,6},{7,8},{9,10},{11,12},{13,14},{2,1},{4,3},{6,5},{... | collective-permute-start | bytes 61448 | tf_op jit(solution)/shard_map/ppermute | solution.py:456
  16.4 7.5 %collective-permute-start = (bf16[80,128]{1,0:T(8,128)(2,1)S(1)}, bf16[80,128]{1,0:T(8,128)(2,1)S(1)}, u32[]{:S(2)}, u32[]{:S(2)}) collective-permute-start(bf16[80,128]{1,0:T(8,128)(2,1)S(1)} %get-tuple-element.25), channel_id=1, source_target_pairs={{0,1},{2,3},{4,5},{6,7},{8,9},{10,11},{12,13},{14,15},{1,0},{3,2},... | collective-permute-start | bytes 61448 | tf_op jit(solution)/shard_map/ppermute | solution.py:457
